TPU v7x, 512 devices: a whole 4x8x8 slice. The times are simulated.
512 devices in a mesh: row: 32 (over z, y_lo), col: 4 (over y_hi, core), head: 4 (over x).
Axes of the slice: x: 4, y: 8 (y_hi: 2, y_lo: 4; y = y_hi * 4 + y_lo), z: 8, core: 2. Of those that a mesh axis runs over, the one named last changes fastest.
Arguments:
- tokens: bfloat16 [512, 128, 1024], P(('row', 'head'), 'col'), may hold values from -6 to 6
- valid: int32 [512, 128], P('row', 'col'), may hold values 0 or 1
- gain: float32 [1024], replicated, may hold values from 0.1 to 1.9
- w_qkv: bfloat16 [1024, 3, 1024], P(None, None, 'head'), may hold values from -0.1875 to 0.1875
- w_proj: bfloat16 [1024, 1024], P('head'), may hold values from -0.1875 to 0.1875
- rel_table: float32 [225, 16], P(None, 'head'), may hold values from -4 to 300
- cotangent: bfloat16 [512, 128, 1024], P(('row', 'head'), 'col'), may hold values from -24 to 24
Outputs:
- mixed: bfloat16 [512, 128, 1024], P(('row', 'head'), 'col')
- token_gradient: bfloat16 [512, 128, 1024], P(('row', 'head'), 'col')
- proj_grad: float32 [1024, 1024], P('head', ('row', 'col'))
- table_grad: float32 [225, 16], P(None, 'head')
All inputs are finite; a program needn't handle non-finite values. No bound on the sum of `valid` on one device may be relied on, other than what follows from the above.
Results may differ from a plain program's by a relative error of at most 0.0078.
Values may be sent and summed in bfloat16 or wider, within the bound.
No kernel may reach another device: no remote copies, remote signals or barrier semaphores. Data moves between devices by JAX's collectives and lax.ppermute only.
A program may use at most 64 MiB of HBM per device.

v0:
```python
import math

import jax
import jax.numpy as jnp
from jax import lax
from jax.sharding import PartitionSpec as P

HD = 64
WIN = 8
SHIFT = 4


EPS = 1e-05
HIGH = lax.Precision.HIGHEST


def passed_along(value, axis, steps):
    count = lax.axis_size(axis)
    pairs = [(source, (source + steps) % count) for source in range(count)]
    return lax.ppermute(value, axis, pairs)


def region(index, grand_total):
    return jnp.where(
        index < grand_total - WIN, 0, jnp.where(index < grand_total - SHIFT, 1, 2)
    ).astype(jnp.int32)


def offsets():
    span = 2 * WIN - 1
    pos = jnp.arange(WIN * WIN, dtype=jnp.int32)
    prow = pos // WIN
    pcol = pos % WIN
    index = (prow[:, None] - prow[None, :] + WIN - 1) * span + (
        pcol[:, None] - pcol[None, :] + WIN - 1
    )
    table_ids = jnp.arange(span * span, dtype=jnp.int32)
    return (
        (index[:, :, None] == table_ids[None, None, :])
        .astype(jnp.float32)
        .reshape(WIN * WIN * WIN * WIN, span * span)
    )


def to_windows(block):
    nrow, ncol, heads, depth = block.shape
    block = block.reshape(nrow // WIN, WIN, ncol // WIN, WIN, heads, depth).transpose(
        0, 2, 4, 1, 3, 5
    )
    return block.reshape(nrow // WIN * (ncol // WIN), heads, WIN * WIN, depth)


def from_windows(block, nrow, ncol):
    count, heads, posn, depth = block.shape
    block = block.reshape(nrow // WIN, ncol // WIN, heads, WIN, WIN, depth).transpose(
        0, 3, 1, 4, 2, 5
    )
    return block.reshape(nrow, ncol, heads * depth)


def rows_in(block):
    return jnp.concatenate([block[SHIFT:], passed_along(block[:SHIFT], "row", -1)], 0)


def cols_in(block):
    return jnp.concatenate([block[:, SHIFT:], passed_along(block[:, :SHIFT], "col", -1)], 1)


def rows_out(block):
    return jnp.concatenate([passed_along(block[-SHIFT:], "row", 1), block[:-SHIFT]], 0)


def cols_out(block):
    return jnp.concatenate([passed_along(block[:, -SHIFT:], "col", 1), block[:, :-SHIFT]], 1)


def roll_in(block):
    return cols_in(rows_in(block))


def roll_out(block):
    return cols_out(rows_out(block))


def roll_pair(first, second, roller):
    return (roller(first), roller(second))


def head_sum(term_fn, part_rows):
    return lax.psum_scatter(
        term_fn(jnp.int32(0), lax.axis_size("head") * part_rows).astype(jnp.bfloat16),
        "head",
        scatter_dimension=0,
        tiled=True,
    ).astype(jnp.float32)


def attend(qkv, grad, labels, valid, bias, onehot):
    nrow, ncol = labels.shape
    feature_width = qkv.shape[3]
    heads = feature_width // HD
    scale = HD ** (-0.5)
    f32 = jnp.float32
    query = to_windows(qkv[:, :, 0].reshape(nrow, ncol, heads, HD))
    key = to_windows(qkv[:, :, 1].reshape(nrow, ncol, heads, HD))
    value = to_windows(qkv[:, :, 2].reshape(nrow, ncol, heads, HD))
    dout = to_windows(grad.reshape(nrow, ncol, heads, HD))
    lab_win = to_windows(labels[:, :, None, None])[:, 0, :, 0]
    val_win = to_windows(valid[:, :, None, None])[:, 0, :, 0]
    diagonal = jnp.eye(WIN * WIN, dtype=bool)
    allowed = (lab_win[:, :, None] == lab_win[:, None, :]) & (
        (val_win[:, None, :] == 1) | diagonal[None]
    )
    scores = (
        jnp.einsum("wiqd,wikd->wiqk", query, key, preferred_element_type=f32) * scale + bias[None]
    )
    scores = jnp.where(allowed[:, None], scores, -1e30)
    top = jnp.max(scores, -1, keepdims=True)
    expo = jnp.exp(scores - top)
    prob = expo / jnp.sum(expo, -1, keepdims=True)
    prob_b = prob.astype(jnp.bfloat16)
    attended = jnp.einsum("wiqk,wikd->wiqd", prob_b, value, preferred_element_type=f32).astype(
        jnp.bfloat16
    )
    dprob = jnp.einsum("wiqd,wikd->wiqk", dout, value, preferred_element_type=f32)
    dvalue = jnp.einsum("wiqk,wiqd->wikd", prob_b, dout, preferred_element_type=f32).astype(
        jnp.bfloat16
    )
    dscore = prob * (dprob - jnp.sum(prob * dprob, -1, keepdims=True))
    dscore_b = dscore.astype(jnp.bfloat16)
    dquery = (
        jnp.einsum("wiqk,wikd->wiqd", dscore_b, key, preferred_element_type=f32) * scale
    ).astype(jnp.bfloat16)
    dkey = (
        jnp.einsum("wiqk,wiqd->wikd", dscore_b, query, preferred_element_type=f32) * scale
    ).astype(jnp.bfloat16)
    summed = jnp.sum(dscore, 0).transpose(1, 2, 0).reshape(WIN * WIN * WIN * WIN, heads)
    tgrad = jnp.dot(onehot.T, summed, precision=HIGH)
    grads = jnp.stack(
        [
            from_windows(dquery, nrow, ncol),
            from_windows(dkey, nrow, ncol),
            from_windows(dvalue, nrow, ncol),
        ],
        2,
    )
    return (from_windows(attended, nrow, ncol), grads, tgrad)


def on_device(tokens, valid, gain, w_qkv, w_proj, rel_table, cotangent):
    part_rows, ncol, feature_width = tokens.shape
    tile_rows = part_rows * lax.axis_size("head")
    row_count = lax.axis_size("row")
    col_count = lax.axis_size("col")
    flat = tokens.astype(jnp.float32)
    token_average = jnp.mean(flat, -1, keepdims=True)
    centered_input = flat - token_average
    inverse_deviation = lax.rsqrt(
        jnp.mean(centered_input * centered_input, -1, keepdims=True) + EPS
    )
    standardized_input = centered_input * inverse_deviation
    normalized_tokens = (standardized_input * gain).astype(jnp.bfloat16)
    grad_tile = lax.all_gather(cotangent, "head", axis=0, tiled=True)
    out_grad = jnp.einsum(
        "rcd,nd->rcn", grad_tile, w_proj, preferred_element_type=jnp.float32
    ).astype(jnp.bfloat16)
    source = lax.all_gather(normalized_tokens, "head", axis=0, tiled=True)
    moved, rolled_grad = roll_pair(source, out_grad, roll_in)
    rolled = jnp.einsum("rcd,dtn->rctn", moved, w_qkv, preferred_element_type=jnp.float32).astype(
        jnp.bfloat16
    )
    row_lab = region(
        lax.axis_index("row") * tile_rows + jnp.arange(tile_rows, dtype=jnp.int32),
        tile_rows * row_count,
    )
    col_lab = region(
        lax.axis_index("col") * ncol + jnp.arange(ncol, dtype=jnp.int32), ncol * col_count
    )
    labels = 3 * row_lab[:, None] + col_lab[None, :]
    onehot = offsets()
    heads = rel_table.shape[1]
    bias = (
        jnp.dot(onehot, rel_table, precision=HIGH)
        .reshape(WIN * WIN, WIN * WIN, heads)
        .transpose(2, 0, 1)
    )
    attended, grads, tgrad = attend(rolled, rolled_grad, labels, valid, bias, onehot)
    attn_out, qkv_grad = roll_pair(attended, grads, roll_out)

    def proj_term(start, count):
        return jnp.einsum("rcn,nd->rcd", attn_out, w_proj, preferred_element_type=jnp.float32)

    def back_term(start, count):
        return jnp.einsum("rctn,dtn->rcd", qkv_grad, w_qkv, preferred_element_type=jnp.float32)

    mixed = (flat + head_sum(proj_term, part_rows)).astype(jnp.bfloat16)
    norm_grad = head_sum(back_term, part_rows)
    scale = 1.0 / math.sqrt(tile_rows * ncol * row_count * col_count)
    weight_term = jnp.einsum("rcn,rcd->nd", attn_out, grad_tile, preferred_element_type=jnp.float32)
    proj_grad = (
        lax.psum_scatter(weight_term, ("row", "col"), scatter_dimension=1, tiled=True) * scale
    )
    table_grad = lax.psum(tgrad, ("row", "col")) * (WIN * scale)
    scaled_tokens = norm_grad * gain
    token_gradient = cotangent.astype(jnp.float32) + inverse_deviation * (
        scaled_tokens
        - jnp.mean(scaled_tokens, -1, keepdims=True)
        - standardized_input * jnp.mean(scaled_tokens * standardized_input, -1, keepdims=True)
    )
    return (mixed, token_gradient.astype(jnp.bfloat16), proj_grad, table_grad)


def solution(mesh):
    return jax.shard_map(
        on_device,
        mesh=mesh,
        in_specs=(
            P(("row", "head"), "col", None),
            P("row", "col"),
            P(),
            P(None, None, "head"),
            P("head", None),
            P(None, "head"),
            P(("row", "head"), "col", None),
        ),
        out_specs=(
            P(("row", "head"), "col", None),
            P(("row", "head"), "col", None),
            P("head", ("row", "col")),
            P(None, "head"),
        ),
        check_vma=False,
    )
```

profile of v0, /device:TPU:6, one launch (start us, length us, event | category | flops | bytes accessed | tf_op | source)
XLA Modules:
  0.0 751.9 jit_solution(1386446947580851297)
XLA Ops:
  7.2 1.2 convert_reduce_fusion
  8.5 1.2 fusion.36
  9.7 0.5 copy-done.17
  10.2 1.9 fusion.30
  12.2 0.7 all-gather.5.cloned.1.call-update
  13.4 0.6 copy-done.19
  14.0 3.4 fusion.17
  17.5 27.8 %all-gather.3.cloned.1.call-done = bf16[16,32,1024]{2,1,0:T(8,128)(2,1)} async-done(((bf16[4,32,1024]{2,1,0:T(8,128)(2,1)}), bf16[16,32,1024]{2,1,0:T(8,128)(2,1)}) %all-gather.3.cloned.1.call-update) | async-done | bytes 1048592 | tf_op jit(solution)/shard_map/all_gather | solution.py:167
  45.3 1.8 slice.77
  47.0 8.6 %collective-permute-start = (bf16[4,32,1024]{2,1,0:T(8,128)(2,1)}, bf16[4,32,1024]{2,1,0:T(8,128)(2,1)S(1)}, u32[]{:S(2)}, u32[]{:S(2)}) collective-permute-start(bf16[4,32,1024]{2,1,0:T(8,128)(2,1)} %slice.77), channel_id=1, source_target_pairs={{0,496},{16,0},{32,16},{48,32},{64,48},{80,64},{96,80},{112,96},{1... | collective-permute-start | bytes 786440 | tf_op jit(solution)/shard_map/ppermute | solution.py:20
  55.6 21.4 %all-gather.5.cloned.1.call-done = bf16[16,32,1024]{2,1,0:T(8,128)(2,1)} async-done(((bf16[4,32,1024]{2,1,0:T(8,128)(2,1)}), bf16[16,32,1024]{2,1,0:T(8,128)(2,1)}) %all-gather.5.cloned.1.call-update) | async-done | bytes 1048592 | tf_op jit(solution)/shard_map/all_gather | solution.py:163
  77.1 1.7 convolution_convert_fusion.3
  78.8 8.6 %collective-permute-start.4 = (bf16[4,32,256]{2,1,0:T(8,128)(2,1)S(1)}, bf16[4,32,256]{2,1,0:T(8,128)(2,1)S(1)}, u32[]{:S(2)}, u32[]{:S(2)}) collective-permute-start(bf16[4,32,256]{2,1,0:T(8,128)(2,1)S(1)} %slice.86), channel_id=1, source_target_pairs={{0,496},{16,0},{32,16},{48,32},{64,48},{80,64},{96,80},{112,96},{1... | collective-permute-start | bytes 196616 | tf_op jit(solution)/shard_map/ppermute | solution.py:20
  87.7 1.0 copy.43
  88.7 0.9 slice.85
  89.7 0.6 pad_maximum_fusion.5
  90.3 2.6 collective-permute-start.5
  93.0 0.8 slice_maximum_fusion.1
  93.8 4.0 collective-permute-start.1
  98.1 2.2 collective-permute-done.1
  100.3 1.0 fusion.9
  101.3 0.8 fusion.56
  102.6 1.2 reshape_reshape_squeeze.10
  103.9 0.4 fusion.14
  104.4 1.0 copy-done.3
  105.3 1.2 fusion.57
  106.6 1.2 reshape_reshape_squeeze.11
  107.8 0.9 copy.44
  108.8 3.0 convolution_convert_fusion.2
  111.7 1.7 copy.46
  113.4 1.0 reshape.236
  114.5 0.8 slice.83
  115.3 1.9 collective-permute-start.2
  117.3 1.7 pad_maximum_fusion.2
  119.0 1.2 reshape_reshape.3
  120.2 0.9 copy.47
  121.1 0.9 slice.84
  122.1 3.3 collective-permute-done.2
  125.4 4.4 collective-permute-start.3
  129.8 2.9 convolution_convert_fusion.1
  132.7 1.7 copy.55
  134.5 1.0 stack_reshape.11
  135.5 2.8 convolution_bitcast_fusion
  138.6 1.9 multiply_reduce_fusion
  140.8 1.2 fusion.16
  142.1 1.3 copy.53
  143.4 1.5 copy.54
  144.9 2.2 stack_reshape.10
  147.7 0.7 copy.51
  148.8 1.9 collective-permute-start.6
  150.8 11.6 %collective-permute-done.6 = bf16[4,32,3,256]{3,1,2,0:T(8,128)(2,1)S(1)} collective-permute-done((bf16[4,32,3,256]{3,1,2,0:T(8,128)(2,1)S(1)}, bf16[4,32,3,256]{3,1,2,0:T(8,128)(2,1)S(1)}, u32[]{:S(2)}, u32[]{:S(2)}) %collective-permute-start.6) | collective-permute-done | bytes 196640 | tf_op jit(solution)/shard_map/ppermute | solution.py:20
  162.5 2.1 collective-permute-start.7
  164.6 7.9 %collective-permute-done.7 = bf16[16,4,3,256]{3,1,2,0:T(4,128)(2,1)S(1)} collective-permute-done((bf16[16,4,3,256]{3,1,2,0:T(4,128)(2,1)S(1)}, bf16[16,4,3,256]{3,1,2,0:T(4,128)(2,1)S(1)}, u32[]{:S(2)}, u32[]{:S(2)}) %collective-permute-start.7) | collective-permute-done | bytes 98336 | tf_op jit(solution)/shard_map/ppermute | solution.py:20
  172.5 2.0 bitcast_convert_fusion
  174.6 1.4 convolution_convert_fusion
  176.2 1.4 fusion.18
  177.6 262.3 %psum.7 = f32[225,4]{0,1:T(4,128)S(1)} all-reduce(f32[225,4]{0,1:T(4,128)S(1)} %fusion.18), channel_id=1, replica_groups=mesh['row'=32,'col'=4,'head'=4] {'row','col'}, use_global_device_ids=true, to_apply=%region_11.12 | all-reduce | flops 900 | bytes 7200 | tf_op jit(solution)/shard_map/psum | solution.py:203
  439.9 0.6 broadcast_multiply_fusion.1
  440.5 242.2 %reduce-scatter.8.cloned.1.call-done = f32[256,8]{0,1:T(8,128)} async-done(((f32[256,1024]{0,1:T(8,128)}), f32[256,8]{0,1:T(8,128)}) %reduce-scatter.8.cloned.1.call-update) | async-done | bytes 8208 | tf_op jit(solution)/shard_map/reduce_scatter | solution.py:201
  682.7 1.3 broadcast_multiply_fusion
  684.0 27.9 %reduce-scatter.6.cloned.1.call-done = bf16[4,32,1024]{2,1,0:T(8,128)(2,1)} async-done(((bf16[16,32,1024]{2,1,0:T(8,128)(2,1)}), bf16[4,32,1024]{2,1,0:T(8,128)(2,1)}) %reduce-scatter.6.cloned.1.call-update) | async-done | bytes 262160 | tf_op jit(solution)/shard_map/reduce_scatter | solution.py:90
  711.9 1.2 fusion.40
  713.1 30.1 %reduce-scatter.4.cloned.1.call-done = bf16[4,32,1024]{2,1,0:T(8,128)(2,1)} async-done(((bf16[16,32,1024]{2,1,0:T(8,128)(2,1)}), bf16[4,32,1024]{2,1,0:T(8,128)(2,1)}) %reduce-scatter.4.cloned.1.call-update) | async-done | bytes 262160 | tf_op jit(solution)/shard_map/reduce_scatter | solution.py:90
  743.3 2.1 fusion.35
  (91 shorter events, 3.7 us)
Async XLA Ops:
  7.2 93.2 %copy-start = (bf16[1024,3,256]{2,0,1:T(8,128)(2,1)S(1)}, bf16[1024,3,256]{2,0,1:T(8,128)(2,1)}, u32[]{:S(2)}) copy-start(bf16[1024,3,256]{2,0,1:T(8,128)(2,1)} %param.10) | copy-start | bytes 4718596
  7.2 5.9 copy-start.21
  7.2 6.8 copy-start.22
  7.2 38.1 %all-gather.3.cloned.1.call-start = ((), (), s32[]{:S(2)}) async-start(), calls=%async_computation.3 | async-start | bytes 1310720 | tf_op jit(solution)/shard_map/all_gather | solution.py:167
  8.4 1.3 copy-start.14
  8.4 68.6 %copy-start.8 = (bf16[256,1024]{1,0:T(8,128)(2,1)S(1)}, bf16[256,1024]{1,0:T(8,128)(2,1)}, u32[]{:S(2)}) copy-start(bf16[256,1024]{1,0:T(8,128)(2,1)} %param.11) | copy-start | bytes 1572868
  9.7 0.5 copy-start.17
  12.1 64.9 %all-gather.5.cloned.1.call-start = ((), (), s32[]{:S(2)}) async-start(), calls=%async_computation.5 | async-start | bytes 1310720 | tf_op jit(solution)/shard_map/all_gather | solution.py:163
  12.9 669.8 %reduce-scatter.8.cloned.1.call-start = ((), (), s32[]{:S(2)}) async-start(), calls=%async_computation.7 | async-start | bytes 1056768 | tf_op jit(solution)/shard_map/reduce_scatter | solution.py:201
  13.4 0.6 copy-start.19
  45.3 44.3 %copy-start.6 = (bf16[16,32,1024]{2,1,0:T(8,128)(2,1)S(1)}, bf16[16,32,1024]{2,1,0:T(8,128)(2,1)}, u32[]{:S(2)}) copy-start(bf16[16,32,1024]{2,1,0:T(8,128)(2,1)} %all-gather.3.cloned.1.call-done) | copy-start | bytes 3145732
  47.0 46.7 %collective-permute-start = (bf16[4,32,1024]{2,1,0:T(8,128)(2,1)}, bf16[4,32,1024]{2,1,0:T(8,128)(2,1)S(1)}, u32[]{:S(2)}, u32[]{:S(2)}) collective-permute-start(bf16[4,32,1024]{2,1,0:T(8,128)(2,1)} %slice.77), channel_id=1, source_target_pairs={{0,496},{16,0},{32,16},{48,32},{64,48},{80,64},{96,80},{112,96},{1... | collective-permute-start | bytes 786440 | tf_op jit(solution)/shard_map/ppermute | solution.py:20
  78.8 8.7 %copy-start.11 = (bf16[16,32,256]{2,1,0:T(8,128)(2,1)}, bf16[16,32,256]{2,1,0:T(8,128)(2,1)S(1)}, u32[]{:S(2)}) copy-start(bf16[16,32,256]{2,1,0:T(8,128)(2,1)S(1)} %convolution_convert_fusion.3) | copy-start | bytes 786436
  78.8 10.9 %collective-permute-start.4 = (bf16[4,32,256]{2,1,0:T(8,128)(2,1)S(1)}, bf16[4,32,256]{2,1,0:T(8,128)(2,1)S(1)}, u32[]{:S(2)}, u32[]{:S(2)}) collective-permute-start(bf16[4,32,256]{2,1,0:T(8,128)(2,1)S(1)} %slice.86), channel_id=1, source_target_pairs={{0,496},{16,0},{32,16},{48,32},{64,48},{80,64},{96,80},{112,96},{1... | collective-permute-start | bytes 196616 | tf_op jit(solution)/shard_map/ppermute | solution.py:20
  90.3 26.9 %collective-permute-start.5 = (bf16[16,4,256]{2,1,0:T(4,128)(2,1)}, bf16[16,4,256]{2,1,0:T(4,128)(2,1)}, u32[]{:S(2)}, u32[]{:S(2)}) collective-permute-start(bf16[16,4,256]{2,1,0:T(4,128)(2,1)} %pad_maximum_fusion.5), channel_id=1, source_target_pairs={{0,12},{4,0},{8,4},{12,8},{1,13},{5,1},{9,5},{13,9},{2,14},{6,2},{... | collective-permute-start | bytes 98312 | tf_op jit(solution)/shard_map/ppermute | solution.py:20
  93.8 6.5 collective-permute-start.1
  104.4 1.0 copy-start.3
  115.3 10.1 %collective-permute-start.2 = (bf16[4,32,256]{2,1,0:T(8,128)(2,1)S(1)}, bf16[4,32,256]{2,1,0:T(8,128)(2,1)S(1)}, u32[]{:S(2)}, u32[]{:S(2)}) collective-permute-start(bf16[4,32,256]{2,1,0:T(8,128)(2,1)S(1)} %slice.83), channel_id=1, source_target_pairs={{0,16},{16,32},{32,48},{48,64},{64,80},{80,96},{96,112},{112,128},... | collective-permute-start | bytes 196616 | tf_op jit(solution)/shard_map/ppermute | solution.py:20
  125.4 10.1 %collective-permute-start.3 = (bf16[16,4,256]{2,1,0:T(4,128)(2,1)S(1)}, bf16[16,4,256]{2,1,0:T(4,128)(2,1)S(1)}, u32[]{:S(2)}, u32[]{:S(2)}) collective-permute-start(bf16[16,4,256]{2,1,0:T(4,128)(2,1)S(1)} %pad_maximum_fusion.6), channel_id=1, source_target_pairs={{0,4},{4,8},{8,12},{12,0},{1,5},{5,9},{9,13},{13,1},{2,6},{6,10},{... | collective-permute-start | bytes 98312 | tf_op jit(solution)/shard_map/ppermute | solution.py:20
  135.5 3.1 copy-start.10
  135.5 2.9 copy-start.12
  138.4 573.5 %reduce-scatter.6.cloned.1.call-start = ((), (), s32[]{:S(2)}) async-start(), calls=%async_computation.6 | async-start | bytes 1310720 | tf_op jit(solution)/shard_map/reduce_scatter | solution.py:90
  138.6 1.9 copy-start.2
  147.4 1.4 copy-start.5
  147.7 1.1 copy-start.4
  148.8 13.6 %collective-permute-start.6 = (bf16[4,32,3,256]{3,1,2,0:T(8,128)(2,1)S(1)}, bf16[4,32,3,256]{3,1,2,0:T(8,128)(2,1)S(1)}, u32[]{:S(2)}, u32[]{:S(2)}) collective-permute-start(bf16[4,32,3,256]{3,1,2,0:T(8,128)(2,1)S(1)} %slice.89), channel_id=1, source_target_pairs={{0,16},{16,32},{32,48},{48,64},{64,80},{80,96},{96,112},{112,128},... | collective-permute-start | bytes 589832 | tf_op jit(solution)/shard_map/ppermute | solution.py:20
  162.5 12.1 %copy-start.9 = (bf16[256,1024]{1,0:T(8,128)(2,1)S(1)}, bf16[256,1024]{1,0:T(8,128)(2,1)}, u32[]{:S(2)}) copy-start(bf16[256,1024]{1,0:T(8,128)(2,1)} %param.11) | copy-start | bytes 1572868
  162.5 12.1 %copy-start.13 = (bf16[16,4,256]{2,1,0:T(4,128)(2,1)S(1)}, bf16[16,4,256]{2,1,0:T(4,128)(2,1)}, u32[]{:S(2)}) copy-start(bf16[16,4,256]{2,1,0:T(4,128)(2,1)} %copy-done.12) | copy-start | bytes 98308
  162.5 10.0 %collective-permute-start.7 = (bf16[16,4,3,256]{3,1,2,0:T(4,128)(2,1)S(1)}, bf16[16,4,3,256]{3,1,2,0:T(4,128)(2,1)S(1)}, u32[]{:S(2)}, u32[]{:S(2)}) collective-permute-start(bf16[16,4,3,256]{3,1,2,0:T(4,128)(2,1)S(1)} %pad_maximum_fusion.4), channel_id=1, source_target_pairs={{0,4},{4,8},{8,12},{12,0},{1,5},{5,9},{9,13},{13,1},{2,6},{6,10},{... | collective-permute-start | bytes 294920 | tf_op jit(solution)/shard_map/ppermute | solution.py:20
  174.5 1.7 copy-start.20
  174.5 568.7 %reduce-scatter.4.cloned.1.call-start = ((), (), s32[]{:S(2)}) async-start(), calls=%async_computation.4 | async-start | bytes 1310720 | tf_op jit(solution)/shard_map/reduce_scatter | solution.py:90
  176.0 535.9 %copy-start.1 = (bf16[4,32,1024]{2,1,0:T(8,128)(2,1)S(1)}, bf16[4,32,1024]{2,1,0:T(8,128)(2,1)}, u32[]{:S(2)}) copy-start(bf16[4,32,1024]{2,1,0:T(8,128)(2,1)} %param.7) | copy-start | bytes 786436
  176.0 535.9 %copy-start.15 = (f32[4,32]{1,0:T(4,128)S(1)}, f32[4,32]{1,0:T(4,128)}, u32[]{:S(2)}) copy-start(f32[4,32]{1,0:T(4,128)} %copy-done.14) | copy-start | bytes 1540
  176.0 535.9 %copy-start.16 = (f32[1024]{0:T(1024)S(1)}, f32[1024]{0:T(1024)}, u32[]{:S(2)}) copy-start(f32[1024]{0:T(1024)} %param.9) | copy-start | bytes 12292
  176.0 535.9 %copy-start.18 = (f32[4,32]{1,0:T(4,128)S(1)}, f32[4,32]{1,0:T(4,128)}, u32[]{:S(2)}) copy-start(f32[4,32]{1,0:T(4,128)} %copy-done.17) | copy-start | bytes 1540
  176.0 567.2 %copy-start.7 = (bf16[4,32,1024]{2,1,0:T(8,128)(2,1)S(1)}, bf16[4,32,1024]{2,1,0:T(8,128)(2,1)}, u32[]{:S(2)}) copy-start(bf16[4,32,1024]{2,1,0:T(8,128)(2,1)} %param.13) | copy-start | bytes 786436
Sparse Core Ops, SparseCore 0:
  12.3 32.9 all-gather.2
  47.4 29.6 all-gather.4
  138.5 544.1 reduce-scatter.7
  685.6 26.1 reduce-scatter.5
  714.6 28.6 reduce-scatter.3
where the time goes:
time: 755 us; the launch traced here: 752 us
  waiting for transfers between devices  375 us (50%)
  blocking collectives  262 us (35%)
  starting transfers between devices  34.6 us (5%)
  local copies, waits for them, and re-layouts  26.9 us (4%)
  matrix products  23.6 us (3%)
  other arithmetic  14.9 us (2%)
  between operations  14.4 us (2%)
    psum x1, blocking collectives, on_device(): table_grad = lax.psum(tgrad, ('row', 'col')) * (WIN * scale)  262 us
    reduce_scatter x1, waiting for transfers between devices, on_device(): lax.psum_scatter(weight_term, ('row', 'col'), scatter_dimension=1, tiled=...  242 us
    reduce_scatter x2, waiting for transfers between devices, head_sum(): lax.psum_scatter(term_fn(jnp.int32(0), lax.axis_size('head') * part_rows)...  58 us
    ppermute x8, starting transfers between devices, passed_along(): return lax.ppermute(value, axis, pairs)  34.2 us
    all_gather x1, waiting for transfers between devices, on_device(): source = lax.all_gather(normalized_tokens, 'head', axis=0, tiled=True)  27.8 us
    ppermute x8, waiting for transfers between devices, passed_along(): return lax.ppermute(value, axis, pairs)  25.1 us
    all_gather x1, waiting for transfers between devices, on_device(): grad_tile = lax.all_gather(cotangent, 'head', axis=0, tiled=True)  21.4 us
  transfers between devices with their start and end apart: 13, of which 9 were waited for; matrix products, arithmetic and copies ran while one was open for 7% of the time, Pallas kernels for 0%

commit v1 on v0

v1 whole, which is shorter than its diff:
```python
import math

import jax
import jax.numpy as jnp
from jax import lax
from jax.experimental import pallas as pl
from jax.experimental.pallas import tpu as pltpu
from jax.sharding import PartitionSpec as P

HD = 64
WIN = 8
SHIFT = 4
EPS = 1e-05
F32 = jnp.float32
BF16 = jnp.bfloat16
SPAN = 2 * WIN - 1
POS = WIN * WIN


def dot(a, b, ca, cb):
    return lax.dot_general(a, b, (((ca,), (cb,)), ((), ())), preferred_element_type=F32)


def rows_to_table(vectors):
    heads = vectors.shape[0] // 2
    even = vectors[:heads].reshape(heads, 8, 16)
    odd = jnp.concatenate([vectors[heads:, 8:], vectors[heads:, :8]], 1).reshape(heads, 8, 16)
    both = jnp.stack([even, odd], 2).reshape(heads, 16, 16)[:, :SPAN, :SPAN]
    return both.reshape(heads, SPAN * SPAN).T


def table_to_rows(table):
    heads = table.shape[1]
    grid = jnp.pad(table.T.reshape(heads, SPAN, SPAN), ((0, 0), (0, 1), (0, 1)))
    grid = grid.reshape(heads, 8, 2, 16)
    even = grid[:, :, 0].reshape(heads, 128)
    odd = grid[:, :, 1].reshape(heads, 128)
    odd = jnp.concatenate([odd[:, 120:], odd[:, :120]], 1)
    return jnp.concatenate([even, odd], 0)


def attention_kernel(
    flags_ref, x_ref, wq_ref, wp_ref, tab_ref, val_ref, rs_ref, keep_ref, send_ref
):
    channels = wp_ref.shape[0]
    heads = channels // HD
    d = wp_ref.shape[1]
    scale = HD ** (-0.5)
    bands = x_ref.shape[0] // 2
    ncol = x_ref.shape[3]
    wins = ncol // WIN
    rows = 2 * x_ref.shape[2] * ncol
    lanes = heads * POS

    lane128 = lax.broadcasted_iota(jnp.int32, (8, 128), 1)
    even_lane = ((lane128 // 8) % 2) == 0

    tab = tab_ref[...]
    shifted = [pltpu.roll(tab, (b - 7) % 128, 1) for b in range(WIN)]
    per_head = []
    for h in range(heads):
        ev = jnp.concatenate([s[h : h + 1] for s in shifted], 0)
        od = jnp.concatenate([s[heads + h : heads + h + 1] for s in shifted], 0)
        per_head.append(jnp.where(even_lane, ev, od))
    bias_rows = []
    for a in range(WIN):
        pieces = []
        for p in range(heads // 2):
            lo = pltpu.roll(per_head[2 * p], (-(7 - a) * 8) % 128, 1)
            hi = pltpu.roll(per_head[2 * p + 1], (64 - (7 - a) * 8) % 128, 1)
            pieces.append(jnp.where(lane128 < 64, lo, hi))
        bias_rows.append(jnp.concatenate(pieces, 1))
    bias = jnp.concatenate(bias_rows, 0)

    key_pos = lax.broadcasted_iota(jnp.int32, (POS, lanes), 0)
    query_pos = lax.broadcasted_iota(jnp.int32, (POS, lanes), 1) % POS
    same_pos = key_pos == query_pos
    same_row_half = (key_pos // (WIN * SHIFT)) == (query_pos // (WIN * SHIFT))
    same_col_half = ((key_pos // SHIFT) % 2) == ((query_pos // SHIFT) % 2)
    last_row = flags_ref[0] == 1
    last_col = flags_ref[1] == 1
    core = flags_ref[2]

    lane_head = lax.broadcasted_iota(jnp.int32, (POS, channels), 1) // HD
    head_f = [(lane_head == h).astype(F32) for h in range(heads)]
    head_b = [m.astype(BF16) for m in head_f]

    ds_total = jnp.zeros((POS, lanes), F32)
    wt = jnp.zeros((d, channels), F32)
    for w in range(bands):
        xn = x_ref[2 * w : 2 * w + 2, 0].reshape(rows, d)
        ct = x_ref[2 * w : 2 * w + 2, 1].reshape(rows, d)
        qkv = dot(xn, wq_ref[...], 1, 0).reshape(WIN, wins, WIN, 3 * channels)
        dog = dot(ct, wp_ref[...], 1, 1).reshape(WIN, wins, WIN, channels)
        outs, dqs, dks, dvs = [], [], [], []
        for u in range(wins):
            part = qkv[:, u].reshape(POS, 3 * channels).astype(BF16)
            q = part[:, :channels]
            k = part[:, channels : 2 * channels]
            v = part[:, 2 * channels :]
            do = dog[:, u].reshape(POS, channels).astype(BF16)
            qbd = jnp.concatenate([q * m for m in head_b], 0)
            dbd = jnp.concatenate([do * m for m in head_b], 0)
            s = dot(k, qbd, 1, 1) * scale + bias
            valid = val_ref[:, w * wins + u : w * wins + u + 1]
            allowed = same_pos | (jnp.broadcast_to(valid, (POS, lanes)) == 1.0)
            if w == bands - 1:
                allowed = allowed & (same_row_half | jnp.logical_not(last_row))
            if u == wins - 1:
                allowed = allowed & (same_col_half | jnp.logical_not(last_col))
            s = jnp.where(allowed, s, -1e30)
            e = jnp.exp(s - jnp.max(s, 0, keepdims=True))
            p = e / jnp.sum(e, 0, keepdims=True)
            pb = p.astype(BF16)
            dp = dot(v, dbd, 1, 1)
            ds = p * (dp - jnp.sum(p * dp, 0, keepdims=True))
            dsb = ds.astype(BF16)
            ds_total = ds_total + ds
            dvs.append(dot(pb, dbd, 1, 0))
            dks.append(dot(dsb, qbd, 1, 0) * scale)
            o_all = dot(pb, v, 0, 0)
            dq_all = dot(dsb, k, 0, 0)
            o = o_all[:POS] * head_f[0]
            dq = dq_all[:POS] * head_f[0]
            for h in range(1, heads):
                o = o + o_all[h * POS : (h + 1) * POS] * head_f[h]
                dq = dq + dq_all[h * POS : (h + 1) * POS] * head_f[h]
            outs.append(o)
            dqs.append(dq * scale)

        def patches(parts):
            parts = [z.reshape(WIN, 1, WIN, channels) for z in parts]
            return jnp.concatenate(parts, 1).reshape(rows, channels).astype(BF16)

        attn = patches(outs)
        grads = jnp.concatenate([patches(dqs), patches(dks), patches(dvs)], 1)
        shape = (2,) + rs_ref.shape[2:]
        rs_ref[2 * w : 2 * w + 2, 0] = dot(attn, wp_ref[...], 1, 0).astype(BF16).reshape(shape)
        rs_ref[2 * w : 2 * w + 2, 1] = dot(grads, wq_ref[...], 1, 1).astype(BF16).reshape(shape)
        wt = wt + dot(ct, attn, 0, 0)

    halves = wt.reshape(d // 16, 2, 8, channels)
    first = core == 0
    keep_ref[: d // 16] = jnp.where(first, halves[:, 0], halves[:, 1])
    send_ref[: d // 16] = jnp.where(first, halves[:, 1], halves[:, 0])

    diag = [jnp.zeros((8, 128), F32) for _ in range(heads)]
    for a in range(WIN):
        for p in range(heads // 2):
            block = ds_total[8 * a : 8 * a + 8, 128 * p : 128 * p + 128]
            lo = jnp.where(lane128 < 64, block, 0.0)
            hi = jnp.where(lane128 < 64, 0.0, block)
            diag[2 * p] = diag[2 * p] + pltpu.roll(lo, (7 - a) * 8, 1)
            diag[2 * p + 1] = diag[2 * p + 1] + pltpu.roll(hi, ((7 - a) * 8 - 64) % 128, 1)
    evens = [jnp.where(even_lane, t, 0.0) for t in diag]
    odds = [jnp.where(even_lane, 0.0, t) for t in diag]
    total = jnp.zeros((8, 128), F32)
    for b in range(WIN):
        line = jnp.concatenate([t[b : b + 1] for t in evens + odds], 0)
        total = total + pltpu.roll(line, 7 - b, 1)
    both = jnp.concatenate([total, jnp.zeros((8, channels - 128), F32)], 1)
    keep_ref[d // 16] = both
    send_ref[d // 16] = both


def attention(flags, gathered, w_qkv, w_proj, table, valid):
    d = w_proj.shape[1]
    channels = w_proj.shape[0]
    piece = jax.ShapeDtypeStruct((d // 16 + 1, 8, channels), F32)
    vmem = pl.BlockSpec(memory_space=pltpu.VMEM)
    return pl.pallas_call(
        attention_kernel,
        out_shape=(jax.ShapeDtypeStruct(gathered.shape, BF16), piece, piece),
        in_specs=[pl.BlockSpec(memory_space=pltpu.SMEM)] + [vmem] * 5,
        out_specs=(vmem, vmem, vmem),
        compiler_params=pltpu.CompilerParams(vmem_limit_bytes=44 * 1024 * 1024),
        cost_estimate=pl.CostEstimate(
            flops=3_000_000_000, bytes_accessed=9_000_000, transcendentals=131072
        ),
        name="window_attention",
    )(flags, gathered, w_qkv, w_proj, table, valid)


def on_device(tokens, valid, gain, w_qkv, w_proj, rel_table, cotangent):
    part_rows, ncol, d = tokens.shape
    n_head = lax.axis_size("head")
    n_row = lax.axis_size("row")
    n_col = lax.axis_size("col")
    tile_rows = part_rows * n_head
    channels = w_proj.shape[0]
    row = lax.axis_index("row")
    col = lax.axis_index("col")
    head = lax.axis_index("head")

    groups = [
        [r * n_head + h for h in range(1, n_head)] + [(r + 1) % n_row * n_head]
        for r in range(n_row)
    ]
    left = [(c, (c - 1) % n_col) for c in range(n_col)]
    right = [(c, (c + 1) % n_col) for c in range(n_col)]

    strips = jnp.stack([tokens[:, :SHIFT], cotangent[:, :SHIFT]])
    strips = lax.ppermute(strips, "col", left)
    down = [(r * n_head, (r + 1) % n_row * n_head) for r in range(n_row)]
    val = valid.astype(F32).reshape(tile_rows // WIN, WIN, ncol // WIN, WIN)
    val = val.transpose(1, 3, 0, 2).reshape(POS, -1)
    val = jnp.where(head == 0, lax.ppermute(val, ("row", "head"), down), val)

    moved = jnp.concatenate([tokens[:, SHIFT:], strips[0]], 1).astype(F32)
    mean = jnp.mean(moved, -1, keepdims=True)
    centered = moved - mean
    rstd = lax.rsqrt(jnp.mean(centered * centered, -1, keepdims=True) + EPS)
    normed = (centered * rstd * gain).astype(BF16)
    moved_grad = jnp.concatenate([cotangent[:, SHIFT:], strips[1]], 1)
    packet = jnp.stack([normed, moved_grad])
    packet = jnp.broadcast_to(packet[None], (n_head,) + packet.shape)
    gathered = lax.all_to_all(
        packet, ("row", "head"), 0, 0, axis_index_groups=groups, tiled=True
    )

    tile = jnp.where(head == 0, (row + n_row - 1) % n_row, row)
    flags = jnp.stack([tile == n_row - 1, col == n_col - 1, col % 2 == 1]).astype(jnp.int32)
    terms, keep, send = attention(
        flags, gathered, w_qkv.reshape(d, 3 * channels), w_proj, table_to_rows(rel_table), val
    )

    swap = [(c, c ^ 1) for c in range(n_col)]
    got = lax.ppermute(send, "col", swap)
    shares = lax.all_to_all(terms, ("row", "head"), 0, 0, axis_index_groups=groups, tiled=True)
    summed = jnp.sum(shares.astype(F32), 0)
    edge = lax.ppermute(summed[:, :, -SHIFT:].astype(BF16), "col", right).astype(F32)
    summed = jnp.concatenate([edge, summed[:, :, :-SHIFT]], 2)

    pair = keep + got
    pieces = pair[:-1].astype(BF16)
    table_part = pair[-1, :, :128]
    table_hi = table_part.astype(BF16)
    table_lo = (table_part - table_hi.astype(F32)).astype(BF16)
    table_part = jnp.concatenate([table_hi, table_lo], 1)
    table_part = jnp.broadcast_to(table_part[None], (pieces.shape[0],) + table_part.shape)
    pieces = jnp.concatenate([pieces, table_part], 1)
    cores = [
        [r * n_col + c for r in range(n_row) for c in range(n_col) if c % 2 == parity]
        for parity in range(2)
    ]
    pieces = lax.all_to_all(pieces, ("row", "col"), 0, 0, axis_index_groups=cores, tiled=True)
    pieces = jnp.sum(pieces.astype(F32), 0)
    scale = 1.0 / math.sqrt(tile_rows * ncol * n_row * n_col)
    proj_grad = pieces[:8].T * scale
    table_grad = rows_to_table(pieces[8:, :128] + pieces[8:, 128:]) * (WIN * scale)

    flat = tokens.astype(F32)
    mean = jnp.mean(flat, -1, keepdims=True)
    centered = flat - mean
    rstd = lax.rsqrt(jnp.mean(centered * centered, -1, keepdims=True) + EPS)
    xhat = centered * rstd
    mixed = (flat + summed[0]).astype(BF16)
    scaled = summed[1] * gain
    token_gradient = cotangent.astype(F32) + rstd * (
        scaled
        - jnp.mean(scaled, -1, keepdims=True)
        - xhat * jnp.mean(scaled * xhat, -1, keepdims=True)
    )
    return (mixed, token_gradient.astype(BF16), proj_grad, table_grad)


def solution(mesh):
    return jax.shard_map(
        on_device,
        mesh=mesh,
        in_specs=(
            P(("row", "head"), "col", None),
            P("row", "col"),
            P(),
            P(None, None, "head"),
            P("head", None),
            P(None, "head"),
            P(("row", "head"), "col", None),
        ),
        out_specs=(
            P(("row", "head"), "col", None),
            P(("row", "head"), "col", None),
            P("head", ("row", "col")),
            P(None, "head"),
        ),
        check_vma=False,
    )
```

time: 755 us -> 166 us (0.22)
  the two profiles are of different devices: /device:TPU:6 before, /device:TPU:4 now
where the time goes in v1:
time: 166 us
  waiting for transfers between devices  79.8 us (48%)
  blocking collectives  41.7 us (25%)
  starting transfers between devices  19.8 us (12%)
  local copies, waits for them, and re-layouts  13 us (8%)
  Pallas kernels  5.91 us (4%)
  other arithmetic  4.49 us (3%)
    all_to_all x1, blocking collectives, on_device(): lax.all_to_all(pieces, ('row', 'col'), 0, 0, axis_index_groups=cores, til...  41.7 us
    all_to_all x1, waiting for transfers between devices, on_device(): lax.all_to_all(terms, ('row', 'head'), 0, 0, axis_index_groups=groups, ti...  39.3 us
    all_to_all x1, waiting for transfers between devices, on_device(): lax.all_to_all(packet, ('row', 'head'), 0, 0, axis_index_groups=groups, t...  32.3 us
    ppermute x1, starting transfers between devices, on_device(): strips = lax.ppermute(strips, 'col', left)  7.17 us
    ppermute x1, waiting for transfers between devices, on_device(): lax.ppermute(summed[:, :, -SHIFT:].astype(BF16), 'col', right).astype(F32)  6.28 us
    pallas_call x1, Pallas kernels, attention(): pl.pallas_call(attention_kernel, out_shape=(jax.ShapeDtypeStruct(gathered...  5.91 us
    all_to_all x1, starting transfers between devices, on_device(): lax.all_to_all(packet, ('row', 'head'), 0, 0, axis_index_groups=groups, t...  4.24 us
    unnamed x17, local copies, waits for them, and re-layouts  4.03 us
  transfers between devices with their start and end apart: 6, of which 4 were waited for; matrix products, arithmetic and copies ran while one was open for 6% of the time, Pallas kernels for 0%

profile of v1, /device:TPU:4, one launch (start us, length us, event | category | flops | bytes accessed | tf_op | source)
XLA Modules:
  0.0 165.6 jit_solution(11169982453327298575)
XLA Ops:
  0.6 0.0 copy-start.5
  0.6 0.9 slice_bitcast_fusion.1
  1.6 7.2 %collective-permute-start = (bf16[2,4,4,1024]{3,2,1,0:T(4,128)(2,1)S(1)}, bf16[2,4,4,1024]{3,2,1,0:T(4,128)(2,1)S(1)}, u32[]{:S(2)}, u32[]{:S(2)}) collective-permute-start(bf16[2,4,4,1024]{3,2,1,0:T(4,128)(2,1)S(1)} %pad_maximum_fusion.4), channel_id=1, source_target_pairs={{0,12},{4,0},{8,4},{12,8},{1,13},{5,1},{9,5},{13,9},{2,14},{6,2},{... | collective-permute-start | bytes 196616 | tf_op jit(solution)/shard_map/ppermute | solution.py:203
  8.8 1.0 fusion.22
  9.8 1.0 slice.75
  10.8 0.0 collective-permute-done
  10.9 0.1 convert_reduce_fusion.3
  11.0 0.2 fusion.11
  11.3 0.0 copy-done.5
  11.3 0.2 multiply_convert_fusion
  11.5 0.1 pad_maximum_fusion.1
  11.6 1.6 broadcast_in_dim.4
  13.2 0.0 copy-start.6
  13.2 0.0 copy-start.7
  13.2 4.2 %all-to-all-start = ((bf16[4,2,4,32,1024]{4,3,2,1,0:T(8,128)(2,1)}), bf16[4,2,4,32,1024]{4,3,2,1,0:T(8,128)(2,1)S(1)}, u32[]{:S(2)}, u32[]{:S(2)}) async-start(bf16[4,2,4,32,1024]{4,3,2,1,0:T(8,128)(2,1)} %broadcast_in_dim.4), calls=%async_computation | async-start | bytes 4194304 | tf_op jit(solution)/shard_map/all_to_all | solution.py:217
  17.5 0.0 copy-done.6
  17.5 0.1 reshape.106
  17.6 0.1 reshape.107
  17.7 0.1 copy.16
  17.7 0.7 collective-permute-start.1
  18.4 0.0 copy-done.7
  18.4 0.1 reshape.104
  18.6 0.1 slice_reduce_fusion.1
  18.7 0.1 reshape_squeeze.7
  18.7 0.1 slice.79
  18.8 0.1 reshape_squeeze.6
  18.9 0.1 maximum_maximum_fusion.tab_ref
  19.0 0.1 add_convert_fusion.flags_ref
  19.0 2.6 %copy.14 = bf16[1024,3,256]{0,2,1:T(8,128)(2,1)} copy(bf16[1024,3,256]{2,0,1:T(8,128)(2,1)} %param.10) | data formatting | bytes 3145728 | tf_op args[3]
  21.6 0.0 copy-start.2
  21.6 2.6 %copy.18.wq_ref = bf16[1024,768]{1,0:T(8,128)(2,1)} copy(bf16[1024,768]{0,1:T(8,128)(2,1)} %bitcast.47) | data formatting | bytes 3145728 | tf_op jit(solution)/shard_map/reshape | solution.py:224
  24.3 0.0 collective-permute-done.1
  24.3 32.3 %all-to-all-done.x_ref = bf16[4,2,4,32,1024]{4,3,2,1,0:T(8,128)(2,1)S(1)} async-done(((bf16[4,2,4,32,1024]{4,3,2,1,0:T(8,128)(2,1)}), bf16[4,2,4,32,1024]{4,3,2,1,0:T(8,128)(2,1)S(1)}, u32[]{:S(2)}, u32[]{:S(2)}) %all-to-all-start) | async-done | bytes 2097184 | tf_op jit(solution)/shard_map/all_to_all | solution.py:217
  56.6 0.0 copy-done.2
  56.6 0.0 copy-start.1
  56.6 1.4 copy-done.1
  58.0 5.9 %window_attention.1 = (bf16[4,2,4,32,1024]{4,3,2,1,0:T(8,128)(2,1)S(1)}, f32[65,8,256]{2,1,0:T(8,128)S(1)}, f32[65,8,256]{2,1,0:T(8,128)S(1)}) custom-call(s32[3]{0:T(128)S(1)} %add_convert_fusion.flags_ref, bf16[4,2,4,32,1024]{4,3,2,1,0:T(8,128)(2,1)S(1)} %all-to-all-done.x_ref, bf16[1024,768]{1,0:T(8,128)(2,1)S(1)} %copy-done.1, ...), custom_call_target="tpu_custom_call" | custom-call | flops 3000000000 | bytes 9000000 | tf_op jit(solution)/shard_map/window_attention/pallas_call | solution.py:171
  64.0 0.0 copy-start
  64.0 1.9 %collective-permute-start.3 = (f32[65,8,256]{2,1,0:T(8,128)S(1)}, f32[65,8,256]{2,1,0:T(8,128)S(1)}, u32[]{:S(2)}, u32[]{:S(2)}) collective-permute-start(f32[65,8,256]{2,1,0:T(8,128)S(1)} %get-tuple-element.9), channel_id=1, source_target_pairs={{0,4},{4,0},{8,12},{12,8},{1,5},{5,1},{9,13},{13,9},{2,6},{6,2},{1... | collective-permute-start | bytes 1597448 | tf_op jit(solution)/shard_map/ppermute | solution.py:228
  65.9 1.9 %collective-permute-done.3 = f32[65,8,256]{2,1,0:T(8,128)S(1)} collective-permute-done((f32[65,8,256]{2,1,0:T(8,128)S(1)}, f32[65,8,256]{2,1,0:T(8,128)S(1)}, u32[]{:S(2)}, u32[]{:S(2)}) %collective-permute-start.3) | collective-permute-done | bytes 532512 | tf_op jit(solution)/shard_map/ppermute | solution.py:228
  67.8 0.1 add.47
  68.0 41.7 %all_to_all.15 = bf16[64,16,256]{2,1,0:T(8,128)(2,1)S(1)} all-to-all(bf16[64,16,256]{2,1,0:T(8,128)(2,1)S(1)} %pad_maximum_fusion.2), channel_id=1, replica_groups={{0,8,16,24,32,40,48,56,64,72,80,88,96,104,112,120,128,136,144,152,160,1..., dimensions={0} | all-to-all | bytes 1048576 | tf_op jit(solution)/shard_map/all_to_all | solution.py:246
  109.7 0.0 copy-done
  109.7 0.0 copy-start.3
  109.7 3.7 %all-to-all-start.1 = ((bf16[4,2,4,32,1024]{4,3,2,1,0:T(8,128)(2,1)}), bf16[4,2,4,32,1024]{4,3,2,1,0:T(8,128)(2,1)S(1)}, u32[]{:S(2)}, u32[]{:S(2)}) async-start(bf16[4,2,4,32,1024]{4,3,2,1,0:T(8,128)(2,1)} %copy-done), calls=%async_computation.1 | async-start | bytes 4194304 | tf_op jit(solution)/shard_map/all_to_all | solution.py:229
  113.4 0.0 copy-done.3
  113.4 0.1 convert_reduce_fusion.2
  113.6 0.2 fusion.9
  113.8 0.1 convert_reduce_fusion.1
  113.9 0.1 slice.91
  114.0 0.1 pad_maximum_fusion.7
  114.1 0.1 stack_reshape.7
  114.1 0.1 stack_reshape.6
  114.3 39.3 %all-to-all-done.1 = bf16[4,2,4,32,1024]{4,3,2,1,0:T(8,128)(2,1)S(1)} async-done(((bf16[4,2,4,32,1024]{4,3,2,1,0:T(8,128)(2,1)}), bf16[4,2,4,32,1024]{4,3,2,1,0:T(8,128)(2,1)S(1)}, u32[]{:S(2)}, u32[]{:S(2)}) %all-to-all-start.1) | async-done | bytes 2097184 | tf_op jit(solution)/shard_map/all_to_all | solution.py:229
  153.6 0.4 convert_reduce_fusion
  154.0 0.0 copy-start.4
  154.0 2.1 %collective-permute-start.2 = (bf16[2,4,4,1024]{3,2,1,0:T(4,128)(2,1)S(1)}, bf16[2,4,4,1024]{3,2,1,0:T(4,128)(2,1)S(1)}, u32[]{:S(2)}, u32[]{:S(2)}) collective-permute-start(bf16[2,4,4,1024]{3,2,1,0:T(4,128)(2,1)S(1)} %slice.139), channel_id=1, source_target_pairs={{0,4},{4,8},{8,12},{12,0},{1,5},{5,9},{9,13},{13,1},{2,6},{6,10},{... | collective-permute-start | bytes 196616 | tf_op jit(solution)/shard_map/ppermute | solution.py:231
  156.1 0.6 fusion.17
  156.7 0.7 mul.109
  157.4 6.3 %collective-permute-done.2 = bf16[2,4,4,1024]{3,2,1,0:T(4,128)(2,1)S(1)} collective-permute-done((bf16[2,4,4,1024]{3,2,1,0:T(4,128)(2,1)S(1)}, bf16[2,4,4,1024]{3,2,1,0:T(4,128)(2,1)S(1)}, u32[]{:S(2)}, u32[]{:S(2)}) %collective-permute-start.2) | collective-permute-done | bytes 65568 | tf_op jit(solution)/shard_map/ppermute | solution.py:231
  163.7 1.0 fusion.19
  164.6 0.0 copy-done.4
  164.6 1.0 fusion.8
  (26 shorter events, 0.4 us)
Async XLA Ops:
  0.6 10.7 %copy-start.5 = (f32[1024]{0:T(1024)S(1)}, f32[1024]{0:T(1024)}, u32[]{:S(2)}) copy-start(f32[1024]{0:T(1024)} %param.9) | copy-start | bytes 12292
  1.6 9.2 %collective-permute-start = (bf16[2,4,4,1024]{3,2,1,0:T(4,128)(2,1)S(1)}, bf16[2,4,4,1024]{3,2,1,0:T(4,128)(2,1)S(1)}, u32[]{:S(2)}, u32[]{:S(2)}) collective-permute-start(bf16[2,4,4,1024]{3,2,1,0:T(4,128)(2,1)S(1)} %pad_maximum_fusion.4), channel_id=1, source_target_pairs={{0,12},{4,0},{8,4},{12,8},{1,13},{5,1},{9,5},{13,9},{2,14},{6,2},{... | collective-permute-start | bytes 196616 | tf_op jit(solution)/shard_map/ppermute | solution.py:203
  13.2 4.2 %copy-start.6 = (s32[16,32]{1,0:T(8,128)S(1)}, s32[16,32]{1,0:T(8,128)}, u32[]{:S(2)}) copy-start(s32[16,32]{1,0:T(8,128)} %param.8) | copy-start | bytes 6148
  13.2 5.2 %copy-start.7 = (f32[225,4]{0,1:T(4,128)S(1)}, f32[225,4]{0,1:T(4,128)}, u32[]{:S(2)}) copy-start(f32[225,4]{0,1:T(4,128)} %param.12) | copy-start | bytes 10804
  13.2 43.4 %all-to-all-start = ((bf16[4,2,4,32,1024]{4,3,2,1,0:T(8,128)(2,1)}), bf16[4,2,4,32,1024]{4,3,2,1,0:T(8,128)(2,1)S(1)}, u32[]{:S(2)}, u32[]{:S(2)}) async-start(bf16[4,2,4,32,1024]{4,3,2,1,0:T(8,128)(2,1)} %broadcast_in_dim.4), calls=%async_computation | async-start | bytes 4194304 | tf_op jit(solution)/shard_map/all_to_all | solution.py:217
  17.7 6.5 %collective-permute-start.1 = (f32[64,8]{1,0:T(8,128)S(1)}, f32[64,8]{1,0:T(8,128)S(1)}, u32[]{:S(2)}, u32[]{:S(2)}) collective-permute-start(f32[64,8]{1,0:T(8,128)S(1)} %copy.16), channel_id=1, source_target_pairs={{0,16},{16,32},{32,48},{48,64},{64,80},{80,96},{96,112},{112,128},... | collective-permute-start | bytes 6152 | tf_op jit(solution)/shard_map/ppermute | solution.py:207
  21.6 35.0 %copy-start.2 = (bf16[256,1024]{1,0:T(8,128)(2,1)S(1)}, bf16[256,1024]{1,0:T(8,128)(2,1)}, u32[]{:S(2)}) copy-start(bf16[256,1024]{1,0:T(8,128)(2,1)} %wp_ref.1) | copy-start | bytes 1572868
  56.6 1.4 copy-start.1
  64.0 45.7 %copy-start = (bf16[4,2,4,32,1024]{4,3,2,1,0:T(8,128)(2,1)}, bf16[4,2,4,32,1024]{4,3,2,1,0:T(8,128)(2,1)S(1)}, u32[]{:S(2)}) copy-start(bf16[4,2,4,32,1024]{4,3,2,1,0:T(8,128)(2,1)S(1)} %get-tuple-element.7) | copy-start | bytes 6291460
  64.0 3.8 %collective-permute-start.3 = (f32[65,8,256]{2,1,0:T(8,128)S(1)}, f32[65,8,256]{2,1,0:T(8,128)S(1)}, u32[]{:S(2)}, u32[]{:S(2)}) collective-permute-start(f32[65,8,256]{2,1,0:T(8,128)S(1)} %get-tuple-element.9), channel_id=1, source_target_pairs={{0,4},{4,0},{8,12},{12,8},{1,5},{5,1},{9,13},{13,9},{2,6},{6,2},{1... | collective-permute-start | bytes 1597448 | tf_op jit(solution)/shard_map/ppermute | solution.py:228
  109.7 3.7 %copy-start.3 = (bf16[4,32,1024]{2,1,0:T(8,128)(2,1)S(1)}, bf16[4,32,1024]{2,1,0:T(8,128)(2,1)}, u32[]{:S(2)}) copy-start(bf16[4,32,1024]{2,1,0:T(8,128)(2,1)} %param.7) | copy-start | bytes 786436
  109.7 43.9 %all-to-all-start.1 = ((bf16[4,2,4,32,1024]{4,3,2,1,0:T(8,128)(2,1)}), bf16[4,2,4,32,1024]{4,3,2,1,0:T(8,128)(2,1)S(1)}, u32[]{:S(2)}, u32[]{:S(2)}) async-start(bf16[4,2,4,32,1024]{4,3,2,1,0:T(8,128)(2,1)} %copy-done), calls=%async_computation.1 | async-start | bytes 4194304 | tf_op jit(solution)/shard_map/all_to_all | solution.py:229
  154.0 10.7 %copy-start.4 = (bf16[4,32,1024]{2,1,0:T(8,128)(2,1)S(1)}, bf16[4,32,1024]{2,1,0:T(8,128)(2,1)}, u32[]{:S(2)}) copy-start(bf16[4,32,1024]{2,1,0:T(8,128)(2,1)} %param.13) | copy-start | bytes 786436
  154.0 9.6 %collective-permute-start.2 = (bf16[2,4,4,1024]{3,2,1,0:T(4,128)(2,1)S(1)}, bf16[2,4,4,1024]{3,2,1,0:T(4,128)(2,1)S(1)}, u32[]{:S(2)}, u32[]{:S(2)}) collective-permute-start(bf16[2,4,4,1024]{3,2,1,0:T(4,128)(2,1)S(1)} %slice.139), channel_id=1, source_target_pairs={{0,4},{4,8},{8,12},{12,0},{1,5},{5,9},{9,13},{13,1},{2,6},{6,10},{... | collective-permute-start | bytes 196616 | tf_op jit(solution)/shard_map/ppermute | solution.py:231

commit v2 on v1

--- a/solution.py
+++ b/solution.py
@@ -15,6 +15,7 @@
 BF16 = jnp.bfloat16
 SPAN = 2 * WIN - 1
 POS = WIN * WIN
+VMEM_LIMIT = 56 * 1024 * 1024
 
 
 def dot(a, b, ca, cb):
@@ -40,17 +41,36 @@
 
 
 def attention_kernel(
-    flags_ref, x_ref, wq_ref, wp_ref, tab_ref, val_ref, rs_ref, keep_ref, send_ref
+    flags_ref, x1, x2, x3, x4, c1, c2, c3, c4, wq_in, wp_in, tab_ref,
+    o1, o2, o3, o4, keep_ref, send_ref,
+    xs_ref, cs_ref, wq_ref, wp_ref, out_ref, grad_cols, attn_cols, attn_edge, sems,
 ):
     channels = wp_ref.shape[0]
     heads = channels // HD
     d = wp_ref.shape[1]
     scale = HD ** (-0.5)
-    bands = x_ref.shape[0] // 2
-    ncol = x_ref.shape[3]
+    parts = cs_ref.shape[0]
+    ncol = grad_cols.shape[1] - WIN
     wins = ncol // WIN
-    rows = 2 * x_ref.shape[2] * ncol
+    own = cs_ref.shape[1]
+    prow = own // ncol
+    strip = prow * SHIFT
+    bands = parts * prow // WIN
+    rows = own * parts // bands
     lanes = heads * POS
+    head = flags_ref[3]
+    slots = []
+    for k in range(parts):
+        slot = SLOTS[0][k]
+        for h in range(1, parts):
+            slot = jnp.where(head == h, SLOTS[h][k], slot)
+        slots.append(slot)
+    moves = [(wp_in, wp_ref), (wq_in, wq_ref)]
+    moves += [(c, cs_ref.at[slot]) for slot, c in zip(slots, (c1, c2, c3, c4))]
+    moves += [(x, xs_ref.at[slot]) for slot, x in zip(slots, (x1, x2, x3, x4))]
+    moves = [pltpu.make_async_copy(a, b, sems.at[i]) for i, (a, b) in enumerate(moves)]
+    for move in moves:
+        move.start()
 
     lane128 = lax.broadcasted_iota(jnp.int32, (8, 128), 1)
     even_lane = ((lane128 // 8) % 2) == 0
@@ -85,24 +105,49 @@
     head_f = [(lane_head == h).astype(F32) for h in range(heads)]
     head_b = [m.astype(BF16) for m in head_f]
 
+    for move in moves:
+        move.wait()
+
+    edge = jnp.concatenate([xs_ref[x, own : own + strip] for x in range(parts)], 0)
+    edge_grad = dot(edge, wp_ref[...], 1, 1)
+    attn_edge[...] = edge_grad
+
+    results = [
+        pltpu.make_async_copy(out_ref.at[slot], out, sems.at[len(moves) + k])
+        for k, (slot, out) in enumerate(zip(slots, (o1, o2, o3, o4)))
+    ]
     ds_total = jnp.zeros((POS, lanes), F32)
     wt = jnp.zeros((d, channels), F32)
+    per_band = parts // bands
     for w in range(bands):
-        xn = x_ref[2 * w : 2 * w + 2, 0].reshape(rows, d)
-        ct = x_ref[2 * w : 2 * w + 2, 1].reshape(rows, d)
-        qkv = dot(xn, wq_ref[...], 1, 0).reshape(WIN, wins, WIN, 3 * channels)
-        dog = dot(ct, wp_ref[...], 1, 1).reshape(WIN, wins, WIN, channels)
+        members = range(w * per_band, (w + 1) * per_band)
+        xn = jnp.concatenate([xs_ref[x, :own] for x in members], 0)
+        ct = jnp.concatenate([cs_ref[x] for x in members], 0)
+        queries, keys, values = [
+            dot(xn, wq_ref[t], 1, 0).reshape(WIN, wins, WIN, channels) for t in range(3)
+        ]
+        marks = xs_ref[w * per_band, own + strip :]
+        key_row = lax.broadcasted_iota(jnp.int32, (POS, marks.shape[0]), 0) // WIN + w * WIN
+        tile_row = lax.broadcasted_iota(jnp.int32, (POS, marks.shape[0]), 1)
+        marks = dot((key_row == tile_row).astype(BF16), marks[:, :128], 1, 0)
+        key_col = lax.broadcasted_iota(jnp.int32, marks.shape, 0) % WIN
+        tile_col = lax.broadcasted_iota(jnp.int32, marks.shape, 1)
+        grad_cols[:, :ncol] = dot(ct, wp_ref[...], 1, 1).reshape(WIN, ncol, channels)
+        for i in range(WIN):
+            at = (w * WIN + i) * SHIFT
+            grad_cols[i, ncol : ncol + SHIFT] = attn_edge[at : at + SHIFT]
+        dog = grad_cols[:, SHIFT : SHIFT + ncol].reshape(WIN, wins, WIN, channels)
         outs, dqs, dks, dvs = [], [], [], []
         for u in range(wins):
-            part = qkv[:, u].reshape(POS, 3 * channels).astype(BF16)
-            q = part[:, :channels]
-            k = part[:, channels : 2 * channels]
-            v = part[:, 2 * channels :]
+            q = queries[:, u].reshape(POS, channels).astype(BF16)
+            k = keys[:, u].reshape(POS, channels).astype(BF16)
+            v = values[:, u].reshape(POS, channels).astype(BF16)
             do = dog[:, u].reshape(POS, channels).astype(BF16)
             qbd = jnp.concatenate([q * m for m in head_b], 0)
             dbd = jnp.concatenate([do * m for m in head_b], 0)
             s = dot(k, qbd, 1, 1) * scale + bias
-            valid = val_ref[:, w * wins + u : w * wins + u + 1]
+            valid = jnp.where(tile_col == key_col + u * WIN, marks, 0.0)
+            valid = jnp.sum(valid, 1, keepdims=True)
             allowed = same_pos | (jnp.broadcast_to(valid, (POS, lanes)) == 1.0)
             if w == bands - 1:
                 allowed = allowed & (same_row_half | jnp.logical_not(last_row))
@@ -128,17 +173,32 @@
             outs.append(o)
             dqs.append(dq * scale)
 
-        def patches(parts):
-            parts = [z.reshape(WIN, 1, WIN, channels) for z in parts]
-            return jnp.concatenate(parts, 1).reshape(rows, channels).astype(BF16)
+        def patches(pieces):
+            pieces = [z.reshape(WIN, 1, WIN, channels) for z in pieces]
+            return jnp.concatenate(pieces, 1).reshape(rows, channels)
 
         attn = patches(outs)
-        grads = jnp.concatenate([patches(dqs), patches(dks), patches(dvs)], 1)
-        shape = (2,) + rs_ref.shape[2:]
-        rs_ref[2 * w : 2 * w + 2, 0] = dot(attn, wp_ref[...], 1, 0).astype(BF16).reshape(shape)
-        rs_ref[2 * w : 2 * w + 2, 1] = dot(grads, wq_ref[...], 1, 1).astype(BF16).reshape(shape)
-        wt = wt + dot(ct, attn, 0, 0)
-
+        back = dot(patches(dqs).astype(BF16), wq_ref[0], 1, 1)
+        back = back + dot(patches(dks).astype(BF16), wq_ref[1], 1, 1)
+        back = (back + dot(patches(dvs).astype(BF16), wq_ref[2], 1, 1)).astype(BF16)
+        branch = dot(attn.astype(BF16), wp_ref[...], 1, 0).astype(BF16)
+        for i, x in enumerate(members):
+            out_ref[x, :own] = back[i * own : (i + 1) * own]
+            out_ref[x, own:] = branch[i * own : (i + 1) * own]
+        for slot, result in zip(slots, results):
+
+            @pl.when(slot // per_band == w)
+            def _(result=result):
+                result.start()
+
+        attn_cols[:, :SHIFT] = jnp.zeros((WIN, SHIFT, channels), F32)
+        attn_cols[:, SHIFT : SHIFT + ncol] = attn.reshape(WIN, ncol, channels)
+        for i in range(WIN):
+            at = (w * WIN + i) * SHIFT
+            attn_edge[at : at + SHIFT] = attn_cols[i, ncol : ncol + SHIFT]
+        wt = wt + dot(ct, attn_cols[:, :ncol].reshape(rows, channels).astype(BF16), 0, 0)
+
+    wt = wt + dot(edge, attn_edge[...].astype(BF16), 0, 0)
     halves = wt.reshape(d // 16, 2, 8, channels)
     first = core == 0
     keep_ref[: d // 16] = jnp.where(first, halves[:, 0], halves[:, 1])
@@ -161,24 +221,106 @@
     both = jnp.concatenate([total, jnp.zeros((8, channels - 128), F32)], 1)
     keep_ref[d // 16] = both
     send_ref[d // 16] = both
-
-
-def attention(flags, gathered, w_qkv, w_proj, table, valid):
-    d = w_proj.shape[1]
-    channels = w_proj.shape[0]
+    for result in results:
+        result.wait()
+
+
+def attention(ncol, flags, normed, grads, w_qkv, w_proj, table):
+    channels, d = w_proj.shape
+    parts = len(grads)
+    own = grads[0].shape[0]
+    prow = own // ncol
     piece = jax.ShapeDtypeStruct((d // 16 + 1, 8, channels), F32)
+    term = jax.ShapeDtypeStruct((2 * own, d), BF16)
     vmem = pl.BlockSpec(memory_space=pltpu.VMEM)
     return pl.pallas_call(
         attention_kernel,
-        out_shape=(jax.ShapeDtypeStruct(gathered.shape, BF16), piece, piece),
-        in_specs=[pl.BlockSpec(memory_space=pltpu.SMEM)] + [vmem] * 5,
-        out_specs=(vmem, vmem, vmem),
-        compiler_params=pltpu.CompilerParams(vmem_limit_bytes=44 * 1024 * 1024),
+        out_shape=(term,) * parts + (piece, piece),
+        in_specs=[pl.BlockSpec(memory_space=pltpu.SMEM)]
+        + [pl.BlockSpec(memory_space=pltpu.HBM)] * (2 * parts + 2)
+        + [vmem],
+        out_specs=(pl.BlockSpec(memory_space=pltpu.HBM),) * parts + (vmem, vmem),
+        scratch_shapes=[
+            pltpu.VMEM((parts,) + normed[0].shape, BF16),
+            pltpu.VMEM((parts,) + grads[0].shape, BF16),
+            pltpu.VMEM(w_qkv.shape, BF16),
+            pltpu.VMEM(w_proj.shape, BF16),
+            pltpu.VMEM((parts, 2 * own, d), BF16),
+            pltpu.VMEM((WIN, ncol + WIN, channels), F32),
+            pltpu.VMEM((WIN, ncol + WIN, channels), F32),
+            pltpu.VMEM((parts * prow * SHIFT, channels), F32),
+            pltpu.SemaphoreType.DMA((3 * parts + 2,)),
+        ],
+        compiler_params=pltpu.CompilerParams(vmem_limit_bytes=VMEM_LIMIT),
         cost_estimate=pl.CostEstimate(
             flops=3_000_000_000, bytes_accessed=9_000_000, transcendentals=131072
         ),
         name="window_attention",
-    )(flags, gathered, w_qkv, w_proj, table, valid)
+    )(flags, *normed, *grads, w_qkv, w_proj, table)
+
+
+def strips_kernel(tokens_ref, grads_ref, out_ref):
+    out_ref[...] = jnp.concatenate([tokens_ref[:, :SHIFT], grads_ref[:, :SHIFT]], 1)
+
+
+def left_strips(tokens, grads):
+    prow, ncol, d = tokens.shape
+    spec = pl.BlockSpec((prow, 16, d), lambda i: (0, 0, 0))
+    return pl.pallas_call(
+        strips_kernel,
+        grid=(1,),
+        out_shape=jax.ShapeDtypeStruct((prow, 2 * SHIFT, d), BF16),
+        in_specs=[spec, spec],
+        out_specs=pl.BlockSpec((prow, 2 * SHIFT, d), lambda i: (0, 0, 0)),
+        compiler_params=pltpu.CompilerParams(vmem_limit_bytes=VMEM_LIMIT),
+        cost_estimate=pl.CostEstimate(flops=0, bytes_accessed=300_000, transcendentals=0),
+        name="left_strips",
+    )(tokens, grads)
+
+
+def norm_kernel(tokens_ref, strips_ref, gain_ref, valid_ref, out_ref, cols, strip_rows):
+    prow, ncol, d = tokens_ref.shape
+    own = prow * ncol
+    strip = prow * SHIFT
+    cols[:, :ncol] = tokens_ref[...].astype(F32)
+    for i in range(prow):
+        both = strips_ref[i].astype(F32)
+        cols[i, ncol : ncol + SHIFT] = both[:SHIFT]
+        strip_rows[i * SHIFT : (i + 1) * SHIFT] = both[SHIFT:]
+    x = cols[:, SHIFT : SHIFT + ncol].reshape(own, d)
+    x = x - jnp.mean(x, -1, keepdims=True)
+    rstd = lax.rsqrt(jnp.mean(x * x, -1, keepdims=True) + EPS)
+    out_ref[:own] = (x * rstd * gain_ref[...]).astype(BF16)
+    out_ref[own : own + strip] = strip_rows[...].astype(BF16)
+    out_ref[own + strip :] = jnp.zeros((valid_ref.shape[0], d), BF16)
+    out_ref[own + strip :, :ncol] = valid_ref[...].astype(F32).astype(BF16)
+
+
+def norm(tokens, strips, gain, valid):
+    prow, ncol, d = tokens.shape
+    strip = prow * SHIFT
+    vmem = pl.BlockSpec(memory_space=pltpu.VMEM)
+    return pl.pallas_call(
+        norm_kernel,
+        out_shape=jax.ShapeDtypeStruct((prow * ncol + strip + valid.shape[0], d), BF16),
+        in_specs=[vmem] * 4,
+        out_specs=vmem,
+        scratch_shapes=[pltpu.VMEM((prow, ncol + WIN, d), F32), pltpu.VMEM((strip, d), F32)],
+        compiler_params=pltpu.CompilerParams(vmem_limit_bytes=VMEM_LIMIT),
+        cost_estimate=pl.CostEstimate(
+            flops=1_500_000, bytes_accessed=600_000, transcendentals=128
+        ),
+        name="layer_norm",
+    )(tokens, strips, gain, valid)
+
+
+ROUTES = (
+    ((0, 3), (0, 0), (0, 1), (1, 2)),
+    ((-1, 1), (0, 2), (0, 3), (0, 0)),
+    ((0, 2), (0, 3), (0, 0), (0, 1)),
+    ((-1, 0), (0, 1), (0, 2), (1, 3)),
+)
+SLOTS = ((0, 2, 1, 3), (1, 3, 2, 0), (2, 0, 3, 1), (3, 1, 0, 2))
 
 
 def on_device(tokens, valid, gain, w_qkv, w_proj, rel_table, cotangent):
@@ -187,80 +329,83 @@
     n_row = lax.axis_size("row")
     n_col = lax.axis_size("col")
     tile_rows = part_rows * n_head
+    own = part_rows * ncol
+    strip = part_rows * SHIFT
     channels = w_proj.shape[0]
     row = lax.axis_index("row")
     col = lax.axis_index("col")
     head = lax.axis_index("head")
 
-    groups = [
-        [r * n_head + h for h in range(1, n_head)] + [(r + 1) % n_row * n_head]
-        for r in range(n_row)
-    ]
     left = [(c, (c - 1) % n_col) for c in range(n_col)]
     right = [(c, (c + 1) % n_col) for c in range(n_col)]
-
-    strips = jnp.stack([tokens[:, :SHIFT], cotangent[:, :SHIFT]])
+    swap = [(c, c ^ 1) for c in range(n_col)]
+    routes = [
+        [
+            (r * n_head + x, (r + step) % n_row * n_head + h)
+            for r in range(n_row)
+            for x, (step, h) in enumerate(route)
+        ]
+        for route in ROUTES
+    ]
+    returns = [[(b, a) for a, b in route] for route in routes]
+
+    def send(value, route):
+        return lax.ppermute(value, ("row", "head"), route)
+
+    strips = left_strips(tokens, cotangent)
+    sent, _ = lax.optimization_barrier((cotangent, strips))
     strips = lax.ppermute(strips, "col", left)
-    down = [(r * n_head, (r + 1) % n_row * n_head) for r in range(n_row)]
-    val = valid.astype(F32).reshape(tile_rows // WIN, WIN, ncol // WIN, WIN)
-    val = val.transpose(1, 3, 0, 2).reshape(POS, -1)
-    val = jnp.where(head == 0, lax.ppermute(val, ("row", "head"), down), val)
-
-    moved = jnp.concatenate([tokens[:, SHIFT:], strips[0]], 1).astype(F32)
-    mean = jnp.mean(moved, -1, keepdims=True)
-    centered = moved - mean
-    rstd = lax.rsqrt(jnp.mean(centered * centered, -1, keepdims=True) + EPS)
-    normed = (centered * rstd * gain).astype(BF16)
-    moved_grad = jnp.concatenate([cotangent[:, SHIFT:], strips[1]], 1)
-    packet = jnp.stack([normed, moved_grad])
-    packet = jnp.broadcast_to(packet[None], (n_head,) + packet.shape)
-    gathered = lax.all_to_all(
-        packet, ("row", "head"), 0, 0, axis_index_groups=groups, tiled=True
+    grads = [send(sent.reshape(own, d), route) for route in routes]
+
+    normed = norm(tokens, strips, gain[None], valid)
+    normed = [send(normed, route) for route in routes]
+
+    last = jnp.where(head >= 2, row == 0, row == n_row - 1)
+    flags = [last.astype(jnp.int32), (col == n_col - 1).astype(jnp.int32), col % 2, head]
+    flags = jnp.stack(flags)
+    outs = attention(
+        ncol,
+        flags,
+        normed,
+        grads,
+        w_qkv.transpose(1, 0, 2),
+        w_proj,
+        table_to_rows(rel_table),
     )
-
-    tile = jnp.where(head == 0, (row + n_row - 1) % n_row, row)
-    flags = jnp.stack([tile == n_row - 1, col == n_col - 1, col % 2 == 1]).astype(jnp.int32)
-    terms, keep, send = attention(
-        flags, gathered, w_qkv.reshape(d, 3 * channels), w_proj, table_to_rows(rel_table), val
-    )
-
-    swap = [(c, c ^ 1) for c in range(n_col)]
-    got = lax.ppermute(send, "col", swap)
-    shares = lax.all_to_all(terms, ("row", "head"), 0, 0, axis_index_groups=groups, tiled=True)
-    summed = jnp.sum(shares.astype(F32), 0)
-    edge = lax.ppermute(summed[:, :, -SHIFT:].astype(BF16), "col", right).astype(F32)
-    summed = jnp.concatenate([edge, summed[:, :, :-SHIFT]], 2)
-
-    pair = keep + got
-    pieces = pair[:-1].astype(BF16)
-    table_part = pair[-1, :, :128]
-    table_hi = table_part.astype(BF16)
-    table_lo = (table_part - table_hi.astype(F32)).astype(BF16)
-    table_part = jnp.concatenate([table_hi, table_lo], 1)
-    table_part = jnp.broadcast_to(table_part[None], (pieces.shape[0],) + table_part.shape)
-    pieces = jnp.concatenate([pieces, table_part], 1)
+    terms = [send(part, route) for part, route in zip(outs[:n_head], returns)]
+
+    pair = outs[-2] + lax.ppermute(outs[-1], "col", swap)
+    table_part = jnp.broadcast_to(pair[-1:, :, :128], (d // 16, 8, 128))
+    pieces = jnp.concatenate([pair[:-1], table_part], 2).astype(BF16)
     cores = [
         [r * n_col + c for r in range(n_row) for c in range(n_col) if c % 2 == parity]
         for parity in range(2)
     ]
+    _, *terms = lax.optimization_barrier((pieces, *terms))
     pieces = lax.all_to_all(pieces, ("row", "col"), 0, 0, axis_index_groups=cores, tiled=True)
     pieces = jnp.sum(pieces.astype(F32), 0)
     scale = 1.0 / math.sqrt(tile_rows * ncol * n_row * n_col)
-    proj_grad = pieces[:8].T * scale
-    table_grad = rows_to_table(pieces[8:, :128] + pieces[8:, 128:]) * (WIN * scale)
+    proj_grad = pieces[:, :channels].T * scale
+    table_grad = rows_to_table(pieces[:, channels:]) * (WIN * scale)
+
+    total = sum(part.astype(F32) for part in terms).reshape(2, part_rows, ncol, d)
+    edges = lax.ppermute(total[:, :, -SHIFT:].astype(BF16), "col", right).astype(F32)
+    total = jnp.concatenate([edges, total[:, :, :-SHIFT]], 2)
+    norm_grad = total[0]
 
     flat = tokens.astype(F32)
     mean = jnp.mean(flat, -1, keepdims=True)
     centered = flat - mean
     rstd = lax.rsqrt(jnp.mean(centered * centered, -1, keepdims=True) + EPS)
     xhat = centered * rstd
-    mixed = (flat + summed[0]).astype(BF16)
-    scaled = summed[1] * gain
+    scaled = norm_grad * gain
     token_gradient = cotangent.astype(F32) + rstd * (
         scaled
         - jnp.mean(scaled, -1, keepdims=True)
         - xhat * jnp.mean(scaled * xhat, -1, keepdims=True)
     )
+
+    mixed = (flat + total[1]).astype(BF16)
     return (mixed, token_gradient.astype(BF16), proj_grad, table_grad)
 
 

time: 166 us -> 119 us (0.72)
  the two profiles are of different devices: /device:TPU:4 before, /device:TPU:6 now
where the time goes in v2:
time: 119 us; the launch traced here: 118 us
  starting transfers between devices  64.6 us (54%)
  waiting for transfers between devices  27.9 us (23%)
  Pallas kernels  14.2 us (12%)
  other arithmetic  6.55 us (6%)
  local copies, waits for them, and re-layouts  3.47 us (3%)
    ppermute x12, starting transfers between devices, send(): return lax.ppermute(value, ('row', 'head'), route)  50.7 us
    ppermute x12, waiting for transfers between devices, send(): return lax.ppermute(value, ('row', 'head'), route)  20.4 us
    pallas_call x1, Pallas kernels, attention(): pl.pallas_call(attention_kernel, out_shape=(term,) * parts + (piece, piec...  10.6 us
    ppermute x1, waiting for transfers between devices, on_device(): lax.ppermute(total[:, :, -SHIFT:].astype(BF16), 'col', right).astype(F32)  7.55 us
    all_to_all x1, starting transfers between devices, on_device(): lax.all_to_all(pieces, ('row', 'col'), 0, 0, axis_index_groups=cores, til...  7.44 us
    ppermute x1, starting transfers between devices, on_device(): strips = lax.ppermute(strips, 'col', left)  2.53 us
  transfers between devices with their start and end apart: 16, of which 5 were waited for; matrix products, arithmetic and copies ran while one was open for 6% of the time, Pallas kernels for 2%

profile of v2, /device:TPU:6, one launch (start us, length us, event | category | flops | bytes accessed | tf_op | source)
XLA Modules:
  0.0 117.9 jit_solution(11306940712983464697)
XLA Ops:
  0.6 1.6 %left_strips.1 = bf16[4,8,1024]{2,1,0:T(8,128)(2,1)} custom-call(bf16[4,32,1024]{2,1,0:T(8,128)(2,1)} %tokens_ref.3, bf16[4,32,1024]{2,1,0:T(8,128)(2,1)} %grads_ref.1), custom_call_target="tpu_custom_call" | custom-call | bytes 300000 | tf_op jit(solution)/shard_map/left_strips/pallas_call | solution.py:269
  2.3 3.7 %collective-permute-start.5 = (bf16[128,1024]{1,0:T(8,128)(2,1)}, bf16[128,1024]{1,0:T(8,128)(2,1)S(1)}, u32[]{:S(2)}, u32[]{:S(2)}) collective-permute-start(bf16[128,1024]{1,0:T(8,128)(2,1)} %bitcast.29), channel_id=1, source_target_pairs={{0,3},{1,0},{2,1},{3,18},{16,19},{17,16},{18,17},{19,34},{32,35},{... | collective-permute-start | bytes 786440 | tf_op jit(solution)/shard_map/ppermute | solution.py:353
  6.0 5.9 %collective-permute-start.6 = (bf16[128,1024]{1,0:T(8,128)(2,1)}, bf16[128,1024]{1,0:T(8,128)(2,1)S(1)}, u32[]{:S(2)}, u32[]{:S(2)}) collective-permute-start(bf16[128,1024]{1,0:T(8,128)(2,1)} %bitcast.30), channel_id=1, source_target_pairs={{0,497},{1,2},{2,3},{3,0},{16,1},{17,18},{18,19},{19,16},{32,17},{... | collective-permute-start | bytes 786440 | tf_op jit(solution)/shard_map/ppermute | solution.py:353
  11.9 3.4 %collective-permute-start.7 = (bf16[128,1024]{1,0:T(8,128)(2,1)}, bf16[128,1024]{1,0:T(8,128)(2,1)S(1)}, u32[]{:S(2)}, u32[]{:S(2)}) collective-permute-start(bf16[128,1024]{1,0:T(8,128)(2,1)} %bitcast.31), channel_id=1, source_target_pairs={{0,2},{1,3},{2,0},{3,1},{16,18},{17,19},{18,16},{19,17},{32,34},{3... | collective-permute-start | bytes 786440 | tf_op jit(solution)/shard_map/ppermute | solution.py:353
  15.3 2.5 %collective-permute-start = (bf16[4,8,1024]{2,1,0:T(8,128)(2,1)}, bf16[4,8,1024]{2,1,0:T(8,128)(2,1)S(1)}, u32[]{:S(2)}, u32[]{:S(2)}) collective-permute-start(bf16[4,8,1024]{2,1,0:T(8,128)(2,1)} %left_strips.1), channel_id=1, source_target_pairs={{0,12},{4,0},{8,4},{12,8},{1,13},{5,1},{9,5},{13,9},{2,14},{6,2},{... | collective-permute-start | bytes 196616 | tf_op jit(solution)/shard_map/ppermute | solution.py:357
  17.9 2.6 %collective-permute-start.8 = (bf16[128,1024]{1,0:T(8,128)(2,1)}, bf16[128,1024]{1,0:T(8,128)(2,1)S(1)}, u32[]{:S(2)}, u32[]{:S(2)}) collective-permute-start(bf16[128,1024]{1,0:T(8,128)(2,1)} %bitcast.32), channel_id=1, source_target_pairs={{0,496},{1,1},{2,2},{3,19},{16,0},{17,17},{18,18},{19,35},{32,16},... | collective-permute-start | bytes 786440 | tf_op jit(solution)/shard_map/ppermute | solution.py:353
  20.5 0.8 reshape.51
  21.3 0.0 collective-permute-done.strips_ref
  21.3 0.0 copy-start.2
  21.3 0.6 copy-done.2
  21.9 2.0 %layer_norm.1 = bf16[160,1024]{1,0:T(8,128)(2,1)} custom-call(bf16[4,32,1024]{2,1,0:T(8,128)(2,1)} %tokens_ref.3, bf16[4,8,1024]{2,1,0:T(8,128)(2,1)} %copy-done.2, f32[1,1024]{1,0:T(1,128)} %bitcast.36, s32[16,32]{1,0:T(8,128)} %valid_ref.1), custom_call_target="tpu_custom_call" | custom-call | flops 1500000 | bytes 600000 | tf_op jit(solution)/shard_map/layer_norm/pallas_call | solution.py:303
  23.9 2.6 %collective-permute-start.1 = (bf16[160,1024]{1,0:T(8,128)(2,1)}, bf16[160,1024]{1,0:T(8,128)(2,1)S(1)}, u32[]{:S(2)}, u32[]{:S(2)}) collective-permute-start(bf16[160,1024]{1,0:T(8,128)(2,1)} %layer_norm.1), channel_id=1, source_target_pairs={{0,3},{1,0},{2,1},{3,18},{16,19},{17,16},{18,17},{19,34},{32,35},{... | collective-permute-start | bytes 983048 | tf_op jit(solution)/shard_map/ppermute | solution.py:353
  26.5 0.0 collective-permute-done.5.c1
  26.5 0.0 copy-start.8
  26.5 11.4 %collective-permute-start.2 = (bf16[160,1024]{1,0:T(8,128)(2,1)}, bf16[160,1024]{1,0:T(8,128)(2,1)S(1)}, u32[]{:S(2)}, u32[]{:S(2)}) collective-permute-start(bf16[160,1024]{1,0:T(8,128)(2,1)} %layer_norm.1), channel_id=1, source_target_pairs={{0,497},{1,2},{2,3},{3,0},{16,1},{17,18},{18,19},{19,16},{32,17},{... | collective-permute-start | bytes 983048 | tf_op jit(solution)/shard_map/ppermute | solution.py:353
  37.9 0.0 collective-permute-done.6.c2
  37.9 0.0 copy-start.9
  37.9 3.4 %collective-permute-start.3 = (bf16[160,1024]{1,0:T(8,128)(2,1)}, bf16[160,1024]{1,0:T(8,128)(2,1)S(1)}, u32[]{:S(2)}, u32[]{:S(2)}) collective-permute-start(bf16[160,1024]{1,0:T(8,128)(2,1)} %layer_norm.1), channel_id=1, source_target_pairs={{0,2},{1,3},{2,0},{3,1},{16,18},{17,19},{18,16},{19,17},{32,34},{3... | collective-permute-start | bytes 983048 | tf_op jit(solution)/shard_map/ppermute | solution.py:353
  41.3 0.0 collective-permute-done.7.c3
  41.3 0.0 copy-start.10
  41.3 1.9 %collective-permute-start.4 = (bf16[160,1024]{1,0:T(8,128)(2,1)}, bf16[160,1024]{1,0:T(8,128)(2,1)S(1)}, u32[]{:S(2)}, u32[]{:S(2)}) collective-permute-start(bf16[160,1024]{1,0:T(8,128)(2,1)} %layer_norm.1), channel_id=1, source_target_pairs={{0,496},{1,1},{2,2},{3,19},{16,0},{17,17},{18,18},{19,35},{32,16},... | collective-permute-start | bytes 983048 | tf_op jit(solution)/shard_map/ppermute | solution.py:353
  43.3 0.1 slice_reduce_fusion.1
  43.4 0.1 reshape_squeeze.7
  43.5 0.1 slice.53
  43.5 0.1 reshape_squeeze.6
  43.6 0.6 pad_add_fusion.flags_ref
  44.2 0.7 maximum_maximum_fusion.tab_ref
  44.9 0.0 collective-permute-done.8.c4
  44.9 0.0 collective-permute-done.1.x1
  44.9 7.0 %collective-permute-done.2.x2 = bf16[160,1024]{1,0:T(8,128)(2,1)S(1)} collective-permute-done((bf16[160,1024]{1,0:T(8,128)(2,1)}, bf16[160,1024]{1,0:T(8,128)(2,1)S(1)}, u32[]{:S(2)}, u32[]{:S(2)}) %collective-permute-start.2) | collective-permute-done | bytes 327712 | tf_op jit(solution)/shard_map/ppermute | solution.py:353
  52.0 1.7 %collective-permute-done.3.x3 = bf16[160,1024]{1,0:T(8,128)(2,1)S(1)} collective-permute-done((bf16[160,1024]{1,0:T(8,128)(2,1)}, bf16[160,1024]{1,0:T(8,128)(2,1)S(1)}, u32[]{:S(2)}, u32[]{:S(2)}) %collective-permute-start.3) | collective-permute-done | bytes 327712 | tf_op jit(solution)/shard_map/ppermute | solution.py:353
  53.7 3.5 %collective-permute-done.4.x4 = bf16[160,1024]{1,0:T(8,128)(2,1)S(1)} collective-permute-done((bf16[160,1024]{1,0:T(8,128)(2,1)}, bf16[160,1024]{1,0:T(8,128)(2,1)S(1)}, u32[]{:S(2)}, u32[]{:S(2)}) %collective-permute-start.4) | collective-permute-done | bytes 327712 | tf_op jit(solution)/shard_map/ppermute | solution.py:353
  57.2 0.7 copy-done.7
  57.9 10.6 %window_attention.1 = (bf16[256,1024]{1,0:T(8,128)(2,1)}, bf16[256,1024]{1,0:T(8,128)(2,1)}, bf16[256,1024]{1,0:T(8,128)(2,1)}, bf16[256,1024]{1,0:T(8,128)(2,1)...) custom-call(s32[4]{0:T(128)} %pad_add_fusion.flags_ref, bf16[160,1024]{1,0:T(8,128)(2,1)} %copy-done.4, ...), custom_call_target="tpu_custom_call" | custom-call | flops 3000000000 | bytes 9000000 | tf_op jit(solution)/shard_map/window_attention/pallas_call | solution.py:236
  68.5 1.9 %collective-permute-start.9 = (f32[65,8,256]{2,1,0:T(8,128)}, f32[65,8,256]{2,1,0:T(8,128)S(1)}, u32[]{:S(2)}, u32[]{:S(2)}) collective-permute-start(f32[65,8,256]{2,1,0:T(8,128)} %get-tuple-element.17), channel_id=1, source_target_pairs={{0,4},{4,0},{8,12},{12,8},{1,5},{5,1},{9,13},{13,9},{2,6},{6,2},{1... | collective-permute-start | bytes 1597448 | tf_op jit(solution)/shard_map/ppermute | solution.py:377
  70.4 0.1 convert_reduce_fusion.1
  70.5 2.6 %collective-permute-start.10 = (bf16[256,1024]{1,0:T(8,128)(2,1)}, bf16[256,1024]{1,0:T(8,128)(2,1)S(1)}, u32[]{:S(2)}, u32[]{:S(2)}) collective-permute-start(bf16[256,1024]{1,0:T(8,128)(2,1)} %get-tuple-element.18), channel_id=1, source_target_pairs={{3,0},{0,1},{1,2},{18,3},{19,16},{16,17},{17,18},{34,19},{35,32},{... | collective-permute-start | bytes 1572872 | tf_op jit(solution)/shard_map/ppermute | solution.py:353
  73.1 2.3 %collective-permute-start.11 = (bf16[256,1024]{1,0:T(8,128)(2,1)}, bf16[256,1024]{1,0:T(8,128)(2,1)S(1)}, u32[]{:S(2)}, u32[]{:S(2)}) collective-permute-start(bf16[256,1024]{1,0:T(8,128)(2,1)} %get-tuple-element.19), channel_id=1, source_target_pairs={{497,0},{2,1},{3,2},{0,3},{1,16},{18,17},{19,18},{16,19},{17,32},{... | collective-permute-start | bytes 1572872 | tf_op jit(solution)/shard_map/ppermute | solution.py:353
  75.5 1.9 %collective-permute-start.12 = (bf16[256,1024]{1,0:T(8,128)(2,1)}, bf16[256,1024]{1,0:T(8,128)(2,1)S(1)}, u32[]{:S(2)}, u32[]{:S(2)}) collective-permute-start(bf16[256,1024]{1,0:T(8,128)(2,1)} %get-tuple-element.20), channel_id=1, source_target_pairs={{2,0},{3,1},{0,2},{1,3},{18,16},{19,17},{16,18},{17,19},{34,32},{3... | collective-permute-start | bytes 1572872 | tf_op jit(solution)/shard_map/ppermute | solution.py:353
  77.4 8.9 %collective-permute-start.13 = (bf16[256,1024]{1,0:T(8,128)(2,1)}, bf16[256,1024]{1,0:T(8,128)(2,1)S(1)}, u32[]{:S(2)}, u32[]{:S(2)}) collective-permute-start(bf16[256,1024]{1,0:T(8,128)(2,1)} %get-tuple-element.21), channel_id=1, source_target_pairs={{496,0},{1,1},{2,2},{19,3},{0,16},{17,17},{18,18},{35,19},{16,32},... | collective-permute-start | bytes 1572872 | tf_op jit(solution)/shard_map/ppermute | solution.py:353
  86.3 0.2 fusion.9
  86.5 0.0 collective-permute-done.9
  86.6 1.1 add.36
  87.7 0.8 pad_maximum_fusion.1
  88.5 7.4 %all-to-all-start = ((bf16[64,8,384]{2,1,0:T(8,128)(2,1)}), bf16[64,8,384]{2,1,0:T(8,128)(2,1)S(1)}, u32[]{:S(2)}, u32[]{:S(2)}) async-start(bf16[64,8,384]{2,1,0:T(8,128)(2,1)} %pad_maximum_fusion.1), calls=%async_computation | async-start | bytes 786432 | tf_op jit(solution)/shard_map/all_to_all | solution.py:385
  96.0 0.0 copy-start.3
  96.0 0.0 collective-permute-done.10
  96.0 0.0 collective-permute-done.11
  96.0 8.1 %collective-permute-done.12 = bf16[256,1024]{1,0:T(8,128)(2,1)S(1)} collective-permute-done((bf16[256,1024]{1,0:T(8,128)(2,1)}, bf16[256,1024]{1,0:T(8,128)(2,1)S(1)}, u32[]{:S(2)}, u32[]{:S(2)}) %collective-permute-start.12) | collective-permute-done | bytes 524320 | tf_op jit(solution)/shard_map/ppermute | solution.py:353
  104.1 0.0 collective-permute-done.13
  104.1 0.3 convert_add_fusion
  104.5 0.0 copy-start.1
  104.5 2.1 %collective-permute-start.14 = (bf16[2,4,4,1024]{3,2,1,0:T(4,128)(2,1)S(1)}, bf16[2,4,4,1024]{3,2,1,0:T(4,128)(2,1)S(1)}, u32[]{:S(2)}, u32[]{:S(2)}) collective-permute-start(bf16[2,4,4,1024]{3,2,1,0:T(4,128)(2,1)S(1)} %slice.101), channel_id=1, source_target_pairs={{0,4},{4,8},{8,12},{12,0},{1,5},{5,9},{9,13},{13,1},{2,6},{6,10},{... | collective-permute-start | bytes 196616 | tf_op jit(solution)/shard_map/ppermute | solution.py:392
  106.6 7.6 %collective-permute-done.14 = bf16[2,4,4,1024]{3,2,1,0:T(4,128)(2,1)S(1)} collective-permute-done((bf16[2,4,4,1024]{3,2,1,0:T(4,128)(2,1)S(1)}, bf16[2,4,4,1024]{3,2,1,0:T(4,128)(2,1)S(1)}, u32[]{:S(2)}, u32[]{:S(2)}) %collective-permute-start.14) | collective-permute-done | bytes 65568 | tf_op jit(solution)/shard_map/ppermute | solution.py:392
  114.2 1.0 fusion.17
  115.1 1.0 fusion.8
  116.1 0.0 all-to-all-done
  116.1 0.1 convert_reduce_fusion
  116.2 0.1 slice.76
  116.3 0.6 fusion.15
  116.9 0.1 pad_maximum_fusion.3
  117.0 0.1 stack_reshape.7
  117.0 0.1 stack_reshape.6
  117.2 0.7 mul.71
  (30 shorter events, 0.2 us)
Async XLA Ops:
  2.3 24.2 %collective-permute-start.5 = (bf16[128,1024]{1,0:T(8,128)(2,1)}, bf16[128,1024]{1,0:T(8,128)(2,1)S(1)}, u32[]{:S(2)}, u32[]{:S(2)}) collective-permute-start(bf16[128,1024]{1,0:T(8,128)(2,1)} %bitcast.29), channel_id=1, source_target_pairs={{0,3},{1,0},{2,1},{3,18},{16,19},{17,16},{18,17},{19,34},{32,35},{... | collective-permute-start | bytes 786440 | tf_op jit(solution)/shard_map/ppermute | solution.py:353
  6.0 31.9 %collective-permute-start.6 = (bf16[128,1024]{1,0:T(8,128)(2,1)}, bf16[128,1024]{1,0:T(8,128)(2,1)S(1)}, u32[]{:S(2)}, u32[]{:S(2)}) collective-permute-start(bf16[128,1024]{1,0:T(8,128)(2,1)} %bitcast.30), channel_id=1, source_target_pairs={{0,497},{1,2},{2,3},{3,0},{16,1},{17,18},{18,19},{19,16},{32,17},{... | collective-permute-start | bytes 786440 | tf_op jit(solution)/shard_map/ppermute | solution.py:353
  11.9 29.4 %collective-permute-start.7 = (bf16[128,1024]{1,0:T(8,128)(2,1)}, bf16[128,1024]{1,0:T(8,128)(2,1)S(1)}, u32[]{:S(2)}, u32[]{:S(2)}) collective-permute-start(bf16[128,1024]{1,0:T(8,128)(2,1)} %bitcast.31), channel_id=1, source_target_pairs={{0,2},{1,3},{2,0},{3,1},{16,18},{17,19},{18,16},{19,17},{32,34},{3... | collective-permute-start | bytes 786440 | tf_op jit(solution)/shard_map/ppermute | solution.py:353
  15.3 5.9 %collective-permute-start = (bf16[4,8,1024]{2,1,0:T(8,128)(2,1)}, bf16[4,8,1024]{2,1,0:T(8,128)(2,1)S(1)}, u32[]{:S(2)}, u32[]{:S(2)}) collective-permute-start(bf16[4,8,1024]{2,1,0:T(8,128)(2,1)} %left_strips.1), channel_id=1, source_target_pairs={{0,12},{4,0},{8,4},{12,8},{1,13},{5,1},{9,5},{13,9},{2,14},{6,2},{... | collective-permute-start | bytes 196616 | tf_op jit(solution)/shard_map/ppermute | solution.py:357
  17.9 27.0 %collective-permute-start.8 = (bf16[128,1024]{1,0:T(8,128)(2,1)}, bf16[128,1024]{1,0:T(8,128)(2,1)S(1)}, u32[]{:S(2)}, u32[]{:S(2)}) collective-permute-start(bf16[128,1024]{1,0:T(8,128)(2,1)} %bitcast.32), channel_id=1, source_target_pairs={{0,496},{1,1},{2,2},{3,19},{16,0},{17,17},{18,18},{19,35},{32,16},... | collective-permute-start | bytes 786440 | tf_op jit(solution)/shard_map/ppermute | solution.py:353
  21.3 0.6 copy-start.2
  23.9 21.0 %collective-permute-start.1 = (bf16[160,1024]{1,0:T(8,128)(2,1)}, bf16[160,1024]{1,0:T(8,128)(2,1)S(1)}, u32[]{:S(2)}, u32[]{:S(2)}) collective-permute-start(bf16[160,1024]{1,0:T(8,128)(2,1)} %layer_norm.1), channel_id=1, source_target_pairs={{0,3},{1,0},{2,1},{3,18},{16,19},{17,16},{18,17},{19,34},{32,35},{... | collective-permute-start | bytes 983048 | tf_op jit(solution)/shard_map/ppermute | solution.py:353
  26.5 30.6 %copy-start.8 = (bf16[128,1024]{1,0:T(8,128)(2,1)}, bf16[128,1024]{1,0:T(8,128)(2,1)S(1)}, u32[]{:S(2)}) copy-start(bf16[128,1024]{1,0:T(8,128)(2,1)S(1)} %collective-permute-done.5.c1) | copy-start | bytes 786436
  26.5 25.4 %collective-permute-start.2 = (bf16[160,1024]{1,0:T(8,128)(2,1)}, bf16[160,1024]{1,0:T(8,128)(2,1)S(1)}, u32[]{:S(2)}, u32[]{:S(2)}) collective-permute-start(bf16[160,1024]{1,0:T(8,128)(2,1)} %layer_norm.1), channel_id=1, source_target_pairs={{0,497},{1,2},{2,3},{3,0},{16,1},{17,18},{18,19},{19,16},{32,17},{... | collective-permute-start | bytes 983048 | tf_op jit(solution)/shard_map/ppermute | solution.py:353
  37.9 19.2 %copy-start.9 = (bf16[128,1024]{1,0:T(8,128)(2,1)}, bf16[128,1024]{1,0:T(8,128)(2,1)S(1)}, u32[]{:S(2)}) copy-start(bf16[128,1024]{1,0:T(8,128)(2,1)S(1)} %collective-permute-done.6.c2) | copy-start | bytes 786436
  37.9 15.7 %collective-permute-start.3 = (bf16[160,1024]{1,0:T(8,128)(2,1)}, bf16[160,1024]{1,0:T(8,128)(2,1)S(1)}, u32[]{:S(2)}, u32[]{:S(2)}) collective-permute-start(bf16[160,1024]{1,0:T(8,128)(2,1)} %layer_norm.1), channel_id=1, source_target_pairs={{0,2},{1,3},{2,0},{3,1},{16,18},{17,19},{18,16},{19,17},{32,34},{3... | collective-permute-start | bytes 983048 | tf_op jit(solution)/shard_map/ppermute | solution.py:353
  41.3 15.8 %copy-start.10 = (bf16[128,1024]{1,0:T(8,128)(2,1)}, bf16[128,1024]{1,0:T(8,128)(2,1)S(1)}, u32[]{:S(2)}) copy-start(bf16[128,1024]{1,0:T(8,128)(2,1)S(1)} %collective-permute-done.7.c3) | copy-start | bytes 786436
  41.3 15.8 %collective-permute-start.4 = (bf16[160,1024]{1,0:T(8,128)(2,1)}, bf16[160,1024]{1,0:T(8,128)(2,1)S(1)}, u32[]{:S(2)}, u32[]{:S(2)}) collective-permute-start(bf16[160,1024]{1,0:T(8,128)(2,1)} %layer_norm.1), channel_id=1, source_target_pairs={{0,496},{1,1},{2,2},{3,19},{16,0},{17,17},{18,18},{19,35},{32,16},... | collective-permute-start | bytes 983048 | tf_op jit(solution)/shard_map/ppermute | solution.py:353
  44.9 12.3 %copy-start.11 = (bf16[128,1024]{1,0:T(8,128)(2,1)}, bf16[128,1024]{1,0:T(8,128)(2,1)S(1)}, u32[]{:S(2)}) copy-start(bf16[128,1024]{1,0:T(8,128)(2,1)S(1)} %collective-permute-done.8.c4) | copy-start | bytes 786436
  44.9 12.3 %copy-start.4 = (bf16[160,1024]{1,0:T(8,128)(2,1)}, bf16[160,1024]{1,0:T(8,128)(2,1)S(1)}, u32[]{:S(2)}) copy-start(bf16[160,1024]{1,0:T(8,128)(2,1)S(1)} %collective-permute-done.1.x1) | copy-start | bytes 983044
  52.0 5.2 %copy-start.5 = (bf16[160,1024]{1,0:T(8,128)(2,1)}, bf16[160,1024]{1,0:T(8,128)(2,1)S(1)}, u32[]{:S(2)}) copy-start(bf16[160,1024]{1,0:T(8,128)(2,1)S(1)} %collective-permute-done.2.x2) | copy-start | bytes 983044
  53.7 3.5 %copy-start.6 = (bf16[160,1024]{1,0:T(8,128)(2,1)}, bf16[160,1024]{1,0:T(8,128)(2,1)S(1)}, u32[]{:S(2)}) copy-start(bf16[160,1024]{1,0:T(8,128)(2,1)S(1)} %collective-permute-done.3.x3) | copy-start | bytes 983044
  57.1 0.7 copy-start.7
  57.9 12.5 %copy-start = (bf16[4,32,1024]{2,1,0:T(8,128)(2,1)S(1)}, bf16[4,32,1024]{2,1,0:T(8,128)(2,1)}, u32[]{:S(2)}) copy-start(bf16[4,32,1024]{2,1,0:T(8,128)(2,1)} %tokens_ref.3) | copy-start | bytes 786436
  68.5 18.1 %collective-permute-start.9 = (f32[65,8,256]{2,1,0:T(8,128)}, f32[65,8,256]{2,1,0:T(8,128)S(1)}, u32[]{:S(2)}, u32[]{:S(2)}) collective-permute-start(f32[65,8,256]{2,1,0:T(8,128)} %get-tuple-element.17), channel_id=1, source_target_pairs={{0,4},{4,0},{8,12},{12,8},{1,5},{5,1},{9,13},{13,9},{2,6},{6,2},{1... | collective-permute-start | bytes 1597448 | tf_op jit(solution)/shard_map/ppermute | solution.py:377
  70.5 25.5 %collective-permute-start.10 = (bf16[256,1024]{1,0:T(8,128)(2,1)}, bf16[256,1024]{1,0:T(8,128)(2,1)S(1)}, u32[]{:S(2)}, u32[]{:S(2)}) collective-permute-start(bf16[256,1024]{1,0:T(8,128)(2,1)} %get-tuple-element.18), channel_id=1, source_target_pairs={{3,0},{0,1},{1,2},{18,3},{19,16},{16,17},{17,18},{34,19},{35,32},{... | collective-permute-start | bytes 1572872 | tf_op jit(solution)/shard_map/ppermute | solution.py:353
  73.1 22.8 %collective-permute-start.11 = (bf16[256,1024]{1,0:T(8,128)(2,1)}, bf16[256,1024]{1,0:T(8,128)(2,1)S(1)}, u32[]{:S(2)}, u32[]{:S(2)}) collective-permute-start(bf16[256,1024]{1,0:T(8,128)(2,1)} %get-tuple-element.19), channel_id=1, source_target_pairs={{497,0},{2,1},{3,2},{0,3},{1,16},{18,17},{19,18},{16,19},{17,32},{... | collective-permute-start | bytes 1572872 | tf_op jit(solution)/shard_map/ppermute | solution.py:353
  75.5 28.7 %collective-permute-start.12 = (bf16[256,1024]{1,0:T(8,128)(2,1)}, bf16[256,1024]{1,0:T(8,128)(2,1)S(1)}, u32[]{:S(2)}, u32[]{:S(2)}) collective-permute-start(bf16[256,1024]{1,0:T(8,128)(2,1)} %get-tuple-element.20), channel_id=1, source_target_pairs={{2,0},{3,1},{0,2},{1,3},{18,16},{19,17},{16,18},{17,19},{34,32},{3... | collective-permute-start | bytes 1572872 | tf_op jit(solution)/shard_map/ppermute | solution.py:353
  77.4 26.7 %collective-permute-start.13 = (bf16[256,1024]{1,0:T(8,128)(2,1)}, bf16[256,1024]{1,0:T(8,128)(2,1)S(1)}, u32[]{:S(2)}, u32[]{:S(2)}) collective-permute-start(bf16[256,1024]{1,0:T(8,128)(2,1)} %get-tuple-element.21), channel_id=1, source_target_pairs={{496,0},{1,1},{2,2},{19,3},{0,16},{17,17},{18,18},{35,19},{16,32},... | collective-permute-start | bytes 1572872 | tf_op jit(solution)/shard_map/ppermute | solution.py:353
  88.5 27.6 %all-to-all-start = ((bf16[64,8,384]{2,1,0:T(8,128)(2,1)}), bf16[64,8,384]{2,1,0:T(8,128)(2,1)S(1)}, u32[]{:S(2)}, u32[]{:S(2)}) async-start(bf16[64,8,384]{2,1,0:T(8,128)(2,1)} %pad_maximum_fusion.1), calls=%async_computation | async-start | bytes 786432 | tf_op jit(solution)/shard_map/all_to_all | solution.py:385
  96.0 18.2 %copy-start.3 = (f32[1024]{0:T(1024)S(1)}, f32[1024]{0:T(1024)}, u32[]{:S(2)}) copy-start(f32[1024]{0:T(1024)} %param.9) | copy-start | bytes 12292
  104.5 10.7 %copy-start.1 = (bf16[4,32,1024]{2,1,0:T(8,128)(2,1)S(1)}, bf16[4,32,1024]{2,1,0:T(8,128)(2,1)}, u32[]{:S(2)}) copy-start(bf16[4,32,1024]{2,1,0:T(8,128)(2,1)} %grads_ref.1) | copy-start | bytes 786436
  104.5 9.6 %collective-permute-start.14 = (bf16[2,4,4,1024]{3,2,1,0:T(4,128)(2,1)S(1)}, bf16[2,4,4,1024]{3,2,1,0:T(4,128)(2,1)S(1)}, u32[]{:S(2)}, u32[]{:S(2)}) collective-permute-start(bf16[2,4,4,1024]{3,2,1,0:T(4,128)(2,1)S(1)} %slice.101), channel_id=1, source_target_pairs={{0,4},{4,8},{8,12},{12,0},{1,5},{5,9},{9,13},{13,1},{2,6},{6,10},{... | collective-permute-start | bytes 196616 | tf_op jit(solution)/shard_map/ppermute | solution.py:392

commit v3 on v2

v3 whole, which is shorter than its diff:
```python
import math

import jax
import jax.numpy as jnp
from jax import lax
from jax.experimental import pallas as pl
from jax.experimental.pallas import tpu as pltpu
from jax.sharding import PartitionSpec as P

HD = 64
WIN = 8
SHIFT = 4
EPS = 1e-05
F32 = jnp.float32
BF16 = jnp.bfloat16
SPAN = 2 * WIN - 1
POS = WIN * WIN
VMEM_LIMIT = 56 * 1024 * 1024


def dot(a, b, ca, cb):
    return lax.dot_general(a, b, (((ca,), (cb,)), ((), ())), preferred_element_type=F32)


def rows_to_table(vectors):
    heads = vectors.shape[0] // 2
    even = vectors[:heads].reshape(heads, 8, 16)
    odd = jnp.concatenate([vectors[heads:, 8:], vectors[heads:, :8]], 1).reshape(heads, 8, 16)
    both = jnp.stack([even, odd], 2).reshape(heads, 16, 16)[:, :SPAN, :SPAN]
    return both.reshape(heads, SPAN * SPAN).T


def table_to_rows(table):
    heads, count = table.shape
    table = jnp.concatenate([table, jnp.zeros((heads, 256 - count), F32)], 1)
    table = jnp.concatenate([table, table], 0)
    lane = lax.broadcasted_iota(jnp.int32, (2 * heads, 128), 1)
    odd = lax.broadcasted_iota(jnp.int32, (2 * heads, 128), 0) >= heads
    rows = jnp.zeros((2 * heads, 128), F32)
    for a in range(SPAN):
        moved = pltpu.roll(table, (-a * (SPAN - 8)) % 256, 1)[:, :128]
        here = (lane >= 8 * a) & (lane < 8 * a + SPAN) & (odd == (a % 2 == 1))
        rows = jnp.where(here, moved, rows)
    return rows


def attention_kernel(
    flags_ref, x_own, x_other, wq_in, wp_in, half_in, other_half_in, tab_ref,
    own_out, other_out, keep_ref, send_ref,
    xs_ref, wq_all, wp_all, sum_ref, out_ref, grad_cols, attn_cols, attn_edge, tab_parts, sems,
):
    groups, channels, d = wp_all.shape
    heads = channels // HD
    scale = HD ** (-0.5)
    parts = xs_ref.shape[0]
    ncol = grad_cols.shape[1] - WIN
    own = WIN // parts * ncol
    wins = ncol // WIN
    strip = own // ncol * SHIFT
    rows = own * parts
    lanes = heads * POS
    last_row = flags_ref[0] == 1
    last_col = flags_ref[1] == 1
    core = flags_ref[2]
    own_slot = flags_ref[3]
    band = flags_ref[4]

    half = d // 2
    tall = channels // 2
    moves = [
        (x_own, xs_ref.at[own_slot]),
        (x_other, xs_ref.at[1 - own_slot]),
        (wp_in, wp_all.at[0]),
        (wq_in, wq_all.at[0]),
    ]
    first_moves = len(moves)
    for source, at in ((half_in, core), (other_half_in, 1 - core)):
        rows_at = pl.ds(pl.multiple_of(at * half, half), half)
        for t in range(3):
            piece = source.at[t * half : (t + 1) * half, :]
            moves.append((piece, wq_all.at[1, t, rows_at, :]))
        rows_at = pl.ds(pl.multiple_of(at * tall, tall), tall)
        for j in range(d // channels):
            piece = source.at[3 * half + j * tall : 3 * half + (j + 1) * tall, :]
            cols = slice(j * channels, (j + 1) * channels)
            moves.append((piece, wp_all.at[1, rows_at, cols]))
    moves.append((half_in.at[half_in.shape[0] - 16 :, :], tab_parts))
    moves = [pltpu.make_async_copy(a, b, sems.at[i]) for i, (a, b) in enumerate(moves)]
    for move in moves:
        move.start()

    lane128 = lax.broadcasted_iota(jnp.int32, (8, 128), 1)
    even_lane = ((lane128 // 8) % 2) == 0

    def bias_of(tab):
        shifted = [pltpu.roll(tab, (b - 7) % 128, 1) for b in range(WIN)]
        per_head = []
        for h in range(heads):
            ev = jnp.concatenate([s[h : h + 1] for s in shifted], 0)
            od = jnp.concatenate([s[heads + h : heads + h + 1] for s in shifted], 0)
            per_head.append(jnp.where(even_lane, ev, od))
        bias_rows = []
        for a in range(WIN):
            pieces = []
            for p in range(heads // 2):
                lo = pltpu.roll(per_head[2 * p], (-(7 - a) * 8) % 128, 1)
                hi = pltpu.roll(per_head[2 * p + 1], (64 - (7 - a) * 8) % 128, 1)
                pieces.append(jnp.where(lane128 < 64, lo, hi))
            bias_rows.append(jnp.concatenate(pieces, 1))
        return jnp.concatenate(bias_rows, 0)

    key_pos = lax.broadcasted_iota(jnp.int32, (POS, lanes), 0)
    query_pos = lax.broadcasted_iota(jnp.int32, (POS, lanes), 1) % POS
    same_pos = key_pos == query_pos
    same_row_half = (key_pos // (WIN * SHIFT)) == (query_pos // (WIN * SHIFT))
    same_col_half = ((key_pos // SHIFT) % 2) == ((query_pos // SHIFT) % 2)
    lane_head = lax.broadcasted_iota(jnp.int32, (POS, channels), 1) // HD
    head_f = [(lane_head == h).astype(F32) for h in range(heads)]
    head_b = [m.astype(BF16) for m in head_f]

    results = [
        pltpu.make_async_copy(out_ref.at[own_slot], own_out, sems.at[len(moves)]),
        pltpu.make_async_copy(out_ref.at[1 - own_slot], other_out, sems.at[len(moves) + 1]),
    ]

    def group(g):
        if g == 0:
            bias = bias_of(table_to_rows(tab_ref[...]))
        for move in moves[:first_moves] if g == 0 else moves[first_moves:]:
            move.wait()
        if g == 1:
            terms = tab_parts[...].astype(F32)
            bias = bias_of(terms[:8, :128] + terms[:8, 128:256] + terms[8:, :128])
        wp = wp_all[g]

        edge = jnp.concatenate([xs_ref[x, 2 * own : 2 * own + strip] for x in range(parts)], 0)
        edge_grad = dot(edge, wp, 1, 1)
        attn_edge[...] = edge_grad

        ds_total = jnp.zeros((POS, lanes), F32)
        xn = xs_ref[:, :own].reshape(rows, d)
        ct = xs_ref[:, own : 2 * own].reshape(rows, d)
        queries, keys, values = [
            dot(xn, wq_all[g, t], 1, 0).reshape(WIN, wins, WIN, channels) for t in range(3)
        ]
        marks = xs_ref[0, 2 * own + strip :]
        key_row = lax.broadcasted_iota(jnp.int32, (POS, marks.shape[0]), 0) // WIN + band * WIN
        tile_row = lax.broadcasted_iota(jnp.int32, (POS, marks.shape[0]), 1)
        marks = dot((key_row == tile_row).astype(BF16), marks[:, :128], 1, 0)
        key_col = lax.broadcasted_iota(jnp.int32, marks.shape, 0) % WIN
        tile_col = lax.broadcasted_iota(jnp.int32, marks.shape, 1)
        grad_cols[:, :ncol] = dot(ct, wp, 1, 1).reshape(WIN, ncol, channels)
        for i in range(WIN):
            grad_cols[i, ncol : ncol + SHIFT] = attn_edge[i * SHIFT : (i + 1) * SHIFT]
        dog = grad_cols[:, SHIFT : SHIFT + ncol].reshape(WIN, wins, WIN, channels)
        outs, dqs, dks, dvs = [], [], [], []
        for u in range(wins):
            q = queries[:, u].reshape(POS, channels).astype(BF16)
            k = keys[:, u].reshape(POS, channels).astype(BF16)
            v = values[:, u].reshape(POS, channels).astype(BF16)
            do = dog[:, u].reshape(POS, channels).astype(BF16)
            qbd = jnp.concatenate([q * m for m in head_b], 0)
            dbd = jnp.concatenate([do * m for m in head_b], 0)
            s = dot(k, qbd, 1, 1) * scale + bias
            valid = jnp.where(tile_col == key_col + u * WIN, marks, 0.0)
            valid = jnp.sum(valid, 1, keepdims=True)
            allowed = same_pos | (jnp.broadcast_to(valid, (POS, lanes)) == 1.0)
            allowed = allowed & (same_row_half | jnp.logical_not(last_row))
            if u == wins - 1:
                allowed = allowed & (same_col_half | jnp.logical_not(last_col))
            s = jnp.where(allowed, s, -1e30)
            e = jnp.exp(s - jnp.max(s, 0, keepdims=True))
            p = e / jnp.sum(e, 0, keepdims=True)
            pb = p.astype(BF16)
            dp = dot(v, dbd, 1, 1)
            ds = p * (dp - jnp.sum(p * dp, 0, keepdims=True))
            dsb = ds.astype(BF16)
            ds_total = ds_total + ds
            dvs.append(dot(pb, dbd, 1, 0))
            dks.append(dot(dsb, qbd, 1, 0) * scale)
            o_all = dot(pb, v, 0, 0)
            dq_all = dot(dsb, k, 0, 0)
            o = o_all[:POS] * head_f[0]
            dq = dq_all[:POS] * head_f[0]
            for h in range(1, heads):
                o = o + o_all[h * POS : (h + 1) * POS] * head_f[h]
                dq = dq + dq_all[h * POS : (h + 1) * POS] * head_f[h]
            outs.append(o)
            dqs.append(dq * scale)

        def patches(pieces):
            pieces = [z.reshape(WIN, 1, WIN, channels) for z in pieces]
            return jnp.concatenate(pieces, 1).reshape(rows, channels)

        attn = patches(outs)
        back = dot(patches(dqs).astype(BF16), wq_all[g, 0], 1, 1)
        back = back + dot(patches(dks).astype(BF16), wq_all[g, 1], 1, 1)
        back = back + dot(patches(dvs).astype(BF16), wq_all[g, 2], 1, 1)
        branch = dot(attn.astype(BF16), wp, 1, 0)
        for j, term in enumerate((back, branch)):
            term = term.reshape(parts, own, d)
            at = slice(j * own, (j + 1) * own)
            if g < groups - 1:
                sum_ref[:, at] = term
            else:
                out_ref[:, at] = (sum_ref[:, at] + term).astype(BF16)
        if g == groups - 1:
            for result in results:
                result.start()
        attn_cols[:, :SHIFT] = jnp.zeros((WIN, SHIFT, channels), F32)
        attn_cols[:, SHIFT : SHIFT + ncol] = attn.reshape(WIN, ncol, channels)
        for i in range(WIN):
            attn_edge[i * SHIFT : (i + 1) * SHIFT] = attn_cols[i, ncol : ncol + SHIFT]
        wt = dot(ct, attn_cols[:, :ncol].reshape(rows, channels).astype(BF16), 0, 0)
        wt = wt + dot(edge, attn_edge[...].astype(BF16), 0, 0)
        halves = wt.reshape(d // 16, 2, 8, channels)
        first = core == 0
        keep_ref[g, : d // 16] = jnp.where(first, halves[:, 0], halves[:, 1])
        send_ref[g, : d // 16] = jnp.where(first, halves[:, 1], halves[:, 0])

        diag = [jnp.zeros((8, 128), F32) for _ in range(heads)]
        for a in range(WIN):
            for p in range(heads // 2):
                block = ds_total[8 * a : 8 * a + 8, 128 * p : 128 * p + 128]
                lo = jnp.where(lane128 < 64, block, 0.0)
                hi = jnp.where(lane128 < 64, 0.0, block)
                diag[2 * p] = diag[2 * p] + pltpu.roll(lo, (7 - a) * 8, 1)
                diag[2 * p + 1] = diag[2 * p + 1] + pltpu.roll(hi, ((7 - a) * 8 - 64) % 128, 1)
        evens = [jnp.where(even_lane, t, 0.0) for t in diag]
        odds = [jnp.where(even_lane, 0.0, t) for t in diag]
        total = jnp.zeros((8, 128), F32)
        for b in range(WIN):
            line = jnp.concatenate([t[b : b + 1] for t in evens + odds], 0)
            total = total + pltpu.roll(line, 7 - b, 1)
        both = jnp.concatenate([total, jnp.zeros((8, channels - 128), F32)], 1)
        keep_ref[g, d // 16] = both
        send_ref[g, d // 16] = both

    for g in range(groups):
        group(g)
    for result in results:
        result.wait()


def attention(ncol, flags, packets, weights, halves, table):
    channels, d = weights[1].shape
    own = WIN // 2 * ncol
    piece = jax.ShapeDtypeStruct((2, d // 16 + 1, 8, channels), F32)
    term = jax.ShapeDtypeStruct((2 * own, d), BF16)
    vmem = pl.BlockSpec(memory_space=pltpu.VMEM)
    hbm = pl.BlockSpec(memory_space=pltpu.HBM)
    return pl.pallas_call(
        attention_kernel,
        out_shape=(term, term, piece, piece),
        in_specs=[pl.BlockSpec(memory_space=pltpu.SMEM)] + [hbm] * 6 + [vmem],
        out_specs=(hbm, hbm, vmem, vmem),
        scratch_shapes=[
            pltpu.VMEM((2,) + packets[0].shape, BF16),
            pltpu.VMEM((2, 3, d, channels), BF16),
            pltpu.VMEM((2, channels, d), BF16),
            pltpu.VMEM((2, 2 * own, d), F32),
            pltpu.VMEM((2, 2 * own, d), BF16),
            pltpu.VMEM((WIN, ncol + WIN, channels), F32),
            pltpu.VMEM((WIN, ncol + WIN, channels), F32),
            pltpu.VMEM((WIN * SHIFT, channels), F32),
            pltpu.VMEM((16, channels), BF16),
            pltpu.SemaphoreType.DMA((2 * (3 + d // channels) + 9,)),
        ],
        compiler_params=pltpu.CompilerParams(vmem_limit_bytes=VMEM_LIMIT),
        cost_estimate=pl.CostEstimate(
            flops=3_000_000_000, bytes_accessed=11_000_000, transcendentals=131072
        ),
        name="window_attention",
    )(flags, *packets, *weights, *halves, table)


def pack_kernel(core_ref, wq_ref, wp_ref, tab_ref, out_ref):
    tall, d = wp_ref.shape
    _, half, channels = wq_ref.shape
    for t in range(3):
        out_ref[t * half : (t + 1) * half] = wq_ref[t]
    for j in range(d // channels):
        at = 3 * half + j * tall
        out_ref[at : at + tall] = wp_ref[:, j * channels : (j + 1) * channels]
    table = table_to_rows(tab_ref[...])
    top = table.astype(BF16)
    table = table - top.astype(F32)
    middle = table.astype(BF16)
    table = table - middle.astype(F32)
    low = jnp.concatenate([table, jnp.zeros_like(table)], 1)
    high = jnp.concatenate([top.astype(F32), middle.astype(F32)], 1)
    at = out_ref.shape[0] - 2 * table.shape[0]
    out_ref[at:, : high.shape[1]] = jnp.concatenate([high, low], 0).astype(BF16)


def packed_half(core, w_qkv, w_proj, table):
    _, d, channels = w_qkv.shape
    rows = 3 * d // 2 + d // channels * (channels // 2) + 4 * table.shape[0]
    return pl.pallas_call(
        pack_kernel,
        out_shape=jax.ShapeDtypeStruct((rows, channels), BF16),
        grid_spec=pltpu.PrefetchScalarGridSpec(
            num_scalar_prefetch=1,
            grid=(1,),
            in_specs=[
                pl.BlockSpec((3, d // 2, channels), lambda i, core: (0, core[0], 0)),
                pl.BlockSpec((channels // 2, d), lambda i, core: (core[0], 0)),
                pl.BlockSpec(table.shape, lambda i, core: (0, 0)),
            ],
            out_specs=pl.BlockSpec((rows, channels), lambda i, core: (0, 0)),
        ),
        compiler_params=pltpu.CompilerParams(vmem_limit_bytes=VMEM_LIMIT),
        cost_estimate=pl.CostEstimate(flops=0, bytes_accessed=2_100_000, transcendentals=0),
        name="packed_half",
    )(core, w_qkv, w_proj, table)


def strips_kernel(tokens_ref, grads_ref, out_ref):
    out_ref[...] = jnp.concatenate([tokens_ref[:, :SHIFT], grads_ref[:, :SHIFT]], 1)


def left_strips(tokens, grads):
    prow, ncol, d = tokens.shape
    spec = pl.BlockSpec((prow, 16, d), lambda i: (0, 0, 0))
    return pl.pallas_call(
        strips_kernel,
        grid=(1,),
        out_shape=jax.ShapeDtypeStruct((prow, 2 * SHIFT, d), BF16),
        in_specs=[spec, spec],
        out_specs=pl.BlockSpec((prow, 2 * SHIFT, d), lambda i: (0, 0, 0)),
        compiler_params=pltpu.CompilerParams(vmem_limit_bytes=VMEM_LIMIT),
        cost_estimate=pl.CostEstimate(flops=0, bytes_accessed=300_000, transcendentals=0),
        name="left_strips",
    )(tokens, grads)


def norm_kernel(tokens_ref, grads_ref, strips_ref, gain_ref, valid_ref, out_ref, cols, strip_rows):
    prow, ncol, d = tokens_ref.shape
    own = prow * ncol
    strip = prow * SHIFT
    cols[:, :ncol] = tokens_ref[...].astype(F32)
    for i in range(prow):
        both = strips_ref[i].astype(F32)
        cols[i, ncol : ncol + SHIFT] = both[:SHIFT]
        strip_rows[i * SHIFT : (i + 1) * SHIFT] = both[SHIFT:]
    x = cols[:, SHIFT : SHIFT + ncol].reshape(own, d)
    x = x - jnp.mean(x, -1, keepdims=True)
    rstd = lax.rsqrt(jnp.mean(x * x, -1, keepdims=True) + EPS)
    out_ref[:own] = (x * rstd * gain_ref[...]).astype(BF16)
    out_ref[own : 2 * own] = grads_ref[...].reshape(own, d)
    out_ref[2 * own : 2 * own + strip] = strip_rows[...].astype(BF16)
    out_ref[2 * own + strip :] = jnp.zeros((valid_ref.shape[0], d), BF16)
    out_ref[2 * own + strip :, :ncol] = valid_ref[...].astype(F32).astype(BF16)


def norm(tokens, grads, strips, gain, valid):
    prow, ncol, d = tokens.shape
    strip = prow * SHIFT
    vmem = pl.BlockSpec(memory_space=pltpu.VMEM)
    return pl.pallas_call(
        norm_kernel,
        out_shape=jax.ShapeDtypeStruct((2 * prow * ncol + strip + valid.shape[0], d), BF16),
        in_specs=[vmem] * 5,
        out_specs=vmem,
        scratch_shapes=[pltpu.VMEM((prow, ncol + WIN, d), F32), pltpu.VMEM((strip, d), F32)],
        compiler_params=pltpu.CompilerParams(vmem_limit_bytes=VMEM_LIMIT),
        cost_estimate=pl.CostEstimate(
            flops=1_500_000, bytes_accessed=600_000, transcendentals=128
        ),
        name="layer_norm",
    )(tokens, grads, strips, gain, valid)


def on_device(tokens, valid, gain, w_qkv, w_proj, rel_table, cotangent):
    part_rows, ncol, d = tokens.shape
    n_head = lax.axis_size("head")
    n_row = lax.axis_size("row")
    n_col = lax.axis_size("col")
    tile_rows = part_rows * n_head
    own = part_rows * ncol
    strip = part_rows * SHIFT
    channels = w_proj.shape[0]
    row = lax.axis_index("row")
    col = lax.axis_index("col")
    head = lax.axis_index("head")

    left = [(c, (c - 1) % n_col) for c in range(n_col)]
    right = [(c, (c + 1) % n_col) for c in range(n_col)]
    swap = [(c, c ^ 1) for c in range(n_col)]
    mates = []
    for r in range(n_row):
        low, high = r * n_head, (r + 1) % n_row * n_head
        mates += [(low + 1, low + 2), (low + 2, low + 1), (low + 3, high), (high, low + 3)]
    beside = [(h, h ^ 1) for h in range(n_head)]

    def trade(value):
        return lax.ppermute(value, ("row", "head"), mates)

    last = ((head == 3) & (row == n_row - 1)) | ((head == 0) & (row == 0))
    inner = (head == 1) | (head == 2)
    flags = [last, col == n_col - 1, col % 2 == 1, head % 2 == 0, jnp.logical_not(inner)]
    flags = jnp.stack([flag.astype(jnp.int32) for flag in flags])
    table = rel_table.T
    w_qkv = w_qkv.transpose(1, 0, 2)

    strips = left_strips(tokens, cotangent)
    w_in, _ = lax.optimization_barrier((w_qkv, strips))
    half = lax.ppermute(packed_half((col % 2)[None], w_in, w_proj, table), "head", beside)
    strips = lax.ppermute(strips, "col", left)
    packet = norm(tokens, cotangent, strips, gain[None], valid)
    packets = (packet, trade(packet))
    half, _ = lax.optimization_barrier((half, packets[1]))
    other_half = lax.ppermute(half, "col", swap)

    own_term, mate_term, keep, send = attention(
        ncol, flags, packets, (w_qkv, w_proj), (half, other_half), table
    )
    pairs = keep + lax.ppermute(send, "col", swap)
    mate_term = trade(mate_term)
    pair_beside = lax.ppermute(pairs[1].astype(BF16), "head", beside)
    pair = pairs[0] + pair_beside.astype(F32)

    table_part = jnp.broadcast_to(pair[-1:, :, :128], (d // 16, 8, 128))
    pieces = jnp.concatenate([pair[:-1], table_part], 2).astype(BF16)
    cores = [
        [r * n_col + c for r in range(n_row) for c in range(n_col) if c % 2 == parity]
        for parity in range(2)
    ]
    mate_term, _ = lax.optimization_barrier((mate_term, pieces))
    pieces = lax.all_to_all(pieces, ("row", "col"), 0, 0, axis_index_groups=cores, tiled=True)
    pieces = jnp.sum(pieces.astype(F32), 0)
    scale = 1.0 / math.sqrt(tile_rows * ncol * n_row * n_col)
    proj_grad = pieces[:, :channels].T * scale
    table_grad = rows_to_table(pieces[:, channels:]) * (WIN * scale)

    total = own_term.astype(F32) + mate_term.astype(F32)
    total = total.reshape(2, part_rows, ncol, d)
    edges = lax.ppermute(total[:, :, -SHIFT:].astype(BF16), "col", right).astype(F32)
    total = jnp.concatenate([edges, total[:, :, :-SHIFT]], 2)
    norm_grad = total[0]

    flat = tokens.astype(F32)
    mean = jnp.mean(flat, -1, keepdims=True)
    centered = flat - mean
    rstd = lax.rsqrt(jnp.mean(centered * centered, -1, keepdims=True) + EPS)
    xhat = centered * rstd
    scaled = norm_grad * gain
    token_gradient = cotangent.astype(F32) + rstd * (
        scaled
        - jnp.mean(scaled, -1, keepdims=True)
        - xhat * jnp.mean(scaled * xhat, -1, keepdims=True)
    )

    mixed = (flat + total[1]).astype(BF16)
    return (mixed, token_gradient.astype(BF16), proj_grad, table_grad)


def solution(mesh):
    return jax.shard_map(
        on_device,
        mesh=mesh,
        in_specs=(
            P(("row", "head"), "col", None),
            P("row", "col"),
            P(),
            P(None, None, "head"),
            P("head", None),
            P(None, "head"),
            P(("row", "head"), "col", None),
        ),
        out_specs=(
            P(("row", "head"), "col", None),
            P(("row", "head"), "col", None),
            P("head", ("row", "col")),
            P(None, "head"),
        ),
        check_vma=False,
    )
```

time: 119 us -> 112 us (0.941)
  starting transfers between devices: 64.6 us -> 39.4 us
  waiting for transfers between devices: 27.9 us -> 44.5 us
  Pallas kernels: 14.2 us -> 17.8 us
    ppermute x13 -> x6, starting transfers between devices: 52.6 us -> 14.9 us  [the longest x2 6.29 us: trade(): return lax.ppermute(value, ('row', 'head'), mates)]
    all_to_all x1, starting transfers between devices: 7.44 us -> 15.7 us  [on_device(): lax.all_to_all(pieces, ('row', 'col'), 0, 0, axis_index_groups=cores, til...]
    ppermute x13 -> x6, waiting for transfers between devices: 20.4 us -> 26.7 us  [the longest x2 17.2 us: trade(): return lax.ppermute(value, ('row', 'head'), mates)]
    ppermute x1, waiting for transfers between devices: 7.55 us -> 12.6 us  [on_device(): lax.ppermute(total[:, :, -SHIFT:].astype(BF16), 'col', right).astype(F32)]
    ppermute x1, starting transfers between devices: 2.53 us -> 6.89 us  [on_device(): strips = lax.ppermute(strips, 'col', left)]
    pallas_call x2 -> x3, Pallas kernels: 12.6 us -> 16.1 us  [the longest x1 11.7 us: attention(): pl.pallas_call(attention_kernel, out_shape=(term, term, piece, piece), in...]
    all_to_all x1, waiting for transfers between devices: 0.01 us -> 3.05 us  [on_device(): lax.all_to_all(pieces, ('row', 'col'), 0, 0, axis_index_groups=cores, til...]
    ppermute x1, waiting for transfers between devices: 0.01 us -> 2.15 us  [on_device(): strips = lax.ppermute(strips, 'col', left)]
  transfers between devices with their start and end apart: 16 -> 9, of which waited for: 5 -> 7; matrix products, arithmetic and copies ran while one was open for 6% -> 4% of each run, Pallas kernels for 2% -> 2%
where the time goes in v3:
time: 112 us; the launch traced here: 111 us
  waiting for transfers between devices  44.5 us (40%)
  starting transfers between devices  39.4 us (35%)
  Pallas kernels  17.8 us (16%)
  other arithmetic  6.03 us (5%)
  local copies, waits for them, and re-layouts  2.82 us (3%)
    ppermute x2, waiting for transfers between devices, trade(): return lax.ppermute(value, ('row', 'head'), mates)  17.2 us
    all_to_all x1, starting transfers between devices, on_device(): lax.all_to_all(pieces, ('row', 'col'), 0, 0, axis_index_groups=cores, til...  15.7 us
    ppermute x1, waiting for transfers between devices, on_device(): lax.ppermute(total[:, :, -SHIFT:].astype(BF16), 'col', right).astype(F32)  12.6 us
    pallas_call x1, Pallas kernels, attention(): pl.pallas_call(attention_kernel, out_shape=(term, term, piece, piece), in...  11.7 us
    ppermute x1, starting transfers between devices, on_device(): strips = lax.ppermute(strips, 'col', left)  6.89 us
    ppermute x2, starting transfers between devices, trade(): return lax.ppermute(value, ('row', 'head'), mates)  6.29 us
    ppermute x1, waiting for transfers between devices, on_device(): pair_beside = lax.ppermute(pairs[1].astype(BF16), 'head', beside)  4.98 us
    all_to_all x1, waiting for transfers between devices, on_device(): lax.all_to_all(pieces, ('row', 'col'), 0, 0, axis_index_groups=cores, til...  3.05 us
  transfers between devices with their start and end apart: 9, of which 7 were waited for; matrix products, arithmetic and copies ran while one was open for 4% of the time, Pallas kernels for 2%

profile of v3, /device:TPU:6, one launch (start us, length us, event | category | flops | bytes accessed | tf_op | source)
XLA Modules:
  0.0 111.5 jit_solution(812068470056721419)
XLA Ops:
  0.6 1.6 %left_strips.1 = bf16[4,8,1024]{2,1,0:T(8,128)(2,1)} custom-call(bf16[4,32,1024]{2,1,0:T(8,128)(2,1)} %tokens_ref.3, bf16[4,32,1024]{2,1,0:T(8,128)(2,1)} %grads_ref.3), custom_call_target="tpu_custom_call" | custom-call | bytes 300000 | tf_op jit(solution)/shard_map/left_strips/pallas_call | solution.py:325
  2.3 0.0 copy-start.3
  2.3 2.3 %packed_half.1 = bf16[2064,256]{1,0:T(8,128)(2,1)} custom-call(s32[1]{0:T(128)} %bitcast.7.core_ref, bf16[3,1024,256]{2,1,0:T(8,128)(2,1)} %bitcast.34, bf16[256,1024]{1,0:T(8,128)(2,1)} %wp_in.1, f32[4,225]{1,0:T(4,128)} %bitcast.38), custom_call_target="tpu_custom_call" | custom-call | bytes 2100000 | tf_op jit(solution)/shard_map/packed_half/pallas_call | solution.py:299
  4.6 2.7 %collective-permute-start.2 = (bf16[2064,256]{1,0:T(8,128)(2,1)}, bf16[2064,256]{1,0:T(8,128)(2,1)S(1)}, u32[]{:S(2)}, u32[]{:S(2)}) collective-permute-start(bf16[2064,256]{1,0:T(8,128)(2,1)} %packed_half.1), channel_id=1, source_target_pairs={{0,1},{1,0},{2,3},{3,2},{4,5},{5,4},{6,7},{7,6},{8,9},{9,8},{10,11... | collective-permute-start | bytes 3170312 | tf_op jit(solution)/shard_map/ppermute | solution.py:408
  7.3 0.0 copy-done.3
  7.3 6.9 %collective-permute-start = (bf16[4,8,1024]{2,1,0:T(8,128)(2,1)S(1)}, bf16[4,8,1024]{2,1,0:T(8,128)(2,1)S(1)}, u32[]{:S(2)}, u32[]{:S(2)}) collective-permute-start(bf16[4,8,1024]{2,1,0:T(8,128)(2,1)S(1)} %copy-done.3), channel_id=1, source_target_pairs={{0,12},{4,0},{8,4},{12,8},{1,13},{5,1},{9,5},{13,9},{2,14},{6,2},{... | collective-permute-start | bytes 196616 | tf_op jit(solution)/shard_map/ppermute | solution.py:409
  14.2 2.2 %collective-permute-done.strips_ref = bf16[4,8,1024]{2,1,0:T(8,128)(2,1)S(1)} collective-permute-done((bf16[4,8,1024]{2,1,0:T(8,128)(2,1)S(1)}, bf16[4,8,1024]{2,1,0:T(8,128)(2,1)S(1)}, u32[]{:S(2)}, u32[]{:S(2)}) %collective-permute-start) | collective-permute-done | bytes 65568 | tf_op jit(solution)/shard_map/ppermute | solution.py:409
  16.4 0.0 copy-start.4
  16.4 0.6 copy-done.4
  17.0 2.2 %layer_norm.1.x_own = bf16[288,1024]{1,0:T(8,128)(2,1)} custom-call(bf16[4,32,1024]{2,1,0:T(8,128)(2,1)} %tokens_ref.3, bf16[4,32,1024]{2,1,0:T(8,128)(2,1)} %grads_ref.3, bf16[4,8,1024]{2,1,0:T(8,128)(2,1)} %copy-done.4, f32[1,1024]{1,0:T(1,128)} %bitcast.37, s32[16,32]{1,0:T(8,128)} %valid_ref.1), custom_call_target="tpu_custom_call" | custom-call | flops 1500000 | bytes 600000 | tf_op jit(solution)/shard_map/layer_norm/pallas_call | solution.py:360
  19.1 3.1 %collective-permute-start.1 = (bf16[288,1024]{1,0:T(8,128)(2,1)}, bf16[288,1024]{1,0:T(8,128)(2,1)S(1)}, u32[]{:S(2)}, u32[]{:S(2)}) collective-permute-start(bf16[288,1024]{1,0:T(8,128)(2,1)} %layer_norm.1.x_own), channel_id=1, source_target_pairs={{1,2},{2,1},{3,16},{16,3},{17,18},{18,17},{19,32},{32,19},{33,34},... | collective-permute-start | bytes 1769480 | tf_op jit(solution)/shard_map/ppermute | solution.py:397
  22.3 17.2 %collective-permute-done.1.x_other = bf16[288,1024]{1,0:T(8,128)(2,1)S(1)} collective-permute-done((bf16[288,1024]{1,0:T(8,128)(2,1)}, bf16[288,1024]{1,0:T(8,128)(2,1)S(1)}, u32[]{:S(2)}, u32[]{:S(2)}) %collective-permute-start.1) | collective-permute-done | bytes 589856 | tf_op jit(solution)/shard_map/ppermute | solution.py:397
  39.4 0.0 copy-start.8
  39.4 0.0 collective-permute-done.2.half_in
  39.4 0.0 copy-start.6
  39.4 1.9 %collective-permute-start.3 = (bf16[2064,256]{1,0:T(8,128)(2,1)S(1)}, bf16[2064,256]{1,0:T(8,128)(2,1)S(1)}, u32[]{:S(2)}, u32[]{:S(2)}) collective-permute-start(bf16[2064,256]{1,0:T(8,128)(2,1)S(1)} %collective-permute-done.2.half_in), channel_id=1, source_target_pairs={{0,4},{4,0},{8,12},{12,8},{1,5},{5,1},{9,13},{13,9},{2,6},{6,2},{1... | collective-permute-start | bytes 3170312 | tf_op jit(solution)/shard_map/ppermute | solution.py:413
  41.4 0.1 stack.33
  41.5 0.5 stack.34.flags_ref
  42.0 0.0 copy-start
  42.0 2.0 %collective-permute-done.3.other_half_in = bf16[2064,256]{1,0:T(8,128)(2,1)S(1)} collective-permute-done((bf16[2064,256]{1,0:T(8,128)(2,1)S(1)}, bf16[2064,256]{1,0:T(8,128)(2,1)S(1)}, u32[]{:S(2)}, u32[]{:S(2)}) %collective-permute-start.3) | collective-permute-done | bytes 1056800 | tf_op jit(solution)/shard_map/ppermute | solution.py:413
  44.0 0.0 copy-done.8
  44.0 0.0 copy-done.6
  44.0 0.0 copy-start.7
  44.0 1.0 copy-done.7
  45.0 11.7 %window_attention.1 = (bf16[256,1024]{1,0:T(8,128)(2,1)}, bf16[256,1024]{1,0:T(8,128)(2,1)}, f32[2,65,8,256]{3,2,1,0:T(8,128)}, f32[2,65,8,256]{3,2,1,0:T(8,128)}) custom-call(s32[5]{0:T(128)} %stack.34.flags_ref, bf16[288,1024]{1,0:T(8,128)(2,1)} %layer_norm.1.x_own, bf16[288,1024]{1,0:T(8,128)(2,1)} %copy-done.8, bf16[3,1024,256]{2,1,0:T(8,128)(2,1)} %bitcast.35, ...), custom_call_target="tpu_custom_call" | custom-call | flops 3000000000 | bytes 11000000 | tf_op jit(solution)/shard_map/window_attention/pallas_call | solution.py:252
  56.7 2.0 %collective-permute-start.5 = (f32[2,65,8,256]{3,2,1,0:T(8,128)}, f32[2,65,8,256]{3,2,1,0:T(8,128)S(1)}, u32[]{:S(2)}, u32[]{:S(2)}) collective-permute-start(f32[2,65,8,256]{3,2,1,0:T(8,128)} %get-tuple-element.16), channel_id=1, source_target_pairs={{0,4},{4,0},{8,12},{12,8},{1,5},{5,1},{9,13},{13,9},{2,6},{6,2},{1... | collective-permute-start | bytes 3194888 | tf_op jit(solution)/shard_map/ppermute | solution.py:418
  58.7 0.0 copy-done
  58.8 0.1 convert_reduce_fusion.1
  58.9 2.6 %collective-permute-done.5 = f32[2,65,8,256]{3,2,1,0:T(8,128)S(1)} collective-permute-done((f32[2,65,8,256]{3,2,1,0:T(8,128)}, f32[2,65,8,256]{3,2,1,0:T(8,128)S(1)}, u32[]{:S(2)}, u32[]{:S(2)}) %collective-permute-start.5) | collective-permute-done | bytes 1064992 | tf_op jit(solution)/shard_map/ppermute | solution.py:418
  61.5 0.0 copy-start.9
  61.5 1.4 %add.36 = f32[2,65,8,256]{3,2,1,0:T(8,128)S(1)} add(f32[2,65,8,256]{3,2,1,0:T(8,128)} %get-tuple-element.15, f32[2,65,8,256]{3,2,1,0:T(8,128)S(1)} %collective-permute-done.5) | non-fusion elementwise | flops 266240 | bytes 3194880 | tf_op jit(solution)/shard_map/add | solution.py:418
  63.0 1.9 %collective-permute-start.6 = (bf16[65,8,256]{2,1,0:T(8,128)(2,1)S(1)}, bf16[65,8,256]{2,1,0:T(8,128)(2,1)S(1)}, u32[]{:S(2)}, u32[]{:S(2)}) collective-permute-start(bf16[65,8,256]{2,1,0:T(8,128)(2,1)S(1)} %fusion.16), channel_id=1, source_target_pairs={{0,1},{1,0},{2,3},{3,2},{4,5},{5,4},{6,7},{7,6},{8,9},{9,8},{10,11... | collective-permute-start | bytes 798728 | tf_op jit(solution)/shard_map/ppermute | solution.py:420
  64.9 0.2 fusion.10
  65.1 0.0 copy-done.9
  65.1 3.2 %collective-permute-start.4 = (bf16[256,1024]{1,0:T(8,128)(2,1)S(1)}, bf16[256,1024]{1,0:T(8,128)(2,1)S(1)}, u32[]{:S(2)}, u32[]{:S(2)}) collective-permute-start(bf16[256,1024]{1,0:T(8,128)(2,1)S(1)} %copy-done.9), channel_id=1, source_target_pairs={{1,2},{2,1},{3,16},{16,3},{17,18},{18,17},{19,32},{32,19},{33,34},... | collective-permute-start | bytes 1572872 | tf_op jit(solution)/shard_map/ppermute | solution.py:397
  68.3 5.0 %collective-permute-done.6 = bf16[65,8,256]{2,1,0:T(8,128)(2,1)S(1)} collective-permute-done((bf16[65,8,256]{2,1,0:T(8,128)(2,1)S(1)}, bf16[65,8,256]{2,1,0:T(8,128)(2,1)S(1)}, u32[]{:S(2)}, u32[]{:S(2)}) %collective-permute-start.6) | collective-permute-done | bytes 266272 | tf_op jit(solution)/shard_map/ppermute | solution.py:420
  73.3 0.1 fusion.4
  73.4 0.0 copy-start.2
  73.4 0.8 pad_maximum_fusion.1
  74.2 15.7 %all-to-all-start = ((bf16[64,8,384]{2,1,0:T(8,128)(2,1)}), bf16[64,8,384]{2,1,0:T(8,128)(2,1)S(1)}, u32[]{:S(2)}, u32[]{:S(2)}) async-start(bf16[64,8,384]{2,1,0:T(8,128)(2,1)} %pad_maximum_fusion.1), calls=%async_computation | async-start | bytes 786432 | tf_op jit(solution)/shard_map/all_to_all | solution.py:430
  89.9 0.0 collective-permute-done.4
  90.0 0.0 copy-done.2
  90.0 0.0 copy-start.5
  90.0 0.2 convert_add_fusion
  90.2 1.9 %collective-permute-start.7 = (bf16[2,4,4,1024]{3,2,1,0:T(4,128)(2,1)S(1)}, bf16[2,4,4,1024]{3,2,1,0:T(4,128)(2,1)S(1)}, u32[]{:S(2)}, u32[]{:S(2)}) collective-permute-start(bf16[2,4,4,1024]{3,2,1,0:T(4,128)(2,1)S(1)} %slice.98), channel_id=1, source_target_pairs={{0,4},{4,8},{8,12},{12,0},{1,5},{5,9},{9,13},{13,1},{2,6},{6,10},{... | collective-permute-start | bytes 196616 | tf_op jit(solution)/shard_map/ppermute | solution.py:438
  92.1 12.6 %collective-permute-done.7 = bf16[2,4,4,1024]{3,2,1,0:T(4,128)(2,1)S(1)} collective-permute-done((bf16[2,4,4,1024]{3,2,1,0:T(4,128)(2,1)S(1)}, bf16[2,4,4,1024]{3,2,1,0:T(4,128)(2,1)S(1)}, u32[]{:S(2)}, u32[]{:S(2)}) %collective-permute-start.7) | collective-permute-done | bytes 65568 | tf_op jit(solution)/shard_map/ppermute | solution.py:438
  104.7 0.0 copy-done.5
  104.7 0.0 copy-start.1
  104.7 1.0 fusion.19
  105.7 0.0 copy-done.1
  105.7 1.0 fusion.9
  106.7 3.0 %all-to-all-done = bf16[64,8,384]{2,1,0:T(8,128)(2,1)S(1)} async-done(((bf16[64,8,384]{2,1,0:T(8,128)(2,1)}), bf16[64,8,384]{2,1,0:T(8,128)(2,1)S(1)}, u32[]{:S(2)}, u32[]{:S(2)}) %all-to-all-start) | async-done | bytes 393248 | tf_op jit(solution)/shard_map/all_to_all | solution.py:430
  109.7 0.1 convert_reduce_fusion
  109.8 0.1 slice.69
  109.9 0.6 fusion.17
  110.5 0.1 pad_maximum_fusion.3
  110.6 0.1 stack_reshape.7
  110.6 0.1 stack_reshape.6
  110.8 0.7 mul.71
  (14 shorter events, 0.2 us)
Async XLA Ops:
  2.3 5.0 %copy-start.3 = (bf16[4,8,1024]{2,1,0:T(8,128)(2,1)S(1)}, bf16[4,8,1024]{2,1,0:T(8,128)(2,1)}, u32[]{:S(2)}) copy-start(bf16[4,8,1024]{2,1,0:T(8,128)(2,1)} %left_strips.1) | copy-start | bytes 196612
  4.6 34.9 %collective-permute-start.2 = (bf16[2064,256]{1,0:T(8,128)(2,1)}, bf16[2064,256]{1,0:T(8,128)(2,1)S(1)}, u32[]{:S(2)}, u32[]{:S(2)}) collective-permute-start(bf16[2064,256]{1,0:T(8,128)(2,1)} %packed_half.1), channel_id=1, source_target_pairs={{0,1},{1,0},{2,3},{3,2},{4,5},{5,4},{6,7},{7,6},{8,9},{9,8},{10,11... | collective-permute-start | bytes 3170312 | tf_op jit(solution)/shard_map/ppermute | solution.py:408
  7.3 9.1 %collective-permute-start = (bf16[4,8,1024]{2,1,0:T(8,128)(2,1)S(1)}, bf16[4,8,1024]{2,1,0:T(8,128)(2,1)S(1)}, u32[]{:S(2)}, u32[]{:S(2)}) collective-permute-start(bf16[4,8,1024]{2,1,0:T(8,128)(2,1)S(1)} %copy-done.3), channel_id=1, source_target_pairs={{0,12},{4,0},{8,4},{12,8},{1,13},{5,1},{9,5},{13,9},{2,14},{6,2},{... | collective-permute-start | bytes 196616 | tf_op jit(solution)/shard_map/ppermute | solution.py:409
  16.4 0.6 copy-start.4
  19.1 20.3 %collective-permute-start.1 = (bf16[288,1024]{1,0:T(8,128)(2,1)}, bf16[288,1024]{1,0:T(8,128)(2,1)S(1)}, u32[]{:S(2)}, u32[]{:S(2)}) collective-permute-start(bf16[288,1024]{1,0:T(8,128)(2,1)} %layer_norm.1.x_own), channel_id=1, source_target_pairs={{1,2},{2,1},{3,16},{16,3},{17,18},{18,17},{19,32},{32,19},{33,34},... | collective-permute-start | bytes 1769480 | tf_op jit(solution)/shard_map/ppermute | solution.py:397
  39.4 4.6 %copy-start.8 = (bf16[288,1024]{1,0:T(8,128)(2,1)}, bf16[288,1024]{1,0:T(8,128)(2,1)S(1)}, u32[]{:S(2)}) copy-start(bf16[288,1024]{1,0:T(8,128)(2,1)S(1)} %collective-permute-done.1.x_other) | copy-start | bytes 1769476
  39.4 4.6 %copy-start.6 = (bf16[2064,256]{1,0:T(8,128)(2,1)}, bf16[2064,256]{1,0:T(8,128)(2,1)S(1)}, u32[]{:S(2)}) copy-start(bf16[2064,256]{1,0:T(8,128)(2,1)S(1)} %collective-permute-done.2.half_in) | copy-start | bytes 3170308
  39.4 4.6 %collective-permute-start.3 = (bf16[2064,256]{1,0:T(8,128)(2,1)S(1)}, bf16[2064,256]{1,0:T(8,128)(2,1)S(1)}, u32[]{:S(2)}, u32[]{:S(2)}) collective-permute-start(bf16[2064,256]{1,0:T(8,128)(2,1)S(1)} %collective-permute-done.2.half_in), channel_id=1, source_target_pairs={{0,4},{4,0},{8,12},{12,8},{1,5},{5,1},{9,13},{13,9},{2,6},{6,2},{1... | collective-permute-start | bytes 3170312 | tf_op jit(solution)/shard_map/ppermute | solution.py:413
  42.0 16.7 %copy-start = (bf16[4,32,1024]{2,1,0:T(8,128)(2,1)S(1)}, bf16[4,32,1024]{2,1,0:T(8,128)(2,1)}, u32[]{:S(2)}) copy-start(bf16[4,32,1024]{2,1,0:T(8,128)(2,1)} %tokens_ref.3) | copy-start | bytes 786436
  44.0 1.0 copy-start.7
  56.7 4.8 %collective-permute-start.5 = (f32[2,65,8,256]{3,2,1,0:T(8,128)}, f32[2,65,8,256]{3,2,1,0:T(8,128)S(1)}, u32[]{:S(2)}, u32[]{:S(2)}) collective-permute-start(f32[2,65,8,256]{3,2,1,0:T(8,128)} %get-tuple-element.16), channel_id=1, source_target_pairs={{0,4},{4,0},{8,12},{12,8},{1,5},{5,1},{9,13},{13,9},{2,6},{6,2},{1... | collective-permute-start | bytes 3194888 | tf_op jit(solution)/shard_map/ppermute | solution.py:418
  61.5 3.6 %copy-start.9 = (bf16[256,1024]{1,0:T(8,128)(2,1)S(1)}, bf16[256,1024]{1,0:T(8,128)(2,1)}, u32[]{:S(2)}) copy-start(bf16[256,1024]{1,0:T(8,128)(2,1)} %get-tuple-element.14) | copy-start | bytes 1572868
  63.0 10.3 %collective-permute-start.6 = (bf16[65,8,256]{2,1,0:T(8,128)(2,1)S(1)}, bf16[65,8,256]{2,1,0:T(8,128)(2,1)S(1)}, u32[]{:S(2)}, u32[]{:S(2)}) collective-permute-start(bf16[65,8,256]{2,1,0:T(8,128)(2,1)S(1)} %fusion.16), channel_id=1, source_target_pairs={{0,1},{1,0},{2,3},{3,2},{4,5},{5,4},{6,7},{7,6},{8,9},{9,8},{10,11... | collective-permute-start | bytes 798728 | tf_op jit(solution)/shard_map/ppermute | solution.py:420
  65.1 24.8 %collective-permute-start.4 = (bf16[256,1024]{1,0:T(8,128)(2,1)S(1)}, bf16[256,1024]{1,0:T(8,128)(2,1)S(1)}, u32[]{:S(2)}, u32[]{:S(2)}) collective-permute-start(bf16[256,1024]{1,0:T(8,128)(2,1)S(1)} %copy-done.9), channel_id=1, source_target_pairs={{1,2},{2,1},{3,16},{16,3},{17,18},{18,17},{19,32},{32,19},{33,34},... | collective-permute-start | bytes 1572872 | tf_op jit(solution)/shard_map/ppermute | solution.py:397
  73.4 16.6 %copy-start.2 = (bf16[256,1024]{1,0:T(8,128)(2,1)S(1)}, bf16[256,1024]{1,0:T(8,128)(2,1)}, u32[]{:S(2)}) copy-start(bf16[256,1024]{1,0:T(8,128)(2,1)} %get-tuple-element.13) | copy-start | bytes 1572868
  74.2 35.5 %all-to-all-start = ((bf16[64,8,384]{2,1,0:T(8,128)(2,1)}), bf16[64,8,384]{2,1,0:T(8,128)(2,1)S(1)}, u32[]{:S(2)}, u32[]{:S(2)}) async-start(bf16[64,8,384]{2,1,0:T(8,128)(2,1)} %pad_maximum_fusion.1), calls=%async_computation | async-start | bytes 786432 | tf_op jit(solution)/shard_map/all_to_all | solution.py:430
  90.0 14.7 %copy-start.5 = (f32[1024]{0:T(1024)S(1)}, f32[1024]{0:T(1024)}, u32[]{:S(2)}) copy-start(f32[1024]{0:T(1024)} %param.9) | copy-start | bytes 12292
  90.2 14.5 %collective-permute-start.7 = (bf16[2,4,4,1024]{3,2,1,0:T(4,128)(2,1)S(1)}, bf16[2,4,4,1024]{3,2,1,0:T(4,128)(2,1)S(1)}, u32[]{:S(2)}, u32[]{:S(2)}) collective-permute-start(bf16[2,4,4,1024]{3,2,1,0:T(4,128)(2,1)S(1)} %slice.98), channel_id=1, source_target_pairs={{0,4},{4,8},{8,12},{12,0},{1,5},{5,9},{9,13},{13,1},{2,6},{6,10},{... | collective-permute-start | bytes 196616 | tf_op jit(solution)/shard_map/ppermute | solution.py:438
  104.7 1.0 copy-start.1

commit v4 on v3

--- a/solution.py
+++ b/solution.py
@@ -45,18 +45,18 @@
 
 
 def attention_kernel(
-    flags_ref, x_own, x_other, wq_in, wp_in, half_in, other_half_in, tab_ref,
-    own_out, other_out, keep_ref, send_ref,
-    xs_ref, wq_all, wp_all, sum_ref, out_ref, grad_cols, attn_cols, attn_edge, tab_parts, sems,
+    flags_ref, t_own, t_other, c_own, c_other, s_own, s_other, wq_in, wp_in,
+    half_in, other_half_in, tab_ref, gain_ref, valid_ref, valid_other_ref,
+    own_out, other_out, keep_out, send_out,
+    keep_ref, send_ref, ts_ref, cs_ref, strips_ref, xn_ref, cols, strip_rows, wq_all, wp_all, sum_ref, out_ref, grad_cols, attn_cols, attn_edge, tab_parts, sems,
 ):
     groups, channels, d = wp_all.shape
     heads = channels // HD
     scale = HD ** (-0.5)
-    parts = xs_ref.shape[0]
+    parts, own = cs_ref.shape[:2]
     ncol = grad_cols.shape[1] - WIN
-    own = WIN // parts * ncol
+    prow = own // ncol
     wins = ncol // WIN
-    strip = own // ncol * SHIFT
     rows = own * parts
     lanes = heads * POS
     last_row = flags_ref[0] == 1
@@ -68,9 +68,13 @@
     half = d // 2
     tall = channels // 2
     moves = [
-        (x_own, xs_ref.at[own_slot]),
-        (x_other, xs_ref.at[1 - own_slot]),
+        (s_own, strips_ref.at[own_slot]),
+        (s_other, strips_ref.at[1 - own_slot]),
+        (t_own, ts_ref.at[own_slot]),
+        (t_other, ts_ref.at[1 - own_slot]),
         (wp_in, wp_all.at[0]),
+        (c_own, cs_ref.at[own_slot]),
+        (c_other, cs_ref.at[1 - own_slot]),
         (wq_in, wq_all.at[0]),
     ]
     first_moves = len(moves)
@@ -82,8 +86,8 @@
         rows_at = pl.ds(pl.multiple_of(at * tall, tall), tall)
         for j in range(d // channels):
             piece = source.at[3 * half + j * tall : 3 * half + (j + 1) * tall, :]
-            cols = slice(j * channels, (j + 1) * channels)
-            moves.append((piece, wp_all.at[1, rows_at, cols]))
+            span = slice(j * channels, (j + 1) * channels)
+            moves.append((piece, wp_all.at[1, rows_at, span]))
     moves.append((half_in.at[half_in.shape[0] - 16 :, :], tab_parts))
     moves = [pltpu.make_async_copy(a, b, sems.at[i]) for i, (a, b) in enumerate(moves)]
     for move in moves:
@@ -122,31 +126,50 @@
         pltpu.make_async_copy(out_ref.at[own_slot], own_out, sems.at[len(moves)]),
         pltpu.make_async_copy(out_ref.at[1 - own_slot], other_out, sems.at[len(moves) + 1]),
     ]
+    for g in range(groups):
+        for j, (source, target) in enumerate(((keep_ref, keep_out), (send_ref, send_out))):
+            sem = sems.at[len(moves) + 2 + 2 * g + j]
+            results.append(pltpu.make_async_copy(source.at[g], target.at[g], sem))
 
     def group(g):
         if g == 0:
             bias = bias_of(table_to_rows(tab_ref[...]))
-        for move in moves[:first_moves] if g == 0 else moves[first_moves:]:
+        for move in moves[:4] if g == 0 else moves[first_moves:]:
             move.wait()
         if g == 1:
             terms = tab_parts[...].astype(F32)
             bias = bias_of(terms[:8, :128] + terms[:8, 128:256] + terms[8:, :128])
+        if g == 0:
+            for x in range(parts):
+                block = ts_ref[x].astype(F32).reshape(prow, ncol, d)
+                cols[x * prow : (x + 1) * prow, :ncol] = block
+                for i in range(prow):
+                    both = strips_ref[x, i].astype(F32)
+                    at = x * prow + i
+                    cols[at, ncol : ncol + SHIFT] = both[:SHIFT]
+                    strip_rows[at * SHIFT : (at + 1) * SHIFT] = both[SHIFT:]
+            moved = cols[:, SHIFT : SHIFT + ncol].reshape(rows, d)
+            moved = moved - jnp.mean(moved, -1, keepdims=True)
+            rstd = lax.rsqrt(jnp.mean(moved * moved, -1, keepdims=True) + EPS)
+            xn_ref[...] = (moved * rstd * gain_ref[...]).astype(BF16)
+            for move in moves[4:first_moves]:
+                move.wait()
+
+        edge = strip_rows[...].astype(BF16)
         wp = wp_all[g]
-
-        edge = jnp.concatenate([xs_ref[x, 2 * own : 2 * own + strip] for x in range(parts)], 0)
         edge_grad = dot(edge, wp, 1, 1)
         attn_edge[...] = edge_grad
 
         ds_total = jnp.zeros((POS, lanes), F32)
-        xn = xs_ref[:, :own].reshape(rows, d)
-        ct = xs_ref[:, own : 2 * own].reshape(rows, d)
+        xn = xn_ref[...]
+        ct = cs_ref[...].reshape(rows, d)
         queries, keys, values = [
             dot(xn, wq_all[g, t], 1, 0).reshape(WIN, wins, WIN, channels) for t in range(3)
         ]
-        marks = xs_ref[0, 2 * own + strip :]
+        marks = jnp.where(flags_ref[5] == 1, valid_other_ref[...], valid_ref[...])
         key_row = lax.broadcasted_iota(jnp.int32, (POS, marks.shape[0]), 0) // WIN + band * WIN
         tile_row = lax.broadcasted_iota(jnp.int32, (POS, marks.shape[0]), 1)
-        marks = dot((key_row == tile_row).astype(BF16), marks[:, :128], 1, 0)
+        marks = dot((key_row == tile_row).astype(BF16), marks.astype(BF16), 1, 0)
         key_col = lax.broadcasted_iota(jnp.int32, marks.shape, 0) % WIN
         tile_col = lax.broadcasted_iota(jnp.int32, marks.shape, 1)
         grad_cols[:, :ncol] = dot(ct, wp, 1, 1).reshape(WIN, ncol, channels)
@@ -205,7 +228,7 @@
             else:
                 out_ref[:, at] = (sum_ref[:, at] + term).astype(BF16)
         if g == groups - 1:
-            for result in results:
+            for result in results[:2]:
                 result.start()
         attn_cols[:, :SHIFT] = jnp.zeros((WIN, SHIFT, channels), F32)
         attn_cols[:, SHIFT : SHIFT + ncol] = attn.reshape(WIN, ncol, channels)
@@ -215,8 +238,9 @@
         wt = wt + dot(edge, attn_edge[...].astype(BF16), 0, 0)
         halves = wt.reshape(d // 16, 2, 8, channels)
         first = core == 0
-        keep_ref[g, : d // 16] = jnp.where(first, halves[:, 0], halves[:, 1])
-        send_ref[g, : d // 16] = jnp.where(first, halves[:, 1], halves[:, 0])
+        low, high = halves[:, 0].astype(BF16), halves[:, 1].astype(BF16)
+        keep_ref[g, : d // 16] = jnp.where(first, low, high)
+        send_ref[g, : d // 16] = jnp.where(first, high, low)
 
         diag = [jnp.zeros((8, 128), F32) for _ in range(heads)]
         for a in range(WIN):
@@ -233,8 +257,11 @@
             line = jnp.concatenate([t[b : b + 1] for t in evens + odds], 0)
             total = total + pltpu.roll(line, 7 - b, 1)
         both = jnp.concatenate([total, jnp.zeros((8, channels - 128), F32)], 1)
+        both = both.astype(BF16)
         keep_ref[g, d // 16] = both
         send_ref[g, d // 16] = both
+        for result in results[2 + 2 * g : 4 + 2 * g]:
+            result.start()
 
     for g in range(groups):
         group(g)
@@ -242,20 +269,28 @@
         result.wait()
 
 
-def attention(ncol, flags, packets, weights, halves, table):
+def attention(flags, tokens, grads, strips, weights, halves, table, gain, valids):
     channels, d = weights[1].shape
-    own = WIN // 2 * ncol
-    piece = jax.ShapeDtypeStruct((2, d // 16 + 1, 8, channels), F32)
+    own = grads[0].shape[0]
+    ncol = own // strips[0].shape[0]
+    piece = jax.ShapeDtypeStruct((2, d // 16 + 1, 8, channels), BF16)
     term = jax.ShapeDtypeStruct((2 * own, d), BF16)
     vmem = pl.BlockSpec(memory_space=pltpu.VMEM)
     hbm = pl.BlockSpec(memory_space=pltpu.HBM)
     return pl.pallas_call(
         attention_kernel,
         out_shape=(term, term, piece, piece),
-        in_specs=[pl.BlockSpec(memory_space=pltpu.SMEM)] + [hbm] * 6 + [vmem],
-        out_specs=(hbm, hbm, vmem, vmem),
+        in_specs=[pl.BlockSpec(memory_space=pltpu.SMEM)] + [hbm] * 10 + [vmem] * 4,
+        out_specs=(hbm,) * 4,
         scratch_shapes=[
-            pltpu.VMEM((2,) + packets[0].shape, BF16),
+            pltpu.VMEM(piece.shape, BF16),
+            pltpu.VMEM(piece.shape, BF16),
+            pltpu.VMEM((2, own, d), BF16),
+            pltpu.VMEM((2, own, d), BF16),
+            pltpu.VMEM((2,) + strips[0].shape, BF16),
+            pltpu.VMEM((2 * own, d), BF16),
+            pltpu.VMEM((WIN, ncol + WIN, d), F32),
+            pltpu.VMEM((WIN * SHIFT, d), F32),
             pltpu.VMEM((2, 3, d, channels), BF16),
             pltpu.VMEM((2, channels, d), BF16),
             pltpu.VMEM((2, 2 * own, d), F32),
@@ -264,14 +299,14 @@
             pltpu.VMEM((WIN, ncol + WIN, channels), F32),
             pltpu.VMEM((WIN * SHIFT, channels), F32),
             pltpu.VMEM((16, channels), BF16),
-            pltpu.SemaphoreType.DMA((2 * (3 + d // channels) + 9,)),
+            pltpu.SemaphoreType.DMA((2 * (3 + d // channels) + 15,)),
         ],
         compiler_params=pltpu.CompilerParams(vmem_limit_bytes=VMEM_LIMIT),
         cost_estimate=pl.CostEstimate(
             flops=3_000_000_000, bytes_accessed=11_000_000, transcendentals=131072
         ),
         name="window_attention",
-    )(flags, *packets, *weights, *halves, table)
+    )(flags, *tokens, *grads, *strips, *weights, *halves, table, gain, *valids)
 
 
 def pack_kernel(core_ref, wq_ref, wp_ref, tab_ref, out_ref):
@@ -334,43 +369,6 @@
     )(tokens, grads)
 
 
-def norm_kernel(tokens_ref, grads_ref, strips_ref, gain_ref, valid_ref, out_ref, cols, strip_rows):
-    prow, ncol, d = tokens_ref.shape
-    own = prow * ncol
-    strip = prow * SHIFT
-    cols[:, :ncol] = tokens_ref[...].astype(F32)
-    for i in range(prow):
-        both = strips_ref[i].astype(F32)
-        cols[i, ncol : ncol + SHIFT] = both[:SHIFT]
-        strip_rows[i * SHIFT : (i + 1) * SHIFT] = both[SHIFT:]
-    x = cols[:, SHIFT : SHIFT + ncol].reshape(own, d)
-    x = x - jnp.mean(x, -1, keepdims=True)
-    rstd = lax.rsqrt(jnp.mean(x * x, -1, keepdims=True) + EPS)
-    out_ref[:own] = (x * rstd * gain_ref[...]).astype(BF16)
-    out_ref[own : 2 * own] = grads_ref[...].reshape(own, d)
-    out_ref[2 * own : 2 * own + strip] = strip_rows[...].astype(BF16)
-    out_ref[2 * own + strip :] = jnp.zeros((valid_ref.shape[0], d), BF16)
-    out_ref[2 * own + strip :, :ncol] = valid_ref[...].astype(F32).astype(BF16)
-
-
-def norm(tokens, grads, strips, gain, valid):
-    prow, ncol, d = tokens.shape
-    strip = prow * SHIFT
-    vmem = pl.BlockSpec(memory_space=pltpu.VMEM)
-    return pl.pallas_call(
-        norm_kernel,
-        out_shape=jax.ShapeDtypeStruct((2 * prow * ncol + strip + valid.shape[0], d), BF16),
-        in_specs=[vmem] * 5,
-        out_specs=vmem,
-        scratch_shapes=[pltpu.VMEM((prow, ncol + WIN, d), F32), pltpu.VMEM((strip, d), F32)],
-        compiler_params=pltpu.CompilerParams(vmem_limit_bytes=VMEM_LIMIT),
-        cost_estimate=pl.CostEstimate(
-            flops=1_500_000, bytes_accessed=600_000, transcendentals=128
-        ),
-        name="layer_norm",
-    )(tokens, grads, strips, gain, valid)
-
-
 def on_device(tokens, valid, gain, w_qkv, w_proj, rel_table, cotangent):
     part_rows, ncol, d = tokens.shape
     n_head = lax.axis_size("head")
@@ -384,7 +382,6 @@
     col = lax.axis_index("col")
     head = lax.axis_index("head")
 
-    left = [(c, (c - 1) % n_col) for c in range(n_col)]
     right = [(c, (c + 1) % n_col) for c in range(n_col)]
     swap = [(c, c ^ 1) for c in range(n_col)]
     mates = []
@@ -398,24 +395,45 @@
 
     last = ((head == 3) & (row == n_row - 1)) | ((head == 0) & (row == 0))
     inner = (head == 1) | (head == 2)
-    flags = [last, col == n_col - 1, col % 2 == 1, head % 2 == 0, jnp.logical_not(inner)]
+    flags = [last, col == n_col - 1, col % 2 == 1, head % 2 == 0, jnp.logical_not(inner), head == 0]
     flags = jnp.stack([flag.astype(jnp.int32) for flag in flags])
     table = rel_table.T
     w_qkv = w_qkv.transpose(1, 0, 2)
 
+    half = lax.ppermute(packed_half((col % 2)[None], w_qkv, w_proj, table), "head", beside)
     strips = left_strips(tokens, cotangent)
-    w_in, _ = lax.optimization_barrier((w_qkv, strips))
-    half = lax.ppermute(packed_half((col % 2)[None], w_in, w_proj, table), "head", beside)
-    strips = lax.ppermute(strips, "col", left)
-    packet = norm(tokens, cotangent, strips, gain[None], valid)
-    packets = (packet, trade(packet))
-    half, _ = lax.optimization_barrier((half, packets[1]))
+    whole = ("row", "col", "head")
+    holder = {a: b for a, b in mates}
+
+    def place(line_head, c):
+        return (line_head // n_head * n_col + c) * n_head + line_head % n_head
+
+    spots = [(i, c) for i in range(n_row * n_head) for c in range(n_col)]
+    straight = [(place(i, (c + 1) % n_col), place(i, c)) for i, c in spots]
+    across = [(place(holder[i], (c + 1) % n_col), place(i, c)) for i, c in spots]
+    strips = (lax.ppermute(strips, whole, straight), lax.ppermute(strips, whole, across))
+    grads = cotangent.reshape(own, d)
+    grads = (grads, trade(grads))
+    patches = tokens.reshape(own, d)
+    patches = (patches, trade(patches))
+    marks = valid.astype(F32)
+    down = [(r * n_head, (r + 1) % n_row * n_head) for r in range(n_row)]
+    marks = (marks, lax.ppermute(marks, ("row", "head"), down))
+    half, *_ = lax.optimization_barrier((half, patches[1], grads[1], *strips, marks[1]))
     other_half = lax.ppermute(half, "col", swap)
 
     own_term, mate_term, keep, send = attention(
-        ncol, flags, packets, (w_qkv, w_proj), (half, other_half), table
+        flags,
+        patches,
+        grads,
+        strips,
+        (w_qkv, w_proj),
+        (half, other_half),
+        table,
+        gain[None],
+        marks,
     )
-    pairs = keep + lax.ppermute(send, "col", swap)
+    pairs = keep.astype(F32) + lax.ppermute(send, "col", swap).astype(F32)
     mate_term = trade(mate_term)
     pair_beside = lax.ppermute(pairs[1].astype(BF16), "head", beside)
     pair = pairs[0] + pair_beside.astype(F32)

time: 112 us -> 110 us (0.982)
  the two profiles are of different devices: /device:TPU:6 before, /device:TPU:2 now
where the time goes in v4:
time: 110 us; the launch traced here: 109 us
  starting transfers between devices  57.1 us (52%)
  waiting for transfers between devices  28.6 us (26%)
  Pallas kernels  14.7 us (13%)
  other arithmetic  5.81 us (5%)
  local copies, waits for them, and re-layouts  2.17 us (2%)
  between operations  1.1 us (1%)
    ppermute x1, starting transfers between devices, on_device(): pair_beside = lax.ppermute(pairs[1].astype(BF16), 'head', beside)  16.5 us
    ppermute x1, waiting for transfers between devices, on_device(): lax.ppermute(total[:, :, -SHIFT:].astype(BF16), 'col', right).astype(F32)  12.7 us
    pallas_call x1, Pallas kernels, attention(): pl.pallas_call(attention_kernel, out_shape=(term, term, piece, piece), in...  10.7 us
    all_to_all x1, starting transfers between devices, on_device(): lax.all_to_all(pieces, ('row', 'col'), 0, 0, axis_index_groups=cores, til...  10.4 us
    ppermute x1, starting transfers between devices, on_device(): lax.ppermute(packed_half((col % 2)[None], w_qkv, w_proj, table), 'head',...  7.8 us
    ppermute x3, starting transfers between devices, trade(): return lax.ppermute(value, ('row', 'head'), mates)  7.76 us
    ppermute x1, waiting for transfers between devices, on_device(): pair_beside = lax.ppermute(pairs[1].astype(BF16), 'head', beside)  4.52 us
    ppermute x1, starting transfers between devices, on_device(): lax.ppermute(strips, whole, across)  4.05 us
  transfers between devices with their start and end apart: 12, of which 7 were waited for; matrix products, arithmetic and copies ran while one was open for 4% of the time, Pallas kernels for 1%

profile of v4, /device:TPU:2, one launch (start us, length us, event | category | flops | bytes accessed | tf_op | source)
XLA Modules:
  0.0 109.4 jit_solution(1910806723676333002)
XLA Ops:
  0.6 0.0 copy-start
  0.7 0.0 copy-start.2
  0.7 0.0 copy-start.5
  0.7 2.3 %packed_half.1 = bf16[2064,256]{1,0:T(8,128)(2,1)} custom-call(s32[1]{0:T(128)} %bitcast.9.core_ref, bf16[3,1024,256]{2,1,0:T(8,128)(2,1)} %bitcast.39, bf16[256,1024]{1,0:T(8,128)(2,1)} %wp_in.1, f32[4,225]{1,0:T(4,128)} %bitcast.44), custom_call_target="tpu_custom_call" | custom-call | bytes 2100000 | tf_op jit(solution)/shard_map/packed_half/pallas_call | solution.py:334
  3.0 7.8 %collective-permute-start.4 = (bf16[2064,256]{1,0:T(8,128)(2,1)}, bf16[2064,256]{1,0:T(8,128)(2,1)S(1)}, u32[]{:S(2)}, u32[]{:S(2)}) collective-permute-start(bf16[2064,256]{1,0:T(8,128)(2,1)} %packed_half.1), channel_id=1, source_target_pairs={{0,1},{1,0},{2,3},{3,2},{4,5},{5,4},{6,7},{7,6},{8,9},{9,8},{10,11... | collective-permute-start | bytes 3170312 | tf_op jit(solution)/shard_map/ppermute | solution.py:403
  10.8 0.0 copy-done
  10.8 1.9 %collective-permute-start = (bf16[128,1024]{1,0:T(8,128)(2,1)S(1)}, bf16[128,1024]{1,0:T(8,128)(2,1)S(1)}, u32[]{:S(2)}, u32[]{:S(2)}) collective-permute-start(bf16[128,1024]{1,0:T(8,128)(2,1)S(1)} %bitcast.36), channel_id=1, source_target_pairs={{1,2},{2,1},{3,16},{16,3},{17,18},{18,17},{19,32},{32,19},{33,34},... | collective-permute-start | bytes 786440 | tf_op jit(solution)/shard_map/ppermute | solution.py:394
  12.8 0.0 copy-done.2
  12.8 3.9 %collective-permute-start.1 = (bf16[128,1024]{1,0:T(8,128)(2,1)S(1)}, bf16[128,1024]{1,0:T(8,128)(2,1)S(1)}, u32[]{:S(2)}, u32[]{:S(2)}) collective-permute-start(bf16[128,1024]{1,0:T(8,128)(2,1)S(1)} %bitcast.42), channel_id=1, source_target_pairs={{1,2},{2,1},{3,16},{16,3},{17,18},{18,17},{19,32},{32,19},{33,34},... | collective-permute-start | bytes 786440 | tf_op jit(solution)/shard_map/ppermute | solution.py:394
  16.7 0.0 copy-done.5
  16.7 0.0 copy-start.6
  16.7 0.7 collective-permute-start.5
  17.4 1.6 %left_strips.1 = bf16[4,8,1024]{2,1,0:T(8,128)(2,1)} custom-call(bf16[4,32,1024]{2,1,0:T(8,128)(2,1)} %tokens_ref.1, bf16[4,32,1024]{2,1,0:T(8,128)(2,1)} %grads_ref.1), custom_call_target="tpu_custom_call" | custom-call | bytes 300000 | tf_op jit(solution)/shard_map/left_strips/pallas_call | solution.py:360
  19.0 1.9 %collective-permute-start.2 = (bf16[4,8,1024]{2,1,0:T(8,128)(2,1)}, bf16[4,8,1024]{2,1,0:T(8,128)(2,1)S(1)}, u32[]{:S(2)}, u32[]{:S(2)}) collective-permute-start(bf16[4,8,1024]{2,1,0:T(8,128)(2,1)} %left_strips.1), channel_id=1, source_target_pairs={{4,0},{8,4},{12,8},{0,12},{5,1},{9,5},{13,9},{1,13},{6,2},{10,6},{... | collective-permute-start | bytes 196616 | tf_op jit(solution)/shard_map/ppermute | solution.py:414
  21.0 0.0 collective-permute-done.5.valid_other_ref
  21.0 0.0 copy-start.15
  21.0 4.1 %collective-permute-start.3 = (bf16[4,8,1024]{2,1,0:T(8,128)(2,1)}, bf16[4,8,1024]{2,1,0:T(8,128)(2,1)S(1)}, u32[]{:S(2)}, u32[]{:S(2)}) collective-permute-start(bf16[4,8,1024]{2,1,0:T(8,128)(2,1)} %left_strips.1), channel_id=1, source_target_pairs={{503,0},{507,4},{511,8},{499,12},{6,1},{10,5},{14,9},{2,13},{5,2},... | collective-permute-start | bytes 196616 | tf_op jit(solution)/shard_map/ppermute | solution.py:414
  25.0 0.0 collective-permute-done.2.s_own
  25.0 0.0 copy-start.13
  25.1 2.5 %collective-permute-done.3.s_other = bf16[4,8,1024]{2,1,0:T(8,128)(2,1)S(1)} collective-permute-done((bf16[4,8,1024]{2,1,0:T(8,128)(2,1)}, bf16[4,8,1024]{2,1,0:T(8,128)(2,1)S(1)}, u32[]{:S(2)}, u32[]{:S(2)}) %collective-permute-start.3) | collective-permute-done | bytes 65568 | tf_op jit(solution)/shard_map/ppermute | solution.py:414
  27.6 0.0 collective-permute-done.t_other
  27.6 0.0 collective-permute-done.1.c_other
  27.6 0.0 copy-start.12
  27.6 2.6 %collective-permute-done.4.half_in = bf16[2064,256]{1,0:T(8,128)(2,1)S(1)} collective-permute-done((bf16[2064,256]{1,0:T(8,128)(2,1)}, bf16[2064,256]{1,0:T(8,128)(2,1)S(1)}, u32[]{:S(2)}, u32[]{:S(2)}) %collective-permute-start.4) | collective-permute-done | bytes 1056800 | tf_op jit(solution)/shard_map/ppermute | solution.py:403
  30.2 3.8 %collective-permute-start.6 = (bf16[2064,256]{1,0:T(8,128)(2,1)S(1)}, bf16[2064,256]{1,0:T(8,128)(2,1)S(1)}, u32[]{:S(2)}, u32[]{:S(2)}) collective-permute-start(bf16[2064,256]{1,0:T(8,128)(2,1)S(1)} %collective-permute-done.4.half_in), channel_id=1, source_target_pairs={{0,4},{4,0},{8,12},{12,8},{1,5},{5,1},{9,13},{13,9},{2,6},{6,2},{1... | collective-permute-start | bytes 3170312 | tf_op jit(solution)/shard_map/ppermute | solution.py:423
  34.1 0.1 stack.38
  34.2 0.5 stack.39.flags_ref
  34.7 1.6 %collective-permute-done.6.other_half_in = bf16[2064,256]{1,0:T(8,128)(2,1)S(1)} collective-permute-done((bf16[2064,256]{1,0:T(8,128)(2,1)S(1)}, bf16[2064,256]{1,0:T(8,128)(2,1)S(1)}, u32[]{:S(2)}, u32[]{:S(2)}) %collective-permute-start.6) | collective-permute-done | bytes 1056800 | tf_op jit(solution)/shard_map/ppermute | solution.py:423
  36.3 0.0 copy-done.6
  36.3 0.0 copy-done.15
  36.3 0.0 copy-done.13
  36.3 0.0 copy-done.14
  36.3 0.0 copy-done.11
  36.3 0.0 copy-done.12
  36.4 0.0 copy-done.8
  36.4 0.9 copy-done.9
  37.3 10.7 %window_attention.1 = (bf16[256,1024]{1,0:T(8,128)(2,1)}, bf16[256,1024]{1,0:T(8,128)(2,1)}, bf16[2,65,8,256]{3,2,1,0:T(8,128)(2,1)}, bf16[2,65,8,256]{3,2,1,0:T(8,128)(2,1)}) custom-call(s32[6]{0:T(128)} %stack.39.flags_ref, bf16[128,1024]{1,0:T(8,128)(2,1)} %bitcast.35, bf16[128,1024]{1,0:T(8,128)(2,1)} %copy-done.11, bf16[128,1024]{1,0:T(8,128)(2,1)} %bitcast.41, ...), custom_call_target="tpu_custom_call" | custom-call | flops 3000000000 | bytes 11000000 | tf_op jit(solution)/shard_map/window_attention/pallas_call | solution.py:280
  48.0 2.3 %collective-permute-start.8 = (bf16[2,65,8,256]{3,2,1,0:T(8,128)(2,1)}, bf16[2,65,8,256]{3,2,1,0:T(8,128)(2,1)S(1)}, u32[]{:S(2)}, u32[]{:S(2)}) collective-permute-start(bf16[2,65,8,256]{3,2,1,0:T(8,128)(2,1)} %get-tuple-element.14), channel_id=1, source_target_pairs={{0,4},{4,0},{8,12},{12,8},{1,5},{5,1},{9,13},{13,9},{2,6},{6,2},{1... | collective-permute-start | bytes 1597448 | tf_op jit(solution)/shard_map/ppermute | solution.py:436
  50.3 0.1 convert_reduce_fusion.1
  50.4 1.6 %collective-permute-done.8 = bf16[2,65,8,256]{3,2,1,0:T(8,128)(2,1)S(1)} collective-permute-done((bf16[2,65,8,256]{3,2,1,0:T(8,128)(2,1)}, bf16[2,65,8,256]{3,2,1,0:T(8,128)(2,1)S(1)}, u32[]{:S(2)}, u32[]{:S(2)}) %collective-permute-start.8) | collective-permute-done | bytes 532512 | tf_op jit(solution)/shard_map/ppermute | solution.py:436
  52.0 1.2 %convert_add_fusion = f32[2,65,8,256]{3,2,1,0:T(8,128)S(1)} fusion(bf16[2,65,8,256]{3,2,1,0:T(8,128)(2,1)S(1)} %collective-permute-done.8, bf16[2,65,8,256]{3,2,1,0:T(8,128)(2,1)} %get-tuple-element.13), kind=kLoop, calls=%fused_computation | loop fusion | flops 798720 | bytes 2129920 | tf_op jit(solution)/shard_map/add | solution.py:436
  53.3 16.5 %collective-permute-start.9 = (bf16[65,8,256]{2,1,0:T(8,128)(2,1)S(1)}, bf16[65,8,256]{2,1,0:T(8,128)(2,1)S(1)}, u32[]{:S(2)}, u32[]{:S(2)}) collective-permute-start(bf16[65,8,256]{2,1,0:T(8,128)(2,1)S(1)} %fusion.16), channel_id=1, source_target_pairs={{0,1},{1,0},{2,3},{3,2},{4,5},{5,4},{6,7},{7,6},{8,9},{9,8},{10,11... | collective-permute-start | bytes 798728 | tf_op jit(solution)/shard_map/ppermute | solution.py:438
  69.8 0.2 fusion.10
  70.0 1.9 %collective-permute-start.7 = (bf16[256,1024]{1,0:T(8,128)(2,1)S(1)}, bf16[256,1024]{1,0:T(8,128)(2,1)S(1)}, u32[]{:S(2)}, u32[]{:S(2)}) collective-permute-start(bf16[256,1024]{1,0:T(8,128)(2,1)S(1)} %copy-done.10), channel_id=1, source_target_pairs={{1,2},{2,1},{3,16},{16,3},{17,18},{18,17},{19,32},{32,19},{33,34},... | collective-permute-start | bytes 1572872 | tf_op jit(solution)/shard_map/ppermute | solution.py:394
  71.9 4.5 %collective-permute-done.9 = bf16[65,8,256]{2,1,0:T(8,128)(2,1)S(1)} collective-permute-done((bf16[65,8,256]{2,1,0:T(8,128)(2,1)S(1)}, bf16[65,8,256]{2,1,0:T(8,128)(2,1)S(1)}, u32[]{:S(2)}, u32[]{:S(2)}) %collective-permute-start.9) | collective-permute-done | bytes 266272 | tf_op jit(solution)/shard_map/ppermute | solution.py:438
  76.4 0.1 fusion.4
  76.6 0.8 pad_maximum_fusion.1
  77.4 10.4 %all-to-all-start = ((bf16[64,8,384]{2,1,0:T(8,128)(2,1)}), bf16[64,8,384]{2,1,0:T(8,128)(2,1)S(1)}, u32[]{:S(2)}, u32[]{:S(2)}) async-start(bf16[64,8,384]{2,1,0:T(8,128)(2,1)} %pad_maximum_fusion.1), calls=%async_computation | async-start | bytes 786432 | tf_op jit(solution)/shard_map/all_to_all | solution.py:448
  87.8 0.0 collective-permute-done.7
  87.8 0.0 copy-start.7
  87.9 0.2 convert_add_fusion.1
  88.1 1.9 %collective-permute-start.10 = (bf16[2,4,4,1024]{3,2,1,0:T(4,128)(2,1)S(1)}, bf16[2,4,4,1024]{3,2,1,0:T(4,128)(2,1)S(1)}, u32[]{:S(2)}, u32[]{:S(2)}) collective-permute-start(bf16[2,4,4,1024]{3,2,1,0:T(4,128)(2,1)S(1)} %slice.98), channel_id=1, source_target_pairs={{0,4},{4,8},{8,12},{12,0},{1,5},{5,9},{9,13},{13,1},{2,6},{6,10},{... | collective-permute-start | bytes 196616 | tf_op jit(solution)/shard_map/ppermute | solution.py:456
  90.0 12.7 %collective-permute-done.10 = bf16[2,4,4,1024]{3,2,1,0:T(4,128)(2,1)S(1)} collective-permute-done((bf16[2,4,4,1024]{3,2,1,0:T(4,128)(2,1)S(1)}, bf16[2,4,4,1024]{3,2,1,0:T(4,128)(2,1)S(1)}, u32[]{:S(2)}, u32[]{:S(2)}) %collective-permute-start.10) | collective-permute-done | bytes 65568 | tf_op jit(solution)/shard_map/ppermute | solution.py:456
  102.7 0.0 copy-start.3
  102.7 1.0 fusion.19
  103.7 1.0 fusion.9
  104.7 3.0 %all-to-all-done = bf16[64,8,384]{2,1,0:T(8,128)(2,1)S(1)} async-done(((bf16[64,8,384]{2,1,0:T(8,128)(2,1)}), bf16[64,8,384]{2,1,0:T(8,128)(2,1)S(1)}, u32[]{:S(2)}, u32[]{:S(2)}) %all-to-all-start) | async-done | bytes 393248 | tf_op jit(solution)/shard_map/all_to_all | solution.py:448
  107.7 0.1 convert_reduce_fusion
  107.8 0.1 slice.69
  107.8 0.6 fusion.17
  108.5 0.1 pad_maximum_fusion.3
  108.5 0.1 stack_reshape.7
  108.6 0.1 stack_reshape.6
  108.7 0.7 mul.71
  (27 shorter events, 0.2 us)
Async XLA Ops:
  0.6 10.2 %copy-start = (bf16[4,32,1024]{2,1,0:T(8,128)(2,1)S(1)}, bf16[4,32,1024]{2,1,0:T(8,128)(2,1)}, u32[]{:S(2)}) copy-start(bf16[4,32,1024]{2,1,0:T(8,128)(2,1)} %tokens_ref.1) | copy-start | bytes 786436
  0.7 12.1 %copy-start.2 = (bf16[4,32,1024]{2,1,0:T(8,128)(2,1)S(1)}, bf16[4,32,1024]{2,1,0:T(8,128)(2,1)}, u32[]{:S(2)}) copy-start(bf16[4,32,1024]{2,1,0:T(8,128)(2,1)} %grads_ref.1) | copy-start | bytes 786436
  0.7 16.0 %copy-start.5 = (s32[16,32]{1,0:T(8,128)S(1)}, s32[16,32]{1,0:T(8,128)}, u32[]{:S(2)}) copy-start(s32[16,32]{1,0:T(8,128)} %param.8) | copy-start | bytes 6148
  3.0 27.2 %collective-permute-start.4 = (bf16[2064,256]{1,0:T(8,128)(2,1)}, bf16[2064,256]{1,0:T(8,128)(2,1)S(1)}, u32[]{:S(2)}, u32[]{:S(2)}) collective-permute-start(bf16[2064,256]{1,0:T(8,128)(2,1)} %packed_half.1), channel_id=1, source_target_pairs={{0,1},{1,0},{2,3},{3,2},{4,5},{5,4},{6,7},{7,6},{8,9},{9,8},{10,11... | collective-permute-start | bytes 3170312 | tf_op jit(solution)/shard_map/ppermute | solution.py:403
  10.8 16.8 %collective-permute-start = (bf16[128,1024]{1,0:T(8,128)(2,1)S(1)}, bf16[128,1024]{1,0:T(8,128)(2,1)S(1)}, u32[]{:S(2)}, u32[]{:S(2)}) collective-permute-start(bf16[128,1024]{1,0:T(8,128)(2,1)S(1)} %bitcast.36), channel_id=1, source_target_pairs={{1,2},{2,1},{3,16},{16,3},{17,18},{18,17},{19,32},{32,19},{33,34},... | collective-permute-start | bytes 786440 | tf_op jit(solution)/shard_map/ppermute | solution.py:394
  12.8 14.8 %collective-permute-start.1 = (bf16[128,1024]{1,0:T(8,128)(2,1)S(1)}, bf16[128,1024]{1,0:T(8,128)(2,1)S(1)}, u32[]{:S(2)}, u32[]{:S(2)}) collective-permute-start(bf16[128,1024]{1,0:T(8,128)(2,1)S(1)} %bitcast.42), channel_id=1, source_target_pairs={{1,2},{2,1},{3,16},{16,3},{17,18},{18,17},{19,32},{32,19},{33,34},... | collective-permute-start | bytes 786440 | tf_op jit(solution)/shard_map/ppermute | solution.py:394
  16.7 19.6 %copy-start.6 = (f32[16,32]{1,0:T(8,128)}, f32[16,32]{1,0:T(8,128)S(1)}, u32[]{:S(2)}) copy-start(f32[16,32]{1,0:T(8,128)S(1)} %convert_element_type.49.valid_ref) | copy-start | bytes 6148
  16.7 4.2 %collective-permute-start.5 = (f32[16,32]{1,0:T(8,128)S(1)}, f32[16,32]{1,0:T(8,128)S(1)}, u32[]{:S(2)}, u32[]{:S(2)}) collective-permute-start(f32[16,32]{1,0:T(8,128)S(1)} %convert_element_type.49.valid_ref), channel_id=1, source_target_pairs={{0,16},{16,32},{32,48},{48,64},{64,80},{80,96},{96,112},{112,128},... | collective-permute-start | bytes 6152 | tf_op jit(solution)/shard_map/ppermute | solution.py:421
  19.0 6.0 %collective-permute-start.2 = (bf16[4,8,1024]{2,1,0:T(8,128)(2,1)}, bf16[4,8,1024]{2,1,0:T(8,128)(2,1)S(1)}, u32[]{:S(2)}, u32[]{:S(2)}) collective-permute-start(bf16[4,8,1024]{2,1,0:T(8,128)(2,1)} %left_strips.1), channel_id=1, source_target_pairs={{4,0},{8,4},{12,8},{0,12},{5,1},{9,5},{13,9},{1,13},{6,2},{10,6},{... | collective-permute-start | bytes 196616 | tf_op jit(solution)/shard_map/ppermute | solution.py:414
  21.0 15.4 %copy-start.15 = (f32[16,32]{1,0:T(8,128)}, f32[16,32]{1,0:T(8,128)S(1)}, u32[]{:S(2)}) copy-start(f32[16,32]{1,0:T(8,128)S(1)} %collective-permute-done.5.valid_other_ref) | copy-start | bytes 6148
  21.0 6.6 %collective-permute-start.3 = (bf16[4,8,1024]{2,1,0:T(8,128)(2,1)}, bf16[4,8,1024]{2,1,0:T(8,128)(2,1)S(1)}, u32[]{:S(2)}, u32[]{:S(2)}) collective-permute-start(bf16[4,8,1024]{2,1,0:T(8,128)(2,1)} %left_strips.1), channel_id=1, source_target_pairs={{503,0},{507,4},{511,8},{499,12},{6,1},{10,5},{14,9},{2,13},{5,2},... | collective-permute-start | bytes 196616 | tf_op jit(solution)/shard_map/ppermute | solution.py:414
  25.0 11.3 %copy-start.13 = (bf16[4,8,1024]{2,1,0:T(8,128)(2,1)}, bf16[4,8,1024]{2,1,0:T(8,128)(2,1)S(1)}, u32[]{:S(2)}) copy-start(bf16[4,8,1024]{2,1,0:T(8,128)(2,1)S(1)} %collective-permute-done.2.s_own) | copy-start | bytes 196612
  27.6 8.7 %copy-start.14 = (bf16[4,8,1024]{2,1,0:T(8,128)(2,1)}, bf16[4,8,1024]{2,1,0:T(8,128)(2,1)S(1)}, u32[]{:S(2)}) copy-start(bf16[4,8,1024]{2,1,0:T(8,128)(2,1)S(1)} %collective-permute-done.3.s_other) | copy-start | bytes 196612
  27.6 8.7 %copy-start.11 = (bf16[128,1024]{1,0:T(8,128)(2,1)}, bf16[128,1024]{1,0:T(8,128)(2,1)S(1)}, u32[]{:S(2)}) copy-start(bf16[128,1024]{1,0:T(8,128)(2,1)S(1)} %collective-permute-done.t_other) | copy-start | bytes 786436
  27.6 8.7 %copy-start.12 = (bf16[128,1024]{1,0:T(8,128)(2,1)}, bf16[128,1024]{1,0:T(8,128)(2,1)S(1)}, u32[]{:S(2)}) copy-start(bf16[128,1024]{1,0:T(8,128)(2,1)S(1)} %collective-permute-done.1.c_other) | copy-start | bytes 786436
  30.2 6.2 %copy-start.8 = (bf16[2064,256]{1,0:T(8,128)(2,1)}, bf16[2064,256]{1,0:T(8,128)(2,1)S(1)}, u32[]{:S(2)}) copy-start(bf16[2064,256]{1,0:T(8,128)(2,1)S(1)} %collective-permute-done.4.half_in) | copy-start | bytes 3170308
  30.2 6.1 %collective-permute-start.6 = (bf16[2064,256]{1,0:T(8,128)(2,1)S(1)}, bf16[2064,256]{1,0:T(8,128)(2,1)S(1)}, u32[]{:S(2)}, u32[]{:S(2)}) collective-permute-start(bf16[2064,256]{1,0:T(8,128)(2,1)S(1)} %collective-permute-done.4.half_in), channel_id=1, source_target_pairs={{0,4},{4,0},{8,12},{12,8},{1,5},{5,1},{9,13},{13,9},{2,6},{6,2},{1... | collective-permute-start | bytes 3170312 | tf_op jit(solution)/shard_map/ppermute | solution.py:423
  36.3 1.0 copy-start.9
  37.3 13.0 %copy-start.1 = (bf16[4,32,1024]{2,1,0:T(8,128)(2,1)S(1)}, bf16[4,32,1024]{2,1,0:T(8,128)(2,1)}, u32[]{:S(2)}) copy-start(bf16[4,32,1024]{2,1,0:T(8,128)(2,1)} %tokens_ref.1) | copy-start | bytes 786436
  48.0 4.0 %collective-permute-start.8 = (bf16[2,65,8,256]{3,2,1,0:T(8,128)(2,1)}, bf16[2,65,8,256]{3,2,1,0:T(8,128)(2,1)S(1)}, u32[]{:S(2)}, u32[]{:S(2)}) collective-permute-start(bf16[2,65,8,256]{3,2,1,0:T(8,128)(2,1)} %get-tuple-element.14), channel_id=1, source_target_pairs={{0,4},{4,0},{8,12},{12,8},{1,5},{5,1},{9,13},{13,9},{2,6},{6,2},{1... | collective-permute-start | bytes 1597448 | tf_op jit(solution)/shard_map/ppermute | solution.py:436
  52.0 17.9 %copy-start.10 = (bf16[256,1024]{1,0:T(8,128)(2,1)S(1)}, bf16[256,1024]{1,0:T(8,128)(2,1)}, u32[]{:S(2)}) copy-start(bf16[256,1024]{1,0:T(8,128)(2,1)} %get-tuple-element.12) | copy-start | bytes 1572868
  53.3 23.1 %collective-permute-start.9 = (bf16[65,8,256]{2,1,0:T(8,128)(2,1)S(1)}, bf16[65,8,256]{2,1,0:T(8,128)(2,1)S(1)}, u32[]{:S(2)}, u32[]{:S(2)}) collective-permute-start(bf16[65,8,256]{2,1,0:T(8,128)(2,1)S(1)} %fusion.16), channel_id=1, source_target_pairs={{0,1},{1,0},{2,3},{3,2},{4,5},{5,4},{6,7},{7,6},{8,9},{9,8},{10,11... | collective-permute-start | bytes 798728 | tf_op jit(solution)/shard_map/ppermute | solution.py:438
  70.0 17.8 %collective-permute-start.7 = (bf16[256,1024]{1,0:T(8,128)(2,1)S(1)}, bf16[256,1024]{1,0:T(8,128)(2,1)S(1)}, u32[]{:S(2)}, u32[]{:S(2)}) collective-permute-start(bf16[256,1024]{1,0:T(8,128)(2,1)S(1)} %copy-done.10), channel_id=1, source_target_pairs={{1,2},{2,1},{3,16},{16,3},{17,18},{18,17},{19,32},{32,19},{33,34},... | collective-permute-start | bytes 1572872 | tf_op jit(solution)/shard_map/ppermute | solution.py:394
  76.5 11.3 %copy-start.4 = (bf16[256,1024]{1,0:T(8,128)(2,1)S(1)}, bf16[256,1024]{1,0:T(8,128)(2,1)}, u32[]{:S(2)}) copy-start(bf16[256,1024]{1,0:T(8,128)(2,1)} %get-tuple-element.11) | copy-start | bytes 1572868
  77.4 30.3 %all-to-all-start = ((bf16[64,8,384]{2,1,0:T(8,128)(2,1)}), bf16[64,8,384]{2,1,0:T(8,128)(2,1)S(1)}, u32[]{:S(2)}, u32[]{:S(2)}) async-start(bf16[64,8,384]{2,1,0:T(8,128)(2,1)} %pad_maximum_fusion.1), calls=%async_computation | async-start | bytes 786432 | tf_op jit(solution)/shard_map/all_to_all | solution.py:448
  87.8 14.9 %copy-start.7 = (f32[1024]{0:T(1024)S(1)}, f32[1024]{0:T(1024)}, u32[]{:S(2)}) copy-start(f32[1024]{0:T(1024)} %param.9) | copy-start | bytes 12292
  88.1 14.6 %collective-permute-start.10 = (bf16[2,4,4,1024]{3,2,1,0:T(4,128)(2,1)S(1)}, bf16[2,4,4,1024]{3,2,1,0:T(4,128)(2,1)S(1)}, u32[]{:S(2)}, u32[]{:S(2)}) collective-permute-start(bf16[2,4,4,1024]{3,2,1,0:T(4,128)(2,1)S(1)} %slice.98), channel_id=1, source_target_pairs={{0,4},{4,8},{8,12},{12,0},{1,5},{5,9},{9,13},{13,1},{2,6},{6,10},{... | collective-permute-start | bytes 196616 | tf_op jit(solution)/shard_map/ppermute | solution.py:456
  102.7 1.0 copy-start.3

commit v5 on v4

--- a/solution.py
+++ b/solution.py
@@ -16,6 +16,8 @@
 SPAN = 2 * WIN - 1
 POS = WIN * WIN
 VMEM_LIMIT = 56 * 1024 * 1024
+STRIPS_VMEM_LIMIT = 4 * 1024 * 1024
+MAIN_VMEM_LIMIT = 36 * 1024 * 1024
 
 
 def dot(a, b, ca, cb):
@@ -301,7 +303,7 @@
             pltpu.VMEM((16, channels), BF16),
             pltpu.SemaphoreType.DMA((2 * (3 + d // channels) + 15,)),
         ],
-        compiler_params=pltpu.CompilerParams(vmem_limit_bytes=VMEM_LIMIT),
+        compiler_params=pltpu.CompilerParams(vmem_limit_bytes=MAIN_VMEM_LIMIT),
         cost_estimate=pl.CostEstimate(
             flops=3_000_000_000, bytes_accessed=11_000_000, transcendentals=131072
         ),
@@ -363,7 +365,7 @@
         out_shape=jax.ShapeDtypeStruct((prow, 2 * SHIFT, d), BF16),
         in_specs=[spec, spec],
         out_specs=pl.BlockSpec((prow, 2 * SHIFT, d), lambda i: (0, 0, 0)),
-        compiler_params=pltpu.CompilerParams(vmem_limit_bytes=VMEM_LIMIT),
+        compiler_params=pltpu.CompilerParams(vmem_limit_bytes=STRIPS_VMEM_LIMIT),
         cost_estimate=pl.CostEstimate(flops=0, bytes_accessed=300_000, transcendentals=0),
         name="left_strips",
     )(tokens, grads)

time: 110 us -> 110 us (level)
  Pallas kernels: 14.7 us -> 12 us
  local copies, waits for them, and re-layouts: 2.17 us -> 4.13 us
    ppermute x1, starting transfers between devices: 16.5 us -> 18.5 us  [on_device(): pair_beside = lax.ppermute(pairs[1].astype(BF16), 'head', beside)]
    unnamed x32 -> x24, local copies, waits for them, and re-layouts: 1.02 us -> 2.97 us
    pallas_call x1, Pallas kernels: 1.63 us -> 0.04 us  [left_strips(): pl.pallas_call(strips_kernel, grid=(1,), out_shape=jax.ShapeDtypeStruct((...]
    pallas_call x1, Pallas kernels: 10.7 us -> 9.49 us  [attention(): pl.pallas_call(attention_kernel, out_shape=(term, term, piece, piece), in...]
    add x1, other arithmetic: 1.21 us -> 0.11 us  [on_device(): pairs = keep.astype(F32) + lax.ppermute(send, 'col', swap).astype(F32)]
  transfers between devices with their start and end apart: 12 -> 12, of which waited for: 7 -> 7; matrix products, arithmetic and copies ran while one was open for 4% -> 4% of each run, Pallas kernels for 1% -> 0%
where the time goes in v5:
time: 110 us; the launch traced here: 109 us
  starting transfers between devices  58.1 us (53%)
  waiting for transfers between devices  29.1 us (26%)
  Pallas kernels  12 us (11%)
  other arithmetic  4.81 us (4%)
  local copies, waits for them, and re-layouts  4.13 us (4%)
    ppermute x1, starting transfers between devices, on_device(): pair_beside = lax.ppermute(pairs[1].astype(BF16), 'head', beside)  18.5 us
    ppermute x1, waiting for transfers between devices, on_device(): lax.ppermute(total[:, :, -SHIFT:].astype(BF16), 'col', right).astype(F32)  12.7 us
    all_to_all x1, starting transfers between devices, on_device(): lax.all_to_all(pieces, ('row', 'col'), 0, 0, axis_index_groups=cores, til...  9.98 us
    pallas_call x1, Pallas kernels, attention(): pl.pallas_call(attention_kernel, out_shape=(term, term, piece, piece), in...  9.49 us
    ppermute x1, starting transfers between devices, on_device(): lax.ppermute(packed_half((col % 2)[None], w_qkv, w_proj, table), 'head',...  7.81 us
    ppermute x3, starting transfers between devices, trade(): return lax.ppermute(value, ('row', 'head'), mates)  7.75 us
    ppermute x1, starting transfers between devices, on_device(): lax.ppermute(strips, whole, across)  4.04 us
    ppermute x1, waiting for transfers between devices, on_device(): pair_beside = lax.ppermute(pairs[1].astype(BF16), 'head', beside)  3.95 us
  transfers between devices with their start and end apart: 12, of which 7 were waited for; matrix products, arithmetic and copies ran while one was open for 4% of the time, Pallas kernels for 0%

profile of v5, /device:TPU:2, one launch (start us, length us, event | category | flops | bytes accessed | tf_op | source)
XLA Modules:
  0.0 109.1 jit_solution(10925867812076254037)
XLA Ops:
  0.6 0.0 copy-start
  0.7 0.0 copy-start.2
  0.7 0.0 copy-start.11
  0.7 0.0 copy-start.1
  0.7 0.0 copy-start.3
  0.7 0.0 copy-start.4
  0.7 0.0 copy-start.5
  0.7 2.4 %packed_half.1 = bf16[2064,256]{1,0:T(8,128)(2,1)} custom-call(s32[1]{0:T(128)} %bitcast.9.core_ref, bf16[3,1024,256]{2,1,0:T(8,128)(2,1)} %bitcast.37, bf16[256,1024]{1,0:T(8,128)(2,1)} %wp_in.1, f32[4,225]{1,0:T(4,128)} %bitcast.41), custom_call_target="tpu_custom_call" | custom-call | bytes 2100000 | tf_op jit(solution)/shard_map/packed_half/pallas_call | solution.py:336
  3.2 7.8 %collective-permute-start.4 = (bf16[2064,256]{1,0:T(8,128)(2,1)}, bf16[2064,256]{1,0:T(8,128)(2,1)}, u32[]{:S(2)}, u32[]{:S(2)}) collective-permute-start(bf16[2064,256]{1,0:T(8,128)(2,1)} %packed_half.1), channel_id=1, source_target_pairs={{0,1},{1,0},{2,3},{3,2},{4,5},{5,4},{6,7},{7,6},{8,9},{9,8},{10,11... | collective-permute-start | bytes 3170312 | tf_op jit(solution)/shard_map/ppermute | solution.py:405
  11.0 0.0 copy-done
  11.0 1.9 %collective-permute-start = (bf16[128,1024]{1,0:T(8,128)(2,1)S(1)}, bf16[128,1024]{1,0:T(8,128)(2,1)S(1)}, u32[]{:S(2)}, u32[]{:S(2)}) collective-permute-start(bf16[128,1024]{1,0:T(8,128)(2,1)S(1)} %bitcast.35), channel_id=1, source_target_pairs={{1,2},{2,1},{3,16},{16,3},{17,18},{18,17},{19,32},{32,19},{33,34},... | collective-permute-start | bytes 786440 | tf_op jit(solution)/shard_map/ppermute | solution.py:396
  12.9 0.0 copy-done.2
  12.9 3.9 %collective-permute-start.1 = (bf16[128,1024]{1,0:T(8,128)(2,1)S(1)}, bf16[128,1024]{1,0:T(8,128)(2,1)S(1)}, u32[]{:S(2)}, u32[]{:S(2)}) collective-permute-start(bf16[128,1024]{1,0:T(8,128)(2,1)S(1)} %bitcast.39), channel_id=1, source_target_pairs={{1,2},{2,1},{3,16},{16,3},{17,18},{18,17},{19,32},{32,19},{33,34},... | collective-permute-start | bytes 786440 | tf_op jit(solution)/shard_map/ppermute | solution.py:396
  16.9 0.0 copy-done.11
  16.9 0.7 collective-permute-start.5
  17.6 1.9 %collective-permute-start.2 = (bf16[4,8,1024]{2,1,0:T(8,128)(2,1)S(1)}, bf16[4,8,1024]{2,1,0:T(8,128)(2,1)S(1)}, u32[]{:S(2)}, u32[]{:S(2)}) collective-permute-start(bf16[4,8,1024]{2,1,0:T(8,128)(2,1)S(1)} %left_strips.1), channel_id=1, source_target_pairs={{4,0},{8,4},{12,8},{0,12},{5,1},{9,5},{13,9},{1,13},{6,2},{10,6},{... | collective-permute-start | bytes 196616 | tf_op jit(solution)/shard_map/ppermute | solution.py:416
  19.5 0.0 collective-permute-done.5.valid_other_ref
  19.5 0.0 copy-start.8
  19.5 0.6 copy-done.8
  20.1 4.0 %collective-permute-start.3 = (bf16[4,8,1024]{2,1,0:T(8,128)(2,1)S(1)}, bf16[4,8,1024]{2,1,0:T(8,128)(2,1)S(1)}, u32[]{:S(2)}, u32[]{:S(2)}) collective-permute-start(bf16[4,8,1024]{2,1,0:T(8,128)(2,1)S(1)} %left_strips.1), channel_id=1, source_target_pairs={{503,0},{507,4},{511,8},{499,12},{6,1},{10,5},{14,9},{2,13},{5,2},... | collective-permute-start | bytes 196616 | tf_op jit(solution)/shard_map/ppermute | solution.py:416
  24.2 0.0 collective-permute-done.2.s_own
  24.2 2.2 %collective-permute-done.3.s_other = bf16[4,8,1024]{2,1,0:T(8,128)(2,1)S(1)} collective-permute-done((bf16[4,8,1024]{2,1,0:T(8,128)(2,1)S(1)}, bf16[4,8,1024]{2,1,0:T(8,128)(2,1)S(1)}, u32[]{:S(2)}, u32[]{:S(2)}) %collective-permute-start.3) | collective-permute-done | bytes 65568 | tf_op jit(solution)/shard_map/ppermute | solution.py:416
  26.4 0.0 collective-permute-done.t_other
  26.4 0.0 collective-permute-done.1.c_other
  26.4 0.7 copy-done.6
  27.1 3.3 %collective-permute-done.4.half_in = bf16[2064,256]{1,0:T(8,128)(2,1)} collective-permute-done((bf16[2064,256]{1,0:T(8,128)(2,1)}, bf16[2064,256]{1,0:T(8,128)(2,1)}, u32[]{:S(2)}, u32[]{:S(2)}) %collective-permute-start.4) | collective-permute-done | bytes 1056800 | tf_op jit(solution)/shard_map/ppermute | solution.py:405
  30.4 3.2 %collective-permute-start.6 = (bf16[2064,256]{1,0:T(8,128)(2,1)}, bf16[2064,256]{1,0:T(8,128)(2,1)}, u32[]{:S(2)}, u32[]{:S(2)}) collective-permute-start(bf16[2064,256]{1,0:T(8,128)(2,1)} %collective-permute-done.4.half_in), channel_id=1, source_target_pairs={{0,4},{4,0},{8,12},{12,8},{1,5},{5,1},{9,13},{13,9},{2,6},{6,2},{1... | collective-permute-start | bytes 3170312 | tf_op jit(solution)/shard_map/ppermute | solution.py:425
  33.7 0.1 stack.38
  33.8 2.5 %collective-permute-done.6.other_half_in = bf16[2064,256]{1,0:T(8,128)(2,1)} collective-permute-done((bf16[2064,256]{1,0:T(8,128)(2,1)}, bf16[2064,256]{1,0:T(8,128)(2,1)}, u32[]{:S(2)}, u32[]{:S(2)}) %collective-permute-start.6) | collective-permute-done | bytes 1056800 | tf_op jit(solution)/shard_map/ppermute | solution.py:425
  36.2 0.0 copy-done.1
  36.3 0.0 copy-done.3
  36.3 0.0 copy-done.4
  36.3 0.0 copy-done.5
  36.3 0.0 copy-start.7
  36.3 0.9 copy-done.7
  37.2 0.7 copy-done.9
  37.9 9.5 %window_attention.1 = (bf16[256,1024]{1,0:T(8,128)(2,1)S(1)}, bf16[256,1024]{1,0:T(8,128)(2,1)}, bf16[2,65,8,256]{3,2,1,0:T(8,128)(2,1)S(1)}, bf16[2,65,8,256]{3,2,1,0:T(8,128)(2,1)S(1)}) custom-call(s32[6]{0:T(128)S(1)} %stack.39.flags_ref, bf16[128,1024]{1,0:T(8,128)(2,1)S(1)} %bitcast.36, bf16[128,1024]{1,0:T(8,128)(2,1)S(1)} %collective-permute-done.t_other, ...), custom_call_target="tpu_custom_call" | custom-call | flops 3000000000 | bytes 11000000 | tf_op jit(solution)/shard_map/window_attention/pallas_call | solution.py:282
  47.4 2.3 %collective-permute-start.8 = (bf16[2,65,8,256]{3,2,1,0:T(8,128)(2,1)S(1)}, bf16[2,65,8,256]{3,2,1,0:T(8,128)(2,1)S(1)}, u32[]{:S(2)}, u32[]{:S(2)}) collective-permute-start(bf16[2,65,8,256]{3,2,1,0:T(8,128)(2,1)S(1)} %get-tuple-element.14), channel_id=1, source_target_pairs={{0,4},{4,0},{8,12},{12,8},{1,5},{5,1},{9,13},{13,9},{2,6},{6,2},{1... | collective-permute-start | bytes 1597448 | tf_op jit(solution)/shard_map/ppermute | solution.py:438
  49.7 0.1 convert_reduce_fusion.1
  49.8 1.4 %collective-permute-done.8 = bf16[2,65,8,256]{3,2,1,0:T(8,128)(2,1)S(1)} collective-permute-done((bf16[2,65,8,256]{3,2,1,0:T(8,128)(2,1)S(1)}, bf16[2,65,8,256]{3,2,1,0:T(8,128)(2,1)S(1)}, u32[]{:S(2)}, u32[]{:S(2)}) %collective-permute-start.8) | collective-permute-done | bytes 532512 | tf_op jit(solution)/shard_map/ppermute | solution.py:438
  51.2 0.1 convert_add_fusion
  51.4 18.5 %collective-permute-start.9 = (bf16[65,8,256]{2,1,0:T(8,128)(2,1)S(1)}, bf16[65,8,256]{2,1,0:T(8,128)(2,1)S(1)}, u32[]{:S(2)}, u32[]{:S(2)}) collective-permute-start(bf16[65,8,256]{2,1,0:T(8,128)(2,1)S(1)} %fusion.16), channel_id=1, source_target_pairs={{0,1},{1,0},{2,3},{3,2},{4,5},{5,4},{6,7},{7,6},{8,9},{9,8},{10,11... | collective-permute-start | bytes 798728 | tf_op jit(solution)/shard_map/ppermute | solution.py:440
  69.9 0.8 fusion.10
  70.7 1.9 %collective-permute-start.7 = (bf16[256,1024]{1,0:T(8,128)(2,1)}, bf16[256,1024]{1,0:T(8,128)(2,1)S(1)}, u32[]{:S(2)}, u32[]{:S(2)}) collective-permute-start(bf16[256,1024]{1,0:T(8,128)(2,1)} %get-tuple-element.12), channel_id=1, source_target_pairs={{1,2},{2,1},{3,16},{16,3},{17,18},{18,17},{19,32},{32,19},{33,34},... | collective-permute-start | bytes 1572872 | tf_op jit(solution)/shard_map/ppermute | solution.py:396
  72.6 4.0 %collective-permute-done.9 = bf16[65,8,256]{2,1,0:T(8,128)(2,1)S(1)} collective-permute-done((bf16[65,8,256]{2,1,0:T(8,128)(2,1)S(1)}, bf16[65,8,256]{2,1,0:T(8,128)(2,1)S(1)}, u32[]{:S(2)}, u32[]{:S(2)}) %collective-permute-start.9) | collective-permute-done | bytes 266272 | tf_op jit(solution)/shard_map/ppermute | solution.py:440
  76.6 0.1 fusion.4
  76.7 0.8 pad_maximum_fusion.1
  77.5 10.0 %all-to-all-start = ((bf16[64,8,384]{2,1,0:T(8,128)(2,1)}), bf16[64,8,384]{2,1,0:T(8,128)(2,1)S(1)}, u32[]{:S(2)}, u32[]{:S(2)}) async-start(bf16[64,8,384]{2,1,0:T(8,128)(2,1)} %pad_maximum_fusion.1), calls=%async_computation | async-start | bytes 786432 | tf_op jit(solution)/shard_map/all_to_all | solution.py:450
  87.5 0.0 collective-permute-done.7
  87.5 0.0 copy-start.10
  87.5 0.2 convert_add_fusion.1
  87.7 1.9 %collective-permute-start.10 = (bf16[2,4,4,1024]{3,2,1,0:T(4,128)(2,1)S(1)}, bf16[2,4,4,1024]{3,2,1,0:T(4,128)(2,1)S(1)}, u32[]{:S(2)}, u32[]{:S(2)}) collective-permute-start(bf16[2,4,4,1024]{3,2,1,0:T(4,128)(2,1)S(1)} %slice.98), channel_id=1, source_target_pairs={{0,4},{4,8},{8,12},{12,0},{1,5},{5,9},{9,13},{13,1},{2,6},{6,10},{... | collective-permute-start | bytes 196616 | tf_op jit(solution)/shard_map/ppermute | solution.py:458
  89.6 0.0 copy-done.10
  89.7 12.7 %collective-permute-done.10 = bf16[2,4,4,1024]{3,2,1,0:T(4,128)(2,1)S(1)} collective-permute-done((bf16[2,4,4,1024]{3,2,1,0:T(4,128)(2,1)S(1)}, bf16[2,4,4,1024]{3,2,1,0:T(4,128)(2,1)S(1)}, u32[]{:S(2)}, u32[]{:S(2)}) %collective-permute-start.10) | collective-permute-done | bytes 65568 | tf_op jit(solution)/shard_map/ppermute | solution.py:458
  102.4 1.0 fusion.19
  103.3 1.0 fusion.9
  104.3 3.0 %all-to-all-done = bf16[64,8,384]{2,1,0:T(8,128)(2,1)S(1)} async-done(((bf16[64,8,384]{2,1,0:T(8,128)(2,1)}), bf16[64,8,384]{2,1,0:T(8,128)(2,1)S(1)}, u32[]{:S(2)}, u32[]{:S(2)}) %all-to-all-start) | async-done | bytes 393248 | tf_op jit(solution)/shard_map/all_to_all | solution.py:450
  107.3 0.1 convert_reduce_fusion
  107.4 0.1 slice.69
  107.5 0.6 fusion.17
  108.1 0.1 pad_maximum_fusion.3
  108.2 0.1 stack_reshape.7
  108.3 0.1 stack_reshape.6
  108.4 0.7 mul.71
  (19 shorter events, 0.2 us)
Async XLA Ops:
  0.6 10.3 %copy-start = (bf16[4,32,1024]{2,1,0:T(8,128)(2,1)S(1)}, bf16[4,32,1024]{2,1,0:T(8,128)(2,1)}, u32[]{:S(2)}) copy-start(bf16[4,32,1024]{2,1,0:T(8,128)(2,1)} %tokens_ref.1) | copy-start | bytes 786436
  0.7 12.3 %copy-start.2 = (bf16[4,32,1024]{2,1,0:T(8,128)(2,1)S(1)}, bf16[4,32,1024]{2,1,0:T(8,128)(2,1)}, u32[]{:S(2)}) copy-start(bf16[4,32,1024]{2,1,0:T(8,128)(2,1)} %grads_ref.1) | copy-start | bytes 786436
  0.7 16.2 %copy-start.11 = (s32[16,32]{1,0:T(8,128)S(1)}, s32[16,32]{1,0:T(8,128)}, u32[]{:S(2)}) copy-start(s32[16,32]{1,0:T(8,128)} %param.8) | copy-start | bytes 6148
  0.7 35.6 %copy-start.1 = (bf16[1024,3,256]{2,0,1:T(8,128)(2,1)S(1)}, bf16[1024,3,256]{2,0,1:T(8,128)(2,1)}, u32[]{:S(2)}) copy-start(bf16[1024,3,256]{2,0,1:T(8,128)(2,1)} %param.10) | copy-start | bytes 4718596
  0.7 35.6 %copy-start.3 = (bf16[256,1024]{1,0:T(8,128)(2,1)S(1)}, bf16[256,1024]{1,0:T(8,128)(2,1)}, u32[]{:S(2)}) copy-start(bf16[256,1024]{1,0:T(8,128)(2,1)} %wp_in.1) | copy-start | bytes 1572868
  0.7 35.6 %copy-start.4 = (f32[225,4]{0,1:T(4,128)S(1)}, f32[225,4]{0,1:T(4,128)}, u32[]{:S(2)}) copy-start(f32[225,4]{0,1:T(4,128)} %param.12) | copy-start | bytes 10804
  0.7 35.6 %copy-start.5 = (f32[1024]{0:T(1024)S(1)}, f32[1024]{0:T(1024)}, u32[]{:S(2)}) copy-start(f32[1024]{0:T(1024)} %param.9) | copy-start | bytes 12292
  3.2 27.3 %collective-permute-start.4 = (bf16[2064,256]{1,0:T(8,128)(2,1)}, bf16[2064,256]{1,0:T(8,128)(2,1)}, u32[]{:S(2)}, u32[]{:S(2)}) collective-permute-start(bf16[2064,256]{1,0:T(8,128)(2,1)} %packed_half.1), channel_id=1, source_target_pairs={{0,1},{1,0},{2,3},{3,2},{4,5},{5,4},{6,7},{7,6},{8,9},{9,8},{10,11... | collective-permute-start | bytes 3170312 | tf_op jit(solution)/shard_map/ppermute | solution.py:405
  11.0 15.4 %collective-permute-start = (bf16[128,1024]{1,0:T(8,128)(2,1)S(1)}, bf16[128,1024]{1,0:T(8,128)(2,1)S(1)}, u32[]{:S(2)}, u32[]{:S(2)}) collective-permute-start(bf16[128,1024]{1,0:T(8,128)(2,1)S(1)} %bitcast.35), channel_id=1, source_target_pairs={{1,2},{2,1},{3,16},{16,3},{17,18},{18,17},{19,32},{32,19},{33,34},... | collective-permute-start | bytes 786440 | tf_op jit(solution)/shard_map/ppermute | solution.py:396
  12.9 13.5 %collective-permute-start.1 = (bf16[128,1024]{1,0:T(8,128)(2,1)S(1)}, bf16[128,1024]{1,0:T(8,128)(2,1)S(1)}, u32[]{:S(2)}, u32[]{:S(2)}) collective-permute-start(bf16[128,1024]{1,0:T(8,128)(2,1)S(1)} %bitcast.39), channel_id=1, source_target_pairs={{1,2},{2,1},{3,16},{16,3},{17,18},{18,17},{19,32},{32,19},{33,34},... | collective-permute-start | bytes 786440 | tf_op jit(solution)/shard_map/ppermute | solution.py:396
  16.9 2.6 %collective-permute-start.5 = (f32[16,32]{1,0:T(8,128)S(1)}, f32[16,32]{1,0:T(8,128)S(1)}, u32[]{:S(2)}, u32[]{:S(2)}) collective-permute-start(f32[16,32]{1,0:T(8,128)S(1)} %convert_element_type.49.valid_ref), channel_id=1, source_target_pairs={{0,16},{16,32},{32,48},{48,64},{64,80},{80,96},{96,112},{112,128},... | collective-permute-start | bytes 6152 | tf_op jit(solution)/shard_map/ppermute | solution.py:423
  17.6 6.6 %collective-permute-start.2 = (bf16[4,8,1024]{2,1,0:T(8,128)(2,1)S(1)}, bf16[4,8,1024]{2,1,0:T(8,128)(2,1)S(1)}, u32[]{:S(2)}, u32[]{:S(2)}) collective-permute-start(bf16[4,8,1024]{2,1,0:T(8,128)(2,1)S(1)} %left_strips.1), channel_id=1, source_target_pairs={{4,0},{8,4},{12,8},{0,12},{5,1},{9,5},{13,9},{1,13},{6,2},{10,6},{... | collective-permute-start | bytes 196616 | tf_op jit(solution)/shard_map/ppermute | solution.py:416
  19.5 0.6 copy-start.8
  20.1 6.3 %collective-permute-start.3 = (bf16[4,8,1024]{2,1,0:T(8,128)(2,1)S(1)}, bf16[4,8,1024]{2,1,0:T(8,128)(2,1)S(1)}, u32[]{:S(2)}, u32[]{:S(2)}) collective-permute-start(bf16[4,8,1024]{2,1,0:T(8,128)(2,1)S(1)} %left_strips.1), channel_id=1, source_target_pairs={{503,0},{507,4},{511,8},{499,12},{6,1},{10,5},{14,9},{2,13},{5,2},... | collective-permute-start | bytes 196616 | tf_op jit(solution)/shard_map/ppermute | solution.py:416
  26.4 0.7 copy-start.6
  30.4 5.8 %collective-permute-start.6 = (bf16[2064,256]{1,0:T(8,128)(2,1)}, bf16[2064,256]{1,0:T(8,128)(2,1)}, u32[]{:S(2)}, u32[]{:S(2)}) collective-permute-start(bf16[2064,256]{1,0:T(8,128)(2,1)} %collective-permute-done.4.half_in), channel_id=1, source_target_pairs={{0,4},{4,0},{8,12},{12,8},{1,5},{5,1},{9,13},{13,9},{2,6},{6,2},{1... | collective-permute-start | bytes 3170312 | tf_op jit(solution)/shard_map/ppermute | solution.py:425
  36.3 1.0 copy-start.7
  37.2 0.7 copy-start.9
  47.4 3.8 %collective-permute-start.8 = (bf16[2,65,8,256]{3,2,1,0:T(8,128)(2,1)S(1)}, bf16[2,65,8,256]{3,2,1,0:T(8,128)(2,1)S(1)}, u32[]{:S(2)}, u32[]{:S(2)}) collective-permute-start(bf16[2,65,8,256]{3,2,1,0:T(8,128)(2,1)S(1)} %get-tuple-element.14), channel_id=1, source_target_pairs={{0,4},{4,0},{8,12},{12,8},{1,5},{5,1},{9,13},{13,9},{2,6},{6,2},{1... | collective-permute-start | bytes 1597448 | tf_op jit(solution)/shard_map/ppermute | solution.py:438
  51.4 25.2 %collective-permute-start.9 = (bf16[65,8,256]{2,1,0:T(8,128)(2,1)S(1)}, bf16[65,8,256]{2,1,0:T(8,128)(2,1)S(1)}, u32[]{:S(2)}, u32[]{:S(2)}) collective-permute-start(bf16[65,8,256]{2,1,0:T(8,128)(2,1)S(1)} %fusion.16), channel_id=1, source_target_pairs={{0,1},{1,0},{2,3},{3,2},{4,5},{5,4},{6,7},{7,6},{8,9},{9,8},{10,11... | collective-permute-start | bytes 798728 | tf_op jit(solution)/shard_map/ppermute | solution.py:440
  70.7 16.8 %collective-permute-start.7 = (bf16[256,1024]{1,0:T(8,128)(2,1)}, bf16[256,1024]{1,0:T(8,128)(2,1)S(1)}, u32[]{:S(2)}, u32[]{:S(2)}) collective-permute-start(bf16[256,1024]{1,0:T(8,128)(2,1)} %get-tuple-element.12), channel_id=1, source_target_pairs={{1,2},{2,1},{3,16},{16,3},{17,18},{18,17},{19,32},{32,19},{33,34},... | collective-permute-start | bytes 1572872 | tf_op jit(solution)/shard_map/ppermute | solution.py:396
  77.5 29.9 %all-to-all-start = ((bf16[64,8,384]{2,1,0:T(8,128)(2,1)}), bf16[64,8,384]{2,1,0:T(8,128)(2,1)S(1)}, u32[]{:S(2)}, u32[]{:S(2)}) async-start(bf16[64,8,384]{2,1,0:T(8,128)(2,1)} %pad_maximum_fusion.1), calls=%async_computation | async-start | bytes 786432 | tf_op jit(solution)/shard_map/all_to_all | solution.py:450
  87.5 2.2 %copy-start.10 = (f32[4,32]{1,0:T(4,128)S(1)}, f32[4,32]{1,0:T(4,128)}, u32[]{:S(2)}) copy-start(f32[4,32]{1,0:T(4,128)} %fusion.10) | copy-start | bytes 1540
  87.7 14.6 %collective-permute-start.10 = (bf16[2,4,4,1024]{3,2,1,0:T(4,128)(2,1)S(1)}, bf16[2,4,4,1024]{3,2,1,0:T(4,128)(2,1)S(1)}, u32[]{:S(2)}, u32[]{:S(2)}) collective-permute-start(bf16[2,4,4,1024]{3,2,1,0:T(4,128)(2,1)S(1)} %slice.98), channel_id=1, source_target_pairs={{0,4},{4,8},{8,12},{12,0},{1,5},{5,9},{9,13},{13,1},{2,6},{6,10},{... | collective-permute-start | bytes 196616 | tf_op jit(solution)/shard_map/ppermute | solution.py:458
